TPU v7x, 128 devices: a whole 4x4x4 slice. The times are simulated.
128 devices in a mesh: wide: 16 (over z, y), narrow: 8 (over x, core).
Axes of the slice: x: 4, y: 4, z: 4, core: 2. Of those that a mesh axis runs over, the one named last changes fastest.
Arguments:
- features: bfloat16 [512, 65536], P('narrow', 'wide'), may hold values from -36 to 36
- edge_tiles: bfloat16 [512, 12, 128, 128], P('wide'), may hold values from 0 to 22, as said below
- block_lists: int32 [512, 12], P('wide'), may hold values from 0 to 63, as said below
- send_lists: int32 [16, 16, 2], P('wide'), may hold values from 0 to 31
- train_ids: int32 [8192], P('wide'), may hold values from 0 to 4095, as said below
- owners: int32 [8192, 1], P('wide'), may hold values from 0 to 127; in each aligned block of 512 rows (0 to 511, 512 to 1023, ...) at most 8 rows name the same one
- cotangent: bfloat16 [4, 512, 8192], P(None, 'narrow', 'wide'), may hold values from -6 to 6
- query_weight: bfloat16 [512, 512], replicated, may hold values from -8 to 8
- key_weight: bfloat16 [512, 512], replicated, may hold values from -8 to 8
- value_weight: bfloat16 [512, 512], replicated, may hold values from -0.25 to 0.25
- out_weight: bfloat16 [512, 512], replicated, may hold values from -0.25 to 0.25
- up_weight: bfloat16 [2048, 512], replicated, may hold values from -0.25 to 0.25
- down_weight: bfloat16 [2048, 512], replicated, may hold values from -0.125 to 0.125
Outputs:
- hop_tokens: bfloat16 [3, 512, 65536], P(None, 'narrow', 'wide')
- grad_attn: float32 [2048, 512], P(('wide', 'narrow'))
- grad_up: float32 [2048, 512], P(('wide', 'narrow'))
- grad_down: float32 [2048, 512], P(('wide', 'narrow'))
Inputs may be any that keep to these rules, and one draw needn't show every extreme that they name: edge_tiles[b, k, s, t] weighs the edge from node s of block source[b, k] to node t of block b; the diagonal of every edge_tiles[b, 0] is positive. block_lists[b, 0] = b mod 32; within every part each position 32 to 63 appears. `train_ids`: distinct within a part. `owners`: at most 8 of the 512 training nodes of one part name the same owner; every owner is named by some node.
All inputs are finite; a program needn't handle non-finite values.
Results may differ from a plain program's by a relative error of at most 0.025.
Values may be sent and summed in bfloat16 or wider, within the bound.
No kernel may reach another device: no remote copies, remote signals or barrier semaphores. Data moves between devices by JAX's collectives and lax.ppermute only.
A program may use at most 128 MiB of HBM per device.

v0:
```python
import math

import jax
import jax.numpy as jnp
from jax import lax
from jax.sharding import PartitionSpec as P

HEADS = 8
HOPS = 3
TOKS = 4
MB = 128


epsilon = 1e-05


def product_of(pattern, first_arg, second_arg):
    return jnp.einsum(pattern, first_arg, second_arg, preferred_element_type=jnp.float32)


def normalize(hidden):
    center = hidden - jnp.mean(hidden, axis=1, keepdims=True)
    inverse = lax.rsqrt(jnp.mean(center * center, axis=1, keepdims=True) + epsilon)
    return (center * inverse, inverse)


def norm_back(upstream, normed, inverse):
    return inverse * (
        upstream
        - jnp.mean(upstream, axis=1, keepdims=True)
        - normed * jnp.mean(upstream * normed, axis=1, keepdims=True)
    )


def gelu_tanh(values):
    return jax.nn.gelu(values, approximate=True)


def layer_grads(
    tokens, cotangent, query_weight, key_weight, value_weight, out_weight, up_weight, down_weight
):
    tok_count, feat_width, row_count = tokens.shape
    head_dim = feat_width // HEADS
    score_scale = 1.0 / math.sqrt(head_dim)
    split_heads = (tok_count, HEADS, head_dim, row_count)
    first_norm, _ = normalize(tokens.astype(jnp.float32))
    normed_a = first_norm.astype(jnp.bfloat16)
    query_heads = (
        product_of("od,tdr->tor", query_weight, normed_a).astype(jnp.bfloat16).reshape(split_heads)
    )
    key_heads = (
        product_of("od,tdr->tor", key_weight, normed_a).astype(jnp.bfloat16).reshape(split_heads)
    )
    value_heads = (
        product_of("od,tdr->tor", value_weight, normed_a).astype(jnp.bfloat16).reshape(split_heads)
    )
    scores = product_of("thdr,uhdr->htur", query_heads, key_heads) * score_scale
    attn_probs = jax.nn.softmax(scores, axis=2)
    attn_low = attn_probs.astype(jnp.bfloat16)
    mixed_heads = (
        product_of("htur,uhdr->thdr", attn_low, value_heads)
        .astype(jnp.bfloat16)
        .reshape(tok_count, feat_width, row_count)
    )
    residual = (
        tokens.astype(jnp.float32) + product_of("od,tdr->tor", out_weight, mixed_heads)
    ).astype(jnp.bfloat16)
    second_norm, second_inv = normalize(residual.astype(jnp.float32))
    normed_b = second_norm.astype(jnp.bfloat16)
    pre_act = product_of("fd,tdr->tfr", up_weight, normed_b)
    activated = gelu_tanh(pre_act).astype(jnp.bfloat16)
    sum_down = product_of("tfr,tdr->fd", activated, cotangent)
    grad_act = product_of("fd,tdr->tfr", down_weight, cotangent)
    _, gelu_back = jax.vjp(gelu_tanh, pre_act)
    grad_pre = gelu_back(grad_act)[0].astype(jnp.bfloat16)
    sum_up = product_of("tfr,tdr->fd", grad_pre, normed_b)
    grad_normed = product_of("fd,tfr->tdr", up_weight, grad_pre)
    grad_resid = (
        cotangent.astype(jnp.float32) + norm_back(grad_normed, second_norm, second_inv)
    ).astype(jnp.bfloat16)
    sum_out = product_of("tor,tdr->od", grad_resid, mixed_heads)
    grad_mixed = (
        product_of("od,tor->tdr", out_weight, grad_resid).astype(jnp.bfloat16).reshape(split_heads)
    )
    grad_probs = product_of("thdr,uhdr->htur", grad_mixed, value_heads)
    grad_value = product_of("htur,thdr->uhdr", attn_low, grad_mixed).astype(jnp.bfloat16)
    grad_scores = (
        attn_probs
        * (grad_probs - jnp.sum(attn_probs * grad_probs, axis=2, keepdims=True))
        * score_scale
    ).astype(jnp.bfloat16)
    grad_query = product_of("htur,uhdr->thdr", grad_scores, key_heads).astype(jnp.bfloat16)
    grad_key = product_of("htur,thdr->uhdr", grad_scores, query_heads).astype(jnp.bfloat16)
    flat_shape = (tok_count, feat_width, row_count)
    sum_query = product_of("tor,tdr->od", grad_query.reshape(flat_shape), normed_a)
    sum_key = product_of("tor,tdr->od", grad_key.reshape(flat_shape), normed_a)
    sum_value = product_of("tor,tdr->od", grad_value.reshape(flat_shape), normed_a)
    return (jnp.concatenate([sum_query, sum_key, sum_value, sum_out], axis=0), sum_up, sum_down)


def smooth_step(field, edge_tiles, block_lists, send_lists, degree):
    feat_width, node_count = field.shape
    count_blocks = block_lists.shape[0]
    blocks = field.reshape(feat_width, count_blocks, -1)
    outgoing = blocks[:, send_lists[0]]
    incoming = lax.all_to_all(outgoing, "wide", split_axis=1, concat_axis=1, tiled=True)
    block_pool = jnp.concatenate(
        [blocks, incoming.reshape(feat_width, -1, blocks.shape[2])], axis=1
    )
    picked = block_pool[:, block_lists]
    summed = product_of("dbks,bkst->dbt", picked, edge_tiles)
    return (summed / degree[None]).astype(jnp.bfloat16).reshape(feat_width, node_count)


def on_device(
    features,
    edge_tiles,
    block_lists,
    send_lists,
    train_ids,
    owners,
    cotangent,
    query_weight,
    key_weight,
    value_weight,
    out_weight,
    up_weight,
    down_weight,
):
    degree = jnp.sum(edge_tiles, axis=(1, 2), dtype=jnp.float32)
    current = features
    hop_list = []
    for hop_index in range(HOPS):
        applied_once = smooth_step(current, edge_tiles, block_lists, send_lists, degree)
        applied_twice = smooth_step(applied_once, edge_tiles, block_lists, send_lists, degree)
        current = (
            0.5 * current.astype(jnp.float32)
            + applied_once.astype(jnp.float32)
            + applied_twice.astype(jnp.float32)
        ).astype(jnp.bfloat16)
        hop_list.append(current)
    hop_tokens = jnp.stack(hop_list)
    everything = jnp.concatenate([features[None], hop_tokens], axis=0)
    width_local = features.shape[0]
    part_count = lax.axis_size("wide")
    narrow = lax.axis_size("narrow")
    devices = part_count * narrow
    train_rows = train_ids.shape[0]
    onehot = (owners == jnp.arange(devices, dtype=jnp.int32)[None]).astype(jnp.int32)
    counts = lax.psum(jnp.sum(onehot, axis=0), "wide")
    inverse = 1.0 / counts.astype(jnp.float32)
    row_scale = jnp.sum(onehot.astype(jnp.float32) * inverse[None], axis=1)
    scaled = (cotangent.astype(jnp.float32) * row_scale[None, None]).astype(jnp.bfloat16)
    capacity = MB // part_count
    slot_rank = jnp.sum(jnp.cumsum(onehot, axis=0) * onehot, axis=1) - 1
    target = owners[:, 0] * capacity + slot_rank
    row_of = (
        jnp.full((devices * capacity,), train_rows, jnp.int32)
        .at[target]
        .set(jnp.arange(train_rows, dtype=jnp.int32))
    )
    filled = row_of < train_rows
    safe_row = jnp.minimum(row_of, train_rows - 1)
    node_of = train_ids[safe_row]
    out_tokens = jnp.where(filled[None, None], everything[:, :, node_of], 0)
    out_grads = jnp.where(filled[None, None], scaled[:, :, safe_row], 0)
    slot_shape = (TOKS, width_local, part_count, narrow, capacity)
    rows_in, grads_in = (
        lax.all_to_all(
            lax.all_to_all(
                out_tokens.reshape(slot_shape), "wide", split_axis=2, concat_axis=4, tiled=True
            ),
            "narrow",
            split_axis=3,
            concat_axis=1,
            tiled=True,
        ),
        lax.all_to_all(
            lax.all_to_all(
                out_grads.reshape(slot_shape), "wide", split_axis=2, concat_axis=4, tiled=True
            ),
            "narrow",
            split_axis=3,
            concat_axis=1,
            tiled=True,
        ),
    )
    full_width = width_local * narrow
    local_sums = layer_grads(
        rows_in.reshape(TOKS, full_width, -1),
        grads_in.reshape(TOKS, full_width, -1),
        query_weight,
        key_weight,
        value_weight,
        out_weight,
        up_weight,
        down_weight,
    )
    attn_part, up_part, down_part = local_sums
    grad_attn, grad_up, grad_down = (
        lax.psum_scatter(attn_part, ("wide", "narrow"), scatter_dimension=0, tiled=True),
        lax.psum_scatter(up_part, ("wide", "narrow"), scatter_dimension=0, tiled=True),
        lax.psum_scatter(down_part, ("wide", "narrow"), scatter_dimension=0, tiled=True),
    )
    return (hop_tokens, grad_attn, grad_up, grad_down)


def solution(mesh):
    in_specs = (
        P("narrow", "wide"),
        P("wide", None, None, None),
        P("wide", None),
        P("wide", None, None),
        P("wide"),
        P("wide", None),
        P(None, "narrow", "wide"),
        P(),
        P(),
        P(),
        P(),
        P(),
        P(),
    )
    out_specs = (
        P(None, "narrow", "wide"),
        P(("wide", "narrow"), None),
        P(("wide", "narrow"), None),
        P(("wide", "narrow"), None),
    )
    return jax.shard_map(
        on_device, mesh=mesh, in_specs=in_specs, out_specs=out_specs, check_vma=False
    )
```

profile of v0, /device:TPU:0, one launch (start us, length us, event | category | flops | bytes accessed | tf_op | source)
XLA Modules:
  0.0 2355.2 jit_solution(9502972488111874107)
XLA Ops:
  10.8 8.1 all-to-all-start
  19.9 7.4 convert_reduce_fusion
  27.2 3.2 all-to-all-done
  32.6 13.3 gather_fusion.1
  45.9 9.0 fusion.61
  56.4 4.2 all-to-all-start.1
  60.9 10.6 all-to-all-done.1
  73.6 13.3 gather_fusion.3
  87.0 9.0 convert_bitcast_fusion.2
  98.6 3.6 all-to-all-start.2
  102.6 18.1 psum.7
  122.8 13.3 gather_fusion.5
  136.1 9.0 fusion.62
  146.5 4.0 all-to-all-start.3
  150.6 10.1 all-to-all-done.3
  162.8 13.3 gather_fusion.7
  176.2 9.0 convert_bitcast_fusion.1
  187.7 3.6 all-to-all-start.4
  191.6 2.6 scatter_custom_fusion
  195.2 6.2 all-to-all-done.4
  203.5 13.3 gather_fusion.9
  216.9 9.1 fusion.63
  227.4 4.5 all-to-all-start.5
  231.9 3.9 copy.297
  236.9 6.9 gather_fusion.12
  243.7 8.6 gather_fusion.14
  252.3 2.4 copy.315
  254.9 3.9 copy.298
  258.8 3.8 copy.299
  263.9 13.3 gather_fusion.11
  277.3 9.0 convert_bitcast_fusion
  286.5 3.9 copy.300
  290.4 14.8 pad_maximum_fusion
  305.2 9.7 gather_fusion.13
  316.3 2.5 broadcast_select_fusion
  319.8 3.0 reshape.397
  322.9 7.3 all-to-all-start.6
  332.4 3.0 reshape.399
  335.4 5.0 all-to-all-done.6
  341.2 3.6 all-to-all-start.8
  344.8 3.0 reshape.398
  347.8 2.5 copy_bitcast_fusion.1
  355.7 4.3 all-to-all-start.7
  360.0 3.0 reshape.400
  363.0 2.5 copy_bitcast_fusion
  367.9 2.5 all-to-all-done.7
  370.3 4.2 all-to-all-start.9
  376.1 2.6 copy.325
  400.0 7.0 fusion.94
  407.0 3.9 fusion.31
  416.1 3.3 fusion.19
  421.2 5.9 convolution_bitcast_fusion
  427.4 6.5 fusion.8
  435.3 3.3 convolution_bitcast_fusion.1
  440.7 3.2 fusion.93
  448.5 2.6 copy.329
  451.0 4.1 fusion.97
  455.1 8.3 fusion.32
  465.6 7.8 fusion.33
  475.7 4.2 fusion.34
  486.4 2.4 pad_maximum_fusion.1
  492.2 577.6 %reduce-scatter.8.cloned.1.call-done = f32[16,512]{1,0:T(8,128)} async-done(((f32[2048,512]{1,0:T(8,128)}), f32[16,512]{1,0:T(8,128)}) %reduce-scatter.8.cloned.1.call-update) | async-done | bytes 32784 | tf_op jit(solution)/shard_map/reduce_scatter | solution.py:203
  1069.8 639.3 %reduce-scatter.6.cloned.1.call-done = f32[16,512]{1,0:T(8,128)} async-done(((f32[2048,512]{1,0:T(8,128)}), f32[16,512]{1,0:T(8,128)}) %reduce-scatter.6.cloned.1.call-update) | async-done | bytes 32784 | tf_op jit(solution)/shard_map/reduce_scatter | solution.py:202
  1709.1 639.2 %reduce-scatter.4.cloned.1.call-done = f32[16,512]{1,0:T(8,128)} async-done(((f32[2048,512]{1,0:T(8,128)}), f32[16,512]{1,0:T(8,128)}) %reduce-scatter.4.cloned.1.call-update) | async-done | bytes 32784 | tf_op jit(solution)/shard_map/reduce_scatter | solution.py:201
  (174 shorter events, 94.8 us)
Async XLA Ops:
  7.2 408.9 %copy-start = (bf16[2048,512]{1,0:T(8,128)(2,1)S(1)}, bf16[2048,512]{1,0:T(8,128)(2,1)}, u32[]{:S(2)}) copy-start(bf16[2048,512]{1,0:T(8,128)(2,1)} %param.24) | copy-start | bytes 6291460
  9.4 17.8 copy-start.24
  10.8 19.7 all-to-all-start
  30.5 0.8 copy-start.34
  45.9 14.7 copy-start.37
  55.0 16.6 copy-start.20
  56.4 15.2 all-to-all-start.1
  71.5 0.8 copy-start.36
  87.0 9.0 copy-start.12
  87.0 9.0 copy-start.21
  96.2 0.8 copy-start.2
  97.2 23.4 copy-start.22
  98.6 22.0 all-to-all-start.2
  120.7 0.8 copy-start.32
  145.1 15.6 copy-start.18
  146.5 14.1 all-to-all-start.3
  160.7 0.8 copy-start.35
  176.1 9.0 copy-start.3
  176.1 9.0 copy-start.19
  185.4 0.8 copy-start.6
  186.3 15.1 copy-start.23
  187.7 13.7 all-to-all-start.4
  201.4 0.8 copy-start.33
  216.9 15.0 copy-start.13
  226.0 9.8 copy-start.16
  226.0 10.9 copy-start.1
  227.4 35.2 %all-to-all-start.5 = ((bf16[64,16,2,128]{3,0,2,1:T(8,128)(2,1)}), bf16[64,16,2,128]{3,0,2,1:T(8,128)(2,1)}, u32[]{:S(2)}, u32[]{:S(2)}) async-start(bf16[64,16,2,128]{3,0,2,1:T(8,128)(2,1)} %bitcast.423), calls=%async_computation.5 | async-start | bytes 1048576 | tf_op jit(solution)/shard_map/all_to_all | solution.py:106
  235.8 19.1 copy-start.4
  236.9 21.9 copy-start.7
  277.3 9.0 copy-start.8
  277.3 9.0 copy-start.17
  286.5 18.7 copy-start.14
  322.9 17.5 all-to-all-start.6
  340.4 0.8 copy-start.26
  341.2 13.7 all-to-all-start.8
  354.9 0.8 copy-start.25
  355.7 14.7 all-to-all-start.7
  370.3 49.0 %all-to-all-start.9 = ((bf16[4,64,1,8,128]{4,1,2,0,3:T(8,128)(2,1)}), bf16[4,64,1,8,128]{4,1,2,0,3:T(8,128)(2,1)}, u32[]{:S(2)}, u32[]{:S(2)}) async-start(bf16[4,64,1,8,128]{4,1,2,0,3:T(8,128)(2,1)} %copy.318), calls=%async_computation.9 | async-start | bytes 1048576 | tf_op jit(solution)/shard_map/all_to_all | solution.py:178
  374.5 695.3 %reduce-scatter.8.cloned.1.call-start = ((), (), s32[]{:S(2)}) async-start(), calls=%async_computation.15 | async-start | bytes 4227072 | tf_op jit(solution)/shard_map/reduce_scatter | solution.py:203
  415.2 0.8 copy-start.9
  420.4 0.8 copy-start.29
  427.2 1281.9 %reduce-scatter.6.cloned.1.call-start = ((), (), s32[]{:S(2)}) async-start(), calls=%async_computation.14 | async-start | bytes 4227072 | tf_op jit(solution)/shard_map/reduce_scatter | solution.py:202
  427.4 7.8 copy-start.10
  433.9 1.3 copy-start.38
  438.6 1909.7 %reduce-scatter.4.cloned.1.call-start = ((), (), s32[]{:S(2)}) async-start(), calls=%async_computation.13 | async-start | bytes 4227072 | tf_op jit(solution)/shard_map/reduce_scatter | solution.py:201
  440.7 3.2 copy-start.11
  440.7 3.2 copy-start.27
  440.7 4.4 copy-start.28
  444.4 0.8 copy-start.15
  482.2 3.3 copy-start.30
  482.2 3.8 copy-start.31
  488.8 1.0 copy-start.5
Sparse Core Ops, SparseCore 0:
  427.3 642.4 reduce-scatter.7
  1072.8 636.2 reduce-scatter.5
  1712.0 636.1 reduce-scatter.3
where the time goes:
time: 2370 us; the launch traced here: 2360 us
  waiting for transfers between devices  1900 us (80%)
  local copies, waits for them, and re-layouts  208 us (9%)
  matrix products  126 us (5%)
  starting transfers between devices  47.8 us (2%)
  other arithmetic  44.5 us (2%)
    reduce_scatter x1, waiting for transfers between devices, on_device(): lax.psum_scatter(up_part, ('wide', 'narrow'), scatter_dimension=0, tiled=...  639 us
    reduce_scatter x1, waiting for transfers between devices, on_device(): lax.psum_scatter(attn_part, ('wide', 'narrow'), scatter_dimension=0, tile...  639 us
    reduce_scatter x1, waiting for transfers between devices, on_device(): lax.psum_scatter(down_part, ('wide', 'narrow'), scatter_dimension=0, tile...  578 us
    dot_general x25, matrix products, product_of(): jnp.einsum(pattern, first_arg, second_arg, preferred_element_type=jnp.flo...  119 us
    gather x6, local copies, waits for them, and re-layouts, smooth_step(): picked = block_pool[:, block_lists]  80.1 us
  transfers between devices with their start and end apart: 13, of which 10 were waited for; matrix products, arithmetic and copies ran while one was open for 7% of the time, Pallas kernels for 0%

commit v1 on v0

v1 whole, which is shorter than its diff:
```python
import functools
import math

import jax
import jax.numpy as jnp
from jax import lax
from jax.experimental import pallas as pl
from jax.experimental.pallas import tpu as pltpu
from jax.sharding import Mesh, PartitionSpec as P

D = 512
FF = 2048
HEADS = 8
HEAD_DIM = 64
HOPS = 3
TOKS = 4
BLK = 128
K = 12
SEND = 2
NB = 32
PARTS = 16
FEATS = 64
NODES = NB * BLK
TRAIN = 512
CHIP_NODES = 128
NARROW = 8
CHIPS = 64
GROUP = 16
STEP_BLOCKS = 4
FF_CHUNK = 256
EPSILON = 1e-05

BF = jnp.bfloat16
F32 = jnp.float32
WIDE = ("z", "y")
NARROW_AXES = ("x", "c")
ALL_CHIPS = ("z", "y", "x")


def params(limit_mib):
    return pltpu.CompilerParams(vmem_limit_bytes=limit_mib * 1024 * 1024)


def dot(left, right):
    return jnp.dot(left, right, preferred_element_type=F32)


def dot_rows(left, right):
    return lax.dot_general(left, right, (((1,), (1,)), ((), ())), preferred_element_type=F32)


def pack_kernel(sends, field, outgoing):
    for slot in range(PARTS * SEND):
        start = pl.multiple_of(sends[slot] * BLK, BLK)
        rows = (slot % SEND) * FEATS
        outgoing[slot // SEND, rows : rows + FEATS, :] = field[:, pl.ds(start, BLK)]


def pack(sends, field):
    return pl.pallas_call(
        pack_kernel,
        out_shape=jax.ShapeDtypeStruct((PARTS, SEND * FEATS, BLK), BF),
        in_specs=[
            pl.BlockSpec(memory_space=pltpu.SMEM),
            pl.BlockSpec((FEATS, NODES), lambda: (0, 0)),
        ],
        compiler_params=params(16),
        name="pack",
    )(sends, field)


def apply_kernel(*refs, second, last, counted):
    refs = list(refs)
    lists, sends, tiles, field, incoming, degree = refs[:6]
    refs = refs[6:]
    previous = refs.pop(0) if second else None
    counts = refs.pop(0) if counted else None
    if second:
        refs.pop(0)
    result = refs.pop(0)
    hops = refs.pop(0) if second else None
    outgoing = None if last else refs.pop(0)
    pool, fresh = refs
    step = pl.program_id(0)

    @pl.when(step == 0)
    def _():
        for j in range(NB):
            pool[j] = field[:, j * BLK : (j + 1) * BLK]
        for j in range(PARTS * SEND):
            rows = (j % SEND) * FEATS
            pool[NB + j] = incoming[j // SEND, rows : rows + FEATS, :]

    for g in range(STEP_BLOCKS):
        b = step * STEP_BLOCKS + g
        picked = jnp.concatenate([pool[lists[b, k]] for k in range(K)], axis=1)
        summed = dot(picked, tiles[g].reshape(K * BLK, BLK))
        value = (summed / degree[pl.ds(b, 1), :]).astype(BF)
        cols = pl.ds(pl.multiple_of(b * BLK, BLK), BLK)
        if second:
            value = (
                0.5 * previous[:, cols].astype(F32) + pool[b].astype(F32) + value.astype(F32)
            ).astype(BF)
            hops[0, :, cols] = value
        result[:, cols] = value
        fresh[b] = value

    if not last:

        @pl.when(step == NB // STEP_BLOCKS - 1)
        def _():
            for slot in range(PARTS * SEND):
                rows = (slot % SEND) * FEATS
                outgoing[slot // SEND, rows : rows + FEATS, :] = fresh[sends[slot]]
            if counted:
                for p in range(PARTS):
                    outgoing[p, SEND * FEATS :, :] = jnp.broadcast_to(
                        counts[...], (GROUP, BLK)
                    ).astype(BF)


def apply(lists, sends, tiles, field, incoming, degree, previous=None, hops=None, hop=0, counts=None):
    second = previous is not None
    last = second and hop == HOPS - 1
    counted = counts is not None
    whole = lambda *shape: pl.BlockSpec(shape, lambda i: (0,) * len(shape))
    smem = pl.BlockSpec(memory_space=pltpu.SMEM)
    operands = [lists, sends, tiles, field, incoming, degree]
    in_specs = [
        smem,
        smem,
        pl.BlockSpec((STEP_BLOCKS, K, BLK, BLK), lambda i: (i, 0, 0, 0)),
        whole(FEATS, NODES),
        whole(*incoming.shape),
        whole(NB, BLK),
    ]
    out_shape = [jax.ShapeDtypeStruct((FEATS, NODES), BF)]
    out_specs = [whole(FEATS, NODES)]
    aliases = {}
    if second:
        operands.append(previous)
        in_specs.append(whole(FEATS, NODES))
    if counted:
        operands.append(counts)
        in_specs.append(whole(1, BLK))
    if second:
        if hops is None:
            operands.append(counts_stub(sends))
            in_specs.append(smem)
        else:
            aliases = {len(operands): 1}
            operands.append(hops)
            in_specs.append(pl.BlockSpec(memory_space=pl.ANY))
        out_shape.append(jax.ShapeDtypeStruct((HOPS, FEATS, NODES), BF))
        out_specs.append(pl.BlockSpec((1, FEATS, NODES), lambda i: (hop, 0, 0)))
    if not last:
        rows = SEND * FEATS + (GROUP if counted else 0)
        out_shape.append(jax.ShapeDtypeStruct((PARTS, rows, BLK), BF))
        out_specs.append(whole(PARTS, rows, BLK))
    return pl.pallas_call(
        functools.partial(apply_kernel, second=second, last=last, counted=counted),
        grid=(NB // STEP_BLOCKS,),
        out_shape=out_shape,
        in_specs=in_specs,
        out_specs=out_specs,
        scratch_shapes=[
            pltpu.VMEM((2 * NB, FEATS, BLK), BF),
            pltpu.VMEM((NB, FEATS, BLK), BF),
        ],
        input_output_aliases=aliases,
        compiler_params=params(32),
        name=f"apply_{'second' if second else 'first'}_{hop}",
    )(*operands)


def counts_stub(sends):
    return sends


def pick_field(field, ids):
    total = None
    for b in range(NB):
        rows = lax.broadcasted_iota(jnp.int32, (BLK, TRAIN), 0) + b * BLK
        chosen = jnp.where(rows == ids, 1.0, 0.0).astype(BF)
        term = dot(field[:, b * BLK : (b + 1) * BLK], chosen)
        total = term if total is None else total + term
    return total.astype(BF)


def pick_kernel(ids, *refs, with_grads):
    refs = list(refs)
    out = refs.pop()
    grads = refs.pop() if with_grads else None
    id_row = ids[...]
    for index, field in enumerate(refs):
        picked = pick_field(field, id_row)
        for n in range(NARROW):
            x = n // 2
            out[n, index * FEATS : (index + 1) * FEATS, :] = picked[
                :, x * CHIP_NODES : (x + 1) * CHIP_NODES
            ]
    if with_grads:
        base = len(refs) * FEATS
        for n in range(NARROW):
            x = n // 2
            out[n, base:, :] = grads[:, x * CHIP_NODES : (x + 1) * CHIP_NODES]


def pick(ids, fields, grads=None):
    rows = FEATS * len(fields) + (0 if grads is None else TOKS * FEATS)
    operands = [ids, *fields] + ([] if grads is None else [grads])
    return pl.pallas_call(
        functools.partial(pick_kernel, with_grads=grads is not None),
        out_shape=jax.ShapeDtypeStruct((NARROW, rows, CHIP_NODES), BF),
        compiler_params=params(32),
        name=f"pick_{len(fields)}_{rows}",
    )(*operands)


def layer_kernel(
    core, first, middle, final, scale, query_w, key_w, value_w, out_w, out_t, up_w, up_t, down_w,
    result, query_s, key_s, value_s, mixed_s, probs_s, act_s, pre_s, gmix_s, gq_s, gk_s, gv_s, gr_s,
):
    own = core[0]
    width = TOKS * CHIP_NODES
    tokens = jnp.concatenate(
        [
            first[:, 0:FEATS, :].reshape(D, CHIP_NODES),
            middle[:, 0:FEATS, :].reshape(D, CHIP_NODES),
            middle[:, FEATS : 2 * FEATS, :].reshape(D, CHIP_NODES),
            final[...].reshape(D, CHIP_NODES),
        ],
        axis=1,
    )
    row_scale = scale[...]
    scaled = jnp.concatenate(
        [
            (
                first[:, (t + 1) * FEATS : (t + 2) * FEATS, :].reshape(D, CHIP_NODES).astype(F32)
                * row_scale
            ).astype(BF)
            for t in range(TOKS)
        ],
        axis=1,
    )

    def normalize(hidden):
        center = hidden - jnp.mean(hidden, axis=0, keepdims=True)
        inverse = lax.rsqrt(jnp.mean(center * center, axis=0, keepdims=True) + EPSILON)
        return center * inverse, inverse

    normed_a = normalize(tokens.astype(F32))[0].astype(BF)
    query_s[...] = dot(query_w[...], normed_a).astype(BF)
    key_s[...] = dot(key_w[...], normed_a).astype(BF)
    value_s[...] = dot(value_w[...], normed_a).astype(BF)
    score_scale = 1.0 / math.sqrt(HEAD_DIM)

    def parts(ref, rows):
        block = ref[rows, :].astype(F32)
        return [block[:, t * CHIP_NODES : (t + 1) * CHIP_NODES] for t in range(TOKS)]

    def forward_head(h, carry):
        rows = pl.ds(pl.multiple_of(h * HEAD_DIM, HEAD_DIM), HEAD_DIM)
        query, key, value = parts(query_s, rows), parts(key_s, rows), parts(value_s, rows)
        all_probs = []
        mixed = []
        for t in range(TOKS):
            scores = [
                jnp.sum(query[t] * key[u], axis=0, keepdims=True) * score_scale
                for u in range(TOKS)
            ]
            top = jnp.maximum(
                jnp.maximum(scores[0], scores[1]), jnp.maximum(scores[2], scores[3])
            )
            raised = [jnp.exp(s - top) for s in scores]
            total = raised[0] + raised[1] + raised[2] + raised[3]
            probs = [r / total for r in raised]
            all_probs += probs
            low = [p.astype(BF).astype(F32) for p in probs]
            mixed.append(
                low[0] * value[0] + low[1] * value[1] + low[2] * value[2] + low[3] * value[3]
            )
        probs_s[h] = jnp.concatenate(all_probs, axis=0)
        mixed_s[rows, :] = jnp.concatenate(mixed, axis=1).astype(BF)
        return carry

    lax.fori_loop(0, HEADS, forward_head, 0)
    residual = (tokens.astype(F32) + dot(out_w[...], mixed_s[...])).astype(BF)
    second_norm, second_inv = normalize(residual.astype(F32))
    normed_b = second_norm.astype(BF)

    root = math.sqrt(2.0 / math.pi)
    groups = FF_CHUNK // (2 * GROUP)

    def ffn_chunk(i, carry):
        rows = pl.ds(pl.multiple_of(i * FF_CHUNK, FF_CHUNK), FF_CHUNK)
        pre = dot(up_w[rows, :], normed_b)
        grad_act = dot(down_w[rows, :], scaled)
        square = pre * pre
        gate = 0.5 + 0.5 * jnp.tanh(pre * (root + (root * 0.044715) * square))
        activated = pre * gate
        slope = gate + activated * (1.0 - gate) * (
            2.0 * root + (6.0 * root * 0.044715) * square
        )
        at = pl.ds(i * groups, groups)
        act_s[at] = activated.astype(BF).reshape(groups, 2, GROUP, width)
        pre_s[at] = (grad_act * slope).astype(BF).reshape(groups, 2, GROUP, width)
        return carry

    lax.fori_loop(0, FF // FF_CHUNK, ffn_chunk, 0)

    half = FF // 2
    grad_down = dot_rows(act_s[:, own].reshape(half, width), scaled)
    result[:, 2 * GROUP : 3 * GROUP, :] = grad_down.astype(BF).reshape(CHIPS, GROUP, D)
    grad_up = dot_rows(pre_s[:, own].reshape(half, width), normed_b)
    result[:, GROUP : 2 * GROUP, :] = grad_up.astype(BF).reshape(CHIPS, GROUP, D)

    grad_normed = dot(up_t[...], pre_s[...].reshape(FF, width))
    grad_resid = (
        scaled.astype(F32)
        + second_inv
        * (
            grad_normed
            - jnp.mean(grad_normed, axis=0, keepdims=True)
            - second_norm * jnp.mean(grad_normed * second_norm, axis=0, keepdims=True)
        )
    ).astype(BF)
    gr_s[...] = grad_resid.reshape(GROUP, 2, GROUP, width)
    gmix_s[...] = dot(out_t[...], grad_resid).astype(BF)

    def backward_head(h, carry):
        rows = pl.ds(pl.multiple_of(h * HEAD_DIM, HEAD_DIM), HEAD_DIM)
        query, key, value = parts(query_s, rows), parts(key_s, rows), parts(value_s, rows)
        grad_mixed = parts(gmix_s, rows)
        saved = probs_s[h]
        prob = lambda t, u: saved[t * TOKS + u : t * TOKS + u + 1, :]
        weights = []
        grad_query = []
        for t in range(TOKS):
            grad_probs = [
                jnp.sum(grad_mixed[t] * value[u], axis=0, keepdims=True) for u in range(TOKS)
            ]
            inner = sum(prob(t, u) * grad_probs[u] for u in range(TOKS))
            weight = [
                (prob(t, u) * (grad_probs[u] - inner) * score_scale).astype(BF).astype(F32)
                for u in range(TOKS)
            ]
            weights.append(weight)
            grad_query.append(sum(weight[u] * key[u] for u in range(TOKS)))
        grad_key = [sum(weights[t][u] * query[t] for t in range(TOKS)) for u in range(TOKS)]
        grad_value = [
            sum(prob(t, u).astype(BF).astype(F32) * grad_mixed[t] for t in range(TOKS))
            for u in range(TOKS)
        ]
        at = pl.ds(h * 2, 2)
        for ref, pieces in ((gq_s, grad_query), (gk_s, grad_key), (gv_s, grad_value)):
            ref[at] = jnp.concatenate(pieces, axis=1).astype(BF).reshape(2, 2, GROUP, width)
        return carry

    lax.fori_loop(0, HEADS, backward_head, 0)
    quarter = D // 2
    stacked = jnp.concatenate(
        [ref[:, own].reshape(quarter, width) for ref in (gq_s, gk_s, gv_s)], axis=0
    )
    count = GROUP * 3
    result[:count, 0:GROUP, :] = dot_rows(stacked, normed_a).astype(BF).reshape(count, GROUP, D)
    sum_out = dot_rows(gr_s[:, own].reshape(quarter, width), mixed_s[...])
    result[count:, 0:GROUP, :] = sum_out.astype(BF).reshape(GROUP, GROUP, D)


def layer(core, first, middle, final, scale, *weights):
    width = TOKS * CHIP_NODES
    square = pltpu.VMEM((D, width), BF)
    grouped = pltpu.VMEM((GROUP, 2, GROUP, width), BF)
    wide = pltpu.VMEM((CHIPS, 2, GROUP, width), BF)
    vmem = pl.BlockSpec(memory_space=pltpu.VMEM)
    return pl.pallas_call(
        layer_kernel,
        out_shape=jax.ShapeDtypeStruct((CHIPS, 3 * GROUP, D), BF),
        in_specs=[pl.BlockSpec(memory_space=pltpu.SMEM)] + [vmem] * 12,
        scratch_shapes=[
            square, square, square, square,
            pltpu.VMEM((HEADS, TOKS * TOKS, CHIP_NODES), F32),
            wide, wide, square, grouped, grouped, grouped, grouped,
        ],
        compiler_params=params(56),
        name="layer",
    )(core, first, middle, final, scale, *weights)


def exchange(array, axes):
    return lax.all_to_all(array, axes, split_axis=0, concat_axis=0, tiled=True)


def on_device(
    features, edge_tiles, block_lists, send_lists, train_ids, owners, cotangent,
    query_weight, key_weight, value_weight, out_weight, up_weight, down_weight,
):
    sends = send_lists.reshape(-1)
    ids = train_ids.reshape(1, TRAIN)
    degree = jnp.sum(edge_tiles, axis=(1, 2), dtype=F32)
    named = (owners == jnp.arange(CHIPS * 2, dtype=jnp.int32)[None]).astype(F32)
    counts = jnp.sum(named, axis=0, keepdims=True)

    incoming = exchange(pack(sends, features), WIDE)
    first_rows = exchange(pick(ids, [features], cotangent.reshape(TOKS * FEATS, TRAIN)), NARROW_AXES)
    current = features
    hops = None
    fields = []
    for hop in range(HOPS):
        once, outgoing = apply(
            block_lists, sends, edge_tiles, current, incoming, degree,
            hop=hop, counts=counts if hop == 0 else None,
        )
        incoming = exchange(outgoing, WIDE)
        if hop == 0:
            total_counts = jnp.sum(incoming[:, SEND * FEATS, :].astype(F32), axis=0)
        results = apply(
            block_lists, sends, edge_tiles, once, incoming, degree,
            previous=current, hops=hops, hop=hop,
        )
        current, hops = results[0], results[1]
        fields.append(current)
        if hop < HOPS - 1:
            incoming = exchange(results[2], WIDE)
        if hop == 1:
            middle_rows = exchange(pick(ids, fields), NARROW_AXES)
    final_rows = exchange(pick(ids, [current]), NARROW_AXES)

    mine = lax.dynamic_slice(owners.reshape(-1), (lax.axis_index("x") * CHIP_NODES,), (CHIP_NODES,))
    owner_of = jnp.arange(CHIPS * 2, dtype=jnp.int32)[:, None] == mine[None, :]
    scale = jnp.sum(
        jnp.where(owner_of, (1.0 / total_counts)[:, None], 0.0), axis=0, keepdims=True
    )
    core = lax.axis_index("c").astype(jnp.int32).reshape(1)
    partial = layer(
        core, first_rows, middle_rows, final_rows, scale,
        query_weight, key_weight, value_weight, out_weight, out_weight.T,
        up_weight, up_weight.T, down_weight,
    )
    gathered = exchange(partial, ALL_CHIPS)
    sums = jnp.sum(gathered.astype(F32), axis=0)
    return (hops, sums[:GROUP], sums[GROUP : 2 * GROUP], sums[2 * GROUP :])


def solution(mesh):
    split = Mesh(mesh.devices.reshape(4, 4, 4, 2), ("z", "y", "x", "c"))
    rows = P(WIDE + NARROW_AXES, None)
    in_specs = (
        P(NARROW_AXES, WIDE),
        P(WIDE, None, None, None),
        P(WIDE, None),
        P(WIDE, None, None),
        P(WIDE),
        P(WIDE, None),
        P(None, NARROW_AXES, WIDE),
        P(), P(), P(), P(), P(), P(),
    )
    out_specs = (P(None, NARROW_AXES, WIDE), rows, rows, rows)
    return jax.shard_map(
        on_device, mesh=split, in_specs=in_specs, out_specs=out_specs, check_vma=False
    )
```

time: 2370 us -> 236 us (0.10)
  waiting for transfers between devices: 1900 us -> 27.9 us
  local copies, waits for them, and re-layouts: 208 us -> 24.4 us
  matrix products: 126 us -> 0 us
  blocking collectives: 18.1 us -> 89 us
  Pallas kernels: 0 us -> 55.4 us
  other arithmetic: 44.5 us -> 9.38 us
    reduce_scatter x3 -> x0, waiting for transfers between devices: 1860 us -> none  [the longest x1 639 us: on_device(): lax.psum_scatter(up_part, ('wide', 'narrow'), scatter_dimension=0, tiled=...]
    dot_general x25 -> x0, matrix products: 119 us -> none  [product_of(): jnp.einsum(pattern, first_arg, second_arg, preferred_element_type=jnp.flo...]
    gather x17 -> x0, local copies, waits for them, and re-layouts: 117 us -> none  [the longest x6 80.1 us: smooth_step(): picked = block_pool[:, block_lists]]
    all_to_all x0 -> x4, blocking collectives: none -> 89 us  [exchange(): return lax.all_to_all(array, axes, split_axis=0, concat_axis=0, tiled=True)]
    pallas_call x0 -> x11, Pallas kernels: none -> 55.4 us  [the longest x6 30.6 us: apply(): pl.pallas_call(functools.partial(apply_kernel, second=second, last=last,...]
    concatenate x8 -> x0, other arithmetic: 25 us -> none  [the longest x1 14.8 us: on_device(): everything = jnp.concatenate([features[None], hop_tokens], axis=0)]
  transfers between devices with their start and end apart: 13 -> 6, of which waited for: 10 -> 5; matrix products, arithmetic and copies ran while one was open for 7% -> 7% of each run, Pallas kernels for 0% -> 7%
where the time goes in v1:
time: 236 us; the launch traced here: 235 us
  blocking collectives  89 us (38%)
  Pallas kernels  55.4 us (23%)
  starting transfers between devices  28.3 us (12%)
  waiting for transfers between devices  27.9 us (12%)
  local copies, waits for them, and re-layouts  24.4 us (10%)
  other arithmetic  9.38 us (4%)
    all_to_all x4, blocking collectives, exchange(): return lax.all_to_all(array, axes, split_axis=0, concat_axis=0, tiled=True)  89 us
    pallas_call x6, Pallas kernels, apply(): pl.pallas_call(functools.partial(apply_kernel, second=second, last=last,...  30.6 us
    all_to_all x6, starting transfers between devices, exchange(): return lax.all_to_all(array, axes, split_axis=0, concat_axis=0, tiled=True)  28.3 us
    all_to_all x6, waiting for transfers between devices, exchange(): return lax.all_to_all(array, axes, split_axis=0, concat_axis=0, tiled=True)  27.9 us
    unnamed x22, local copies, waits for them, and re-layouts  23 us
    pallas_call x1, Pallas kernels, layer(): pl.pallas_call(layer_kernel, out_shape=jax.ShapeDtypeStruct((CHIPS, 3 * G...  18.4 us
    reduce_sum x1, other arithmetic, on_device(): degree = jnp.sum(edge_tiles, axis=(1, 2), dtype=F32)  7.42 us
    pallas_call x3, Pallas kernels, pick(): pl.pallas_call(functools.partial(pick_kernel, with_grads=grads is not Non...  5.02 us
  transfers between devices with their start and end apart: 6, of which 5 were waited for; matrix products, arithmetic and copies ran while one was open for 7% of the time, Pallas kernels for 7%

profile of v1, /device:TPU:0, one launch (start us, length us, event | category | flops | bytes accessed | tf_op | source)
XLA Modules:
  0.0 235.1 jit_solution(3180062211403895831)
XLA Ops:
  0.6 0.8 copy.37
  1.4 0.1 reshape.28.sends.refs_1_.refs_7_
  1.5 0.0 copy-start.3
  1.5 1.0 copy-done.3
  2.5 1.5 pack.1
  4.0 8.1 %all-to-all-start = ((bf16[16,128,128]{2,1,0:T(8,128)(2,1)}), bf16[16,128,128]{2,1,0:T(8,128)(2,1)S(1)}, u32[]{:S(2)}, u32[]{:S(2)}) async-start(bf16[16,128,128]{2,1,0:T(8,128)(2,1)} %pack.1), calls=%async_computation | async-start | bytes 1048576 | tf_op jit(solution)/shard_map/all_to_all | solution.py:392
  12.1 0.8 convert_reduce_fusion.2
  13.0 0.8 copy.43.refs_0_
  13.7 0.0 copy-start.4
  13.7 7.4 %convert_reduce_fusion.refs_5_ = f32[32,128]{1,0:T(8,128)S(1)} fusion(bf16[32,12,128,128]{3,2,1,0:T(8,128)(2,1)} %refs_2_.11), kind=kLoop, calls=%fused_computation | loop fusion | flops 12578816 | bytes 12599296 | tf_op jit(solution)/shard_map/reduce_sum | solution.py:401
  21.2 2.5 %all-to-all-done.refs_4_ = bf16[16,128,128]{2,1,0:T(8,128)(2,1)S(1)} async-done(((bf16[16,128,128]{2,1,0:T(8,128)(2,1)}), bf16[16,128,128]{2,1,0:T(8,128)(2,1)S(1)}, u32[]{:S(2)}, u32[]{:S(2)}) %all-to-all-start) | async-done | bytes 524320 | tf_op jit(solution)/shard_map/all_to_all | solution.py:392
  23.7 0.0 copy-done.4
  23.7 0.0 copy-start
  23.7 4.6 %copy-done = bf16[32,12,128,128]{3,2,1,0:T(8,128)(2,1)S(1)} copy-done((bf16[32,12,128,128]{3,2,1,0:T(8,128)(2,1)S(1)}, bf16[32,12,128,128]{3,2,1,0:T(8,128)(2,1)}, u32[]{:S(2)}) %copy-start) | copy-done | bytes 12582936
  28.2 4.5 %apply_first_0.1 = (bf16[64,4096]{1,0:T(8,128)(2,1)S(1)}, bf16[16,144,128]{2,1,0:T(8,128)(2,1)S(1)}) custom-call(s32[32,12]{1,0:T(8,128)S(1)} %copy.43.refs_0_, s32[32]{0:T(128)S(1)} %reshape.28.sends.refs_1_.refs_7_, bf16[32,12,128,128]{3,2,1,0:T(8,128)(2,1)S(1)} %copy-done, bf16[64,4096]{1,0:T(8,128)(2,1)S(1)} %copy-done.4, ...), custom_call_target="tpu_custom_call" | custom-call | tf_op jit(solution)/shard_map/apply_first_0/pallas_call | solution.py:160
  32.8 16.3 %all_to_all.50.refs_4_ = bf16[16,144,128]{2,1,0:T(8,128)(2,1)S(1)} all-to-all(bf16[16,144,128]{2,1,0:T(8,128)(2,1)S(1)} %get-tuple-element.19), channel_id=1, replica_groups=mesh['z'=4,'y'=4,'x'=4,'c'=2] {'z','y'}, dimensions={0} | all-to-all | bytes 1179648 | tf_op jit(solution)/shard_map/all_to_all | solution.py:392
  49.0 5.4 %apply_second_0.1 = (bf16[64,4096]{1,0:T(8,128)(2,1)S(1)}, bf16[3,64,4096]{2,1,0:T(8,128)(2,1)}, bf16[16,128,128]{2,1,0:T(8,128)(2,1)S(1)}) custom-call(s32[32,12]{1,0:T(8,128)S(1)} %copy.43.refs_0_, s32[32]{0:T(128)S(1)} %reshape.28.sends.refs_1_.refs_7_, bf16[32,12,128,128]{3,2,1,0:T(8,128)(2,1)S(1)} %copy-done, ...), custom_call_target="tpu_custom_call" | custom-call | tf_op jit(solution)/shard_map/apply_second_0/pallas_call | solution.py:160
  54.4 13.3 %all_to_all.51.refs_4_ = bf16[16,128,128]{2,1,0:T(8,128)(2,1)S(1)} all-to-all(bf16[16,128,128]{2,1,0:T(8,128)(2,1)S(1)} %get-tuple-element.21), channel_id=1, replica_groups=mesh['z'=4,'y'=4,'x'=4,'c'=2] {'z','y'}, dimensions={0} | all-to-all | bytes 1048576 | tf_op jit(solution)/shard_map/all_to_all | solution.py:392
  67.7 4.5 %apply_first_1.1 = (bf16[64,4096]{1,0:T(8,128)(2,1)S(1)}, bf16[16,128,128]{2,1,0:T(8,128)(2,1)S(1)}) custom-call(s32[32,12]{1,0:T(8,128)S(1)} %copy.43.refs_0_, s32[32]{0:T(128)S(1)} %reshape.28.sends.refs_1_.refs_7_, bf16[32,12,128,128]{3,2,1,0:T(8,128)(2,1)S(1)} %copy-done, bf16[64,4096]{1,0:T(8,128)(2,1)S(1)} %get-tuple-element.20.refs_3_.refs_6_.refs_0_, ...), custom_call_target="tpu_custom_call" | custom-call | tf_op jit(solution)/shard_map/apply_first_1/pallas_call | solution.py:160
  72.2 13.2 %all_to_all.52.refs_4_ = bf16[16,128,128]{2,1,0:T(8,128)(2,1)S(1)} all-to-all(bf16[16,128,128]{2,1,0:T(8,128)(2,1)S(1)} %get-tuple-element.23), channel_id=1, replica_groups=mesh['z'=4,'y'=4,'x'=4,'c'=2] {'z','y'}, dimensions={0} | all-to-all | bytes 1048576 | tf_op jit(solution)/shard_map/all_to_all | solution.py:392
  85.4 0.0 copy-start.5
  85.4 0.0 copy-start.6
  85.4 5.6 %apply_second_1.1 = (bf16[64,4096]{1,0:T(8,128)(2,1)S(1)}, bf16[3,64,4096]{2,1,0:T(8,128)(2,1)}, bf16[16,128,128]{2,1,0:T(8,128)(2,1)}) custom-call(s32[32,12]{1,0:T(8,128)S(1)} %copy.43.refs_0_, s32[32]{0:T(128)S(1)} %reshape.28.sends.refs_1_.refs_7_, bf16[32,12,128,128]{3,2,1,0:T(8,128)(2,1)S(1)} %copy-done, ...), custom_call_target="tpu_custom_call", output_to_operand_aliasing={{1}: (7, {})} | custom-call | tf_op jit(solution)/shard_map/apply_second_1/pallas_call | solution.py:160
  90.9 3.6 %all-to-all-start.4 = ((bf16[16,128,128]{2,1,0:T(8,128)(2,1)}), bf16[16,128,128]{2,1,0:T(8,128)(2,1)S(1)}, u32[]{:S(2)}, u32[]{:S(2)}) async-start(bf16[16,128,128]{2,1,0:T(8,128)(2,1)} %get-tuple-element.26), calls=%async_computation.4 | async-start | bytes 1048576 | tf_op jit(solution)/shard_map/all_to_all | solution.py:392
  94.5 0.0 copy-done.5
  94.5 0.0 copy-done.6
  94.5 1.6 pick_1_320.1
  96.1 8.5 %all-to-all-done.4.refs_4_ = bf16[16,128,128]{2,1,0:T(8,128)(2,1)S(1)} async-done(((bf16[16,128,128]{2,1,0:T(8,128)(2,1)}), bf16[16,128,128]{2,1,0:T(8,128)(2,1)S(1)}, u32[]{:S(2)}, u32[]{:S(2)}) %all-to-all-start.4) | async-done | bytes 524320 | tf_op jit(solution)/shard_map/all_to_all | solution.py:392
  104.6 4.3 %all-to-all-start.6 = ((bf16[8,320,128]{2,1,0:T(8,128)(2,1)}), bf16[8,320,128]{2,1,0:T(8,128)(2,1)S(1)}, u32[]{:S(2)}, u32[]{:S(2)}) async-start(bf16[8,320,128]{2,1,0:T(8,128)(2,1)} %pick_1_320.1), calls=%async_computation.6 | async-start | bytes 1310720 | tf_op jit(solution)/shard_map/all_to_all | solution.py:392
  108.9 0.0 copy-start.1
  108.9 4.6 %copy-done.1 = bf16[32,12,128,128]{3,2,1,0:T(8,128)(2,1)S(1)} copy-done((bf16[32,12,128,128]{3,2,1,0:T(8,128)(2,1)S(1)}, bf16[32,12,128,128]{3,2,1,0:T(8,128)(2,1)}, u32[]{:S(2)}) %copy-start.1) | copy-done | bytes 12582936
  113.5 5.3 %apply_first_2.1 = (bf16[64,4096]{1,0:T(8,128)(2,1)S(1)}, bf16[16,128,128]{2,1,0:T(8,128)(2,1)}) custom-call(s32[32,12]{1,0:T(8,128)S(1)} %copy.43.refs_0_, s32[32]{0:T(128)S(1)} %reshape.28.sends.refs_1_.refs_7_, bf16[32,12,128,128]{3,2,1,0:T(8,128)(2,1)S(1)} %copy-done.1, bf16[64,4096]{1,0:T(8,128)(2,1)S(1)} %get-tuple-element.25.refs_3_.refs_6_.refs_1_, ...), custom_call_target="tpu_custom_call" | custom-call | tf_op jit(solution)/shard_map/apply_first_2/pallas_call | solution.py:160
  118.8 1.9 all-to-all-done.6.first
  120.7 0.0 copy-start.7
  120.7 3.6 %all-to-all-start.5 = ((bf16[16,128,128]{2,1,0:T(8,128)(2,1)}), bf16[16,128,128]{2,1,0:T(8,128)(2,1)S(1)}, u32[]{:S(2)}, u32[]{:S(2)}) async-start(bf16[16,128,128]{2,1,0:T(8,128)(2,1)} %get-tuple-element.28), calls=%async_computation.5 | async-start | bytes 1048576 | tf_op jit(solution)/shard_map/all_to_all | solution.py:392
  124.3 2.1 pick_2_128.1
  126.4 9.5 %all-to-all-done.5.refs_4_ = bf16[16,128,128]{2,1,0:T(8,128)(2,1)S(1)} async-done(((bf16[16,128,128]{2,1,0:T(8,128)(2,1)}), bf16[16,128,128]{2,1,0:T(8,128)(2,1)S(1)}, u32[]{:S(2)}, u32[]{:S(2)}) %all-to-all-start.5) | async-done | bytes 524320 | tf_op jit(solution)/shard_map/all_to_all | solution.py:392
  135.8 4.0 %all-to-all-start.7 = ((bf16[8,128,128]{2,1,0:T(8,128)(2,1)}), bf16[8,128,128]{2,1,0:T(8,128)(2,1)}, u32[]{:S(2)}, u32[]{:S(2)}) async-start(bf16[8,128,128]{2,1,0:T(8,128)(2,1)} %pick_2_128.1), calls=%async_computation.7 | async-start | bytes 524288 | tf_op jit(solution)/shard_map/all_to_all | solution.py:392
  139.9 2.1 copy.44
  142.0 4.0 %copy.45 = bf16[2048,512]{0,1:T(8,128)(2,1)} copy(bf16[2048,512]{1,0:T(8,128)(2,1)} %up_w.1) | data formatting | bytes 4194304 | tf_op args[11]
  145.9 0.0 copy-done.7
  145.9 0.7 dynamic-slice_bitcast_fusion
  146.6 0.0 copy-start.2
  146.6 4.6 %copy-done.2 = bf16[32,12,128,128]{3,2,1,0:T(8,128)(2,1)S(1)} copy-done((bf16[32,12,128,128]{3,2,1,0:T(8,128)(2,1)S(1)}, bf16[32,12,128,128]{3,2,1,0:T(8,128)(2,1)}, u32[]{:S(2)}) %copy-start.2) | copy-done | bytes 12582936
  151.2 5.3 %apply_second_2.1 = (bf16[64,4096]{1,0:T(8,128)(2,1)S(1)}, bf16[3,64,4096]{2,1,0:T(8,128)(2,1)}) custom-call(s32[32,12]{1,0:T(8,128)S(1)} %copy.43.refs_0_, s32[32]{0:T(128)S(1)} %reshape.28.sends.refs_1_.refs_7_, bf16[32,12,128,128]{3,2,1,0:T(8,128)(2,1)S(1)} %copy-done.2, ...), custom_call_target="tpu_custom_call", output_to_operand_aliasing={{1}: (7, {})} | custom-call | tf_op jit(solution)/shard_map/apply_second_2/pallas_call | solution.py:160
  156.5 1.4 pick_1_64.1
  157.9 0.0 all-to-all-done.7.middle
  157.9 4.7 %all-to-all-start.8 = ((bf16[8,64,128]{2,1,0:T(8,128)(2,1)}), bf16[8,64,128]{2,1,0:T(8,128)(2,1)S(1)}, u32[]{:S(2)}, u32[]{:S(2)}) async-start(bf16[8,64,128]{2,1,0:T(8,128)(2,1)} %pick_1_64.1), calls=%async_computation.8 | async-start | bytes 262144 | tf_op jit(solution)/shard_map/all_to_all | solution.py:392
  162.6 0.6 select_reduce_fusion
  163.2 5.5 %all-to-all-done.8.final = bf16[8,64,128]{2,1,0:T(8,128)(2,1)S(1)} async-done(((bf16[8,64,128]{2,1,0:T(8,128)(2,1)}), bf16[8,64,128]{2,1,0:T(8,128)(2,1)S(1)}, u32[]{:S(2)}, u32[]{:S(2)}) %all-to-all-start.8) | async-done | bytes 131104 | tf_op jit(solution)/shard_map/all_to_all | solution.py:392
  168.7 0.0 copy-start.8
  168.7 0.7 copy-done.8
  169.4 18.4 %layer.1 = bf16[64,48,512]{2,1,0:T(8,128)(2,1)} custom-call(s32[1]{0:T(128)} %bitcast.2.core, bf16[8,320,128]{2,1,0:T(8,128)(2,1)} %copy-done.7, bf16[8,128,128]{2,1,0:T(8,128)(2,1)} %all-to-all-done.7.middle, bf16[8,64,128]{2,1,0:T(8,128)(2,1)} %copy-done.8, f32[1,128]{1,0:T(1,128)} %bitcast.18, bf16[512,512]{1,0:T(8,128)(2,1)} %query_w.1, ...), custom_call_target="tpu_custom_call" | custom-call | tf_op jit(solution)/shard_map/layer/pallas_call | solution.py:377
  187.7 46.2 %all_to_all.53 = bf16[64,48,512]{2,1,0:T(8,128)(2,1)S(1)} all-to-all(bf16[64,48,512]{2,1,0:T(8,128)(2,1)} %layer.1), channel_id=1, replica_groups=mesh['z'=4,'y'=4,'x'=4,'c'=2] {'z','y','x'}, dimensions={0} | all-to-all | bytes 6291456 | tf_op jit(solution)/shard_map/all_to_all | solution.py:392
  234.0 0.5 convert_reduce_fusion.1
  234.4 0.6 fusion.1
  (2 shorter events, 0.0 us)
Async XLA Ops:
  1.5 1.0 copy-start.3
  4.0 19.7 %all-to-all-start = ((bf16[16,128,128]{2,1,0:T(8,128)(2,1)}), bf16[16,128,128]{2,1,0:T(8,128)(2,1)S(1)}, u32[]{:S(2)}, u32[]{:S(2)}) async-start(bf16[16,128,128]{2,1,0:T(8,128)(2,1)} %pack.1), calls=%async_computation | async-start | bytes 1048576 | tf_op jit(solution)/shard_map/all_to_all | solution.py:392
  13.7 9.9 %copy-start.4 = (bf16[64,4096]{1,0:T(8,128)(2,1)S(1)}, bf16[64,4096]{1,0:T(8,128)(2,1)}, u32[]{:S(2)}) copy-start(bf16[64,4096]{1,0:T(8,128)(2,1)} %refs_0_.7) | copy-start | bytes 1572868
  23.7 4.6 %copy-start = (bf16[32,12,128,128]{3,2,1,0:T(8,128)(2,1)S(1)}, bf16[32,12,128,128]{3,2,1,0:T(8,128)(2,1)}, u32[]{:S(2)}) copy-start(bf16[32,12,128,128]{3,2,1,0:T(8,128)(2,1)} %refs_2_.11) | copy-start | bytes 37748740
  85.4 9.1 %copy-start.5 = (bf16[4,64,512]{2,1,0:T(8,128)(2,1)S(1)}, bf16[4,64,512]{2,1,0:T(8,128)(2,1)}, u32[]{:S(2)}) copy-start(bf16[4,64,512]{2,1,0:T(8,128)(2,1)} %param.19) | copy-start | bytes 786436
  85.4 9.2 %copy-start.6 = (s32[512]{0:T(512)S(1)}, s32[512]{0:T(512)}, u32[]{:S(2)}) copy-start(s32[512]{0:T(512)} %param.17) | copy-start | bytes 6148
  90.9 13.7 %all-to-all-start.4 = ((bf16[16,128,128]{2,1,0:T(8,128)(2,1)}), bf16[16,128,128]{2,1,0:T(8,128)(2,1)S(1)}, u32[]{:S(2)}, u32[]{:S(2)}) async-start(bf16[16,128,128]{2,1,0:T(8,128)(2,1)} %get-tuple-element.26), calls=%async_computation.4 | async-start | bytes 1048576 | tf_op jit(solution)/shard_map/all_to_all | solution.py:392
  104.6 16.1 %all-to-all-start.6 = ((bf16[8,320,128]{2,1,0:T(8,128)(2,1)}), bf16[8,320,128]{2,1,0:T(8,128)(2,1)S(1)}, u32[]{:S(2)}, u32[]{:S(2)}) async-start(bf16[8,320,128]{2,1,0:T(8,128)(2,1)} %pick_1_320.1), calls=%async_computation.6 | async-start | bytes 1310720 | tf_op jit(solution)/shard_map/all_to_all | solution.py:392
  108.9 4.6 %copy-start.1 = (bf16[32,12,128,128]{3,2,1,0:T(8,128)(2,1)S(1)}, bf16[32,12,128,128]{3,2,1,0:T(8,128)(2,1)}, u32[]{:S(2)}) copy-start(bf16[32,12,128,128]{3,2,1,0:T(8,128)(2,1)} %refs_2_.11) | copy-start | bytes 37748740
  120.7 25.2 %copy-start.7 = (bf16[8,320,128]{2,1,0:T(8,128)(2,1)}, bf16[8,320,128]{2,1,0:T(8,128)(2,1)S(1)}, u32[]{:S(2)}) copy-start(bf16[8,320,128]{2,1,0:T(8,128)(2,1)S(1)} %all-to-all-done.6.first) | copy-start | bytes 1966084
  120.7 15.2 %all-to-all-start.5 = ((bf16[16,128,128]{2,1,0:T(8,128)(2,1)}), bf16[16,128,128]{2,1,0:T(8,128)(2,1)S(1)}, u32[]{:S(2)}, u32[]{:S(2)}) async-start(bf16[16,128,128]{2,1,0:T(8,128)(2,1)} %get-tuple-element.28), calls=%async_computation.5 | async-start | bytes 1048576 | tf_op jit(solution)/shard_map/all_to_all | solution.py:392
  135.8 22.0 %all-to-all-start.7 = ((bf16[8,128,128]{2,1,0:T(8,128)(2,1)}), bf16[8,128,128]{2,1,0:T(8,128)(2,1)}, u32[]{:S(2)}, u32[]{:S(2)}) async-start(bf16[8,128,128]{2,1,0:T(8,128)(2,1)} %pick_2_128.1), calls=%async_computation.7 | async-start | bytes 524288 | tf_op jit(solution)/shard_map/all_to_all | solution.py:392
  146.6 4.6 %copy-start.2 = (bf16[32,12,128,128]{3,2,1,0:T(8,128)(2,1)S(1)}, bf16[32,12,128,128]{3,2,1,0:T(8,128)(2,1)}, u32[]{:S(2)}) copy-start(bf16[32,12,128,128]{3,2,1,0:T(8,128)(2,1)} %refs_2_.11) | copy-start | bytes 37748740
  157.9 10.8 %all-to-all-start.8 = ((bf16[8,64,128]{2,1,0:T(8,128)(2,1)}), bf16[8,64,128]{2,1,0:T(8,128)(2,1)S(1)}, u32[]{:S(2)}, u32[]{:S(2)}) async-start(bf16[8,64,128]{2,1,0:T(8,128)(2,1)} %pick_1_64.1), calls=%async_computation.8 | async-start | bytes 262144 | tf_op jit(solution)/shard_map/all_to_all | solution.py:392
  168.7 0.7 copy-start.8

commit v2 on v1

v2 whole, which is shorter than its diff:
```python
import functools
import math

import jax
import jax.numpy as jnp
from jax import lax
from jax.experimental import pallas as pl
from jax.experimental.pallas import tpu as pltpu
from jax.sharding import Mesh, PartitionSpec as P

D = 512
FF = 2048
HEADS = 8
HEAD_DIM = 64
HOPS = 3
TOKS = 4
BLK = 128
K = 12
SEND = 2
NB = 32
PARTS = 16
FEATS = 64
NODES = NB * BLK
TRAIN = 512
CHIP_NODES = 128
NARROW = 8
CHIPS = 64
GROUP = 16
UNROLL = 4
FF_CHUNK = 256
EPSILON = 1e-05

BF = jnp.bfloat16
F32 = jnp.float32
WIDE = ("z", "y")
NARROW_AXES = ("x", "c")
ALL_CHIPS = ("z", "y", "x")


def params(limit_mib):
    return pltpu.CompilerParams(vmem_limit_bytes=limit_mib * 1024 * 1024)


def dot(left, right):
    return jnp.dot(left, right, preferred_element_type=F32)


def dot_rows(left, right):
    return lax.dot_general(left, right, (((1,), (1,)), ((), ())), preferred_element_type=F32)


def pack_kernel(sends, field, outgoing, sems):
    copies = []
    for slot in range(PARTS * SEND):
        start = pl.multiple_of(sends[0, slot // SEND, slot % SEND] * BLK, BLK)
        rows = (slot % SEND) * FEATS
        copies.append(
            pltpu.make_async_copy(
                field.at[:, pl.ds(start, BLK)],
                outgoing.at[slot // SEND, rows : rows + FEATS, :],
                sems.at[slot],
            )
        )
    for copy in copies:
        copy.start()
    for copy in copies:
        copy.wait()


def pack(sends, field):
    return pl.pallas_call(
        pack_kernel,
        out_shape=jax.ShapeDtypeStruct((PARTS, SEND * FEATS, BLK), BF),
        in_specs=[
            pl.BlockSpec(memory_space=pltpu.SMEM),
            pl.BlockSpec(memory_space=pltpu.HBM),
        ],
        scratch_shapes=[pltpu.SemaphoreType.DMA((PARTS * SEND,))],
        compiler_params=params(4),
        name="pack",
    )(sends, in_hbm(field))


def apply_kernel(*refs, second, first, last):
    refs = list(refs)
    lists, sends, tiles, field, incoming = refs[:5]
    refs = refs[5:]
    degree = None if first else refs.pop(0)
    counts = refs.pop(0) if first else None
    previous = refs.pop(0) if second else None
    aliased = second and refs.pop(0)
    result = refs.pop(0)
    hops = refs.pop(0) if second else None
    outgoing = None if last else refs.pop(0)
    degree_out = refs.pop(0) if first else None
    pool, fresh = refs[:2]

    for j in range(NB):
        pool[j] = field[:, j * BLK : (j + 1) * BLK]
    for j in range(PARTS * SEND):
        rows = (j % SEND) * FEATS
        pool[NB + j] = incoming[j // SEND, rows : rows + FEATS, :]

    def one_block(b, carry):
        picked = jnp.concatenate([pool[lists[b, k]] for k in range(K)], axis=1)
        if first:
            picked = jnp.concatenate([picked, jnp.ones((GROUP, K * BLK), BF)], axis=0)
        summed = dot(picked, tiles[b].reshape(K * BLK, BLK))
        if first:
            share = summed[FEATS : FEATS + 1, :]
            degree_out[pl.ds(b, 1), :] = share
            summed = summed[:FEATS, :]
        else:
            share = degree[pl.ds(b, 1), :]
        value = (summed / share).astype(BF)
        cols = pl.ds(pl.multiple_of(b * BLK, BLK), BLK)
        if second:
            value = (
                0.5 * previous[:, cols].astype(F32) + pool[b].astype(F32) + value.astype(F32)
            ).astype(BF)
        result[:, cols] = value
        fresh[b] = value
        return carry

    lax.fori_loop(0, NB, one_block, 0, unroll=UNROLL)
    if second:
        store = pltpu.make_async_copy(result, hops.at[second - 1], refs[2])
        store.start()
    if not last:
        for slot in range(PARTS * SEND):
            rows = (slot % SEND) * FEATS
            outgoing[slot // SEND, rows : rows + FEATS, :] = fresh[
                sends[0, slot // SEND, slot % SEND]
            ]
        if first:
            for p in range(PARTS):
                outgoing[p, SEND * FEATS :, :] = jnp.broadcast_to(
                    counts[...], (GROUP, BLK)
                ).astype(BF)
    if second:
        store.wait()


def apply(lists, sends, tiles, field, incoming, extra, previous=None, hops=None, hop=0):
    second = previous is not None
    last = second and hop == HOPS - 1
    first = hop == 0 and not second
    smem = pl.BlockSpec(memory_space=pltpu.SMEM)
    vmem = pl.BlockSpec(memory_space=pltpu.VMEM)
    hbm = pl.BlockSpec(memory_space=pltpu.HBM)
    operands = [lists, sends, tiles, field, incoming, extra]
    in_specs = [smem, smem, vmem, vmem, vmem, vmem]
    out_shape = [jax.ShapeDtypeStruct((FEATS, NODES), BF)]
    out_specs = [vmem]
    aliases = {}
    if second:
        operands.append(previous)
        in_specs.append(vmem)
        if hops is None:
            operands.append(sends)
            in_specs.append(smem)
        else:
            aliases = {len(operands): 1}
            operands.append(hops)
            in_specs.append(hbm)
        out_shape.append(jax.ShapeDtypeStruct((HOPS, FEATS, NODES), BF))
        out_specs.append(hbm)
    if not last:
        rows = SEND * FEATS + (GROUP if first else 0)
        out_shape.append(jax.ShapeDtypeStruct((PARTS, rows, BLK), BF))
        out_specs.append(vmem)
    if first:
        out_shape.append(jax.ShapeDtypeStruct((NB, BLK), F32))
        out_specs.append(vmem)
    scratch = [pltpu.VMEM((2 * NB, FEATS, BLK), BF), pltpu.VMEM((NB, FEATS, BLK), BF)]
    if second:
        scratch.append(pltpu.SemaphoreType.DMA)
    return pl.pallas_call(
        functools.partial(apply_kernel, second=second and hop + 1, first=first, last=last),
        out_shape=out_shape,
        in_specs=in_specs,
        out_specs=out_specs,
        scratch_shapes=scratch,
        input_output_aliases=aliases,
        compiler_params=params(20),
        name=f"apply_{'second' if second else 'first'}_{hop}",
    )(*operands)


def pick_kernel(ids, *refs, with_grads):
    refs = list(refs)
    out = refs.pop()
    grads = refs.pop() if with_grads else None
    id_row = ids[...]
    total = None
    for b in range(NB):
        rows = lax.broadcasted_iota(jnp.int32, (BLK, TRAIN), 0) + b * BLK
        chosen = jnp.where(rows == id_row, 1.0, 0.0).astype(BF)
        fields = jnp.concatenate([field[:, b * BLK : (b + 1) * BLK] for field in refs], axis=0)
        term = dot(fields, chosen)
        total = term if total is None else total + term
    picked = total.astype(BF)
    base = len(refs) * FEATS
    for n in range(NARROW):
        cols = slice((n // 2) * CHIP_NODES, (n // 2 + 1) * CHIP_NODES)
        out[n, :base, :] = picked[:, cols]
        if with_grads:
            for t in range(TOKS):
                out[n, base + t * FEATS : base + (t + 1) * FEATS, :] = grads[t, :, cols]


def pick(ids, fields, grads=None):
    rows = FEATS * len(fields) + (0 if grads is None else TOKS * FEATS)
    operands = [ids, *fields] + ([] if grads is None else [grads])
    return pl.pallas_call(
        functools.partial(pick_kernel, with_grads=grads is not None),
        out_shape=jax.ShapeDtypeStruct((NARROW, rows, CHIP_NODES), BF),
        compiler_params=params(8),
        name=f"pick_{len(fields)}_{rows}",
    )(*operands)


def layer_kernel(
    place, first, later, counted, owners, query_h, key_h, value_h, out_h, out_th, up_h, up_th, down_h,
    result, query_s, key_s, value_s, mixed_s, probs_s, act_s, pre_s, gmix_s, gq_s, gk_s, gv_s, gr_s,
    query_w, key_w, value_w, out_w, out_t, up_w, up_t, down_w, sems,
):
    loads = {}
    pairs = (
        (query_h, query_w), (key_h, key_w), (value_h, value_w), (out_h, out_w),
        (up_h, up_w), (down_h, down_w), (up_th, up_t), (out_th, out_t),
    )
    for index, (source, target) in enumerate(pairs):
        loads[index] = pltpu.make_async_copy(source, target, sems.at[index])
        loads[index].start()
    own = place[0]
    width = TOKS * CHIP_NODES
    tokens = jnp.concatenate(
        [
            first[:, 0:FEATS, :].reshape(D, CHIP_NODES),
        ]
        + [later[:, t * FEATS : (t + 1) * FEATS, :].reshape(D, CHIP_NODES) for t in range(HOPS)],
        axis=1,
    )
    totals = counted[0, SEND * FEATS : SEND * FEATS + 1, :].astype(F32)
    for p in range(1, PARTS):
        totals = totals + counted[p, SEND * FEATS : SEND * FEATS + 1, :].astype(F32)
    by_owner = jnp.transpose(jnp.broadcast_to(1.0 / totals, (BLK, BLK)))
    named = lax.broadcasted_iota(jnp.int32, (BLK, BLK), 0) == owners[pl.ds(place[1], 1), :]
    row_scale = jnp.sum(jnp.where(named, by_owner, 0.0), axis=0, keepdims=True)
    scaled = jnp.concatenate(
        [
            (
                first[:, (t + 1) * FEATS : (t + 2) * FEATS, :].reshape(D, CHIP_NODES).astype(F32)
                * row_scale
            ).astype(BF)
            for t in range(TOKS)
        ],
        axis=1,
    )

    def normalize(hidden):
        center = hidden - jnp.mean(hidden, axis=0, keepdims=True)
        inverse = lax.rsqrt(jnp.mean(center * center, axis=0, keepdims=True) + EPSILON)
        return center * inverse, inverse

    normed_a = normalize(tokens.astype(F32))[0].astype(BF)
    loads[0].wait()
    query_s[...] = dot(query_w[...], normed_a).astype(BF)
    loads[1].wait()
    key_s[...] = dot(key_w[...], normed_a).astype(BF)
    loads[2].wait()
    value_s[...] = dot(value_w[...], normed_a).astype(BF)
    score_scale = 1.0 / math.sqrt(HEAD_DIM)

    def parts(ref, rows):
        block = ref[rows, :].astype(F32)
        return [block[:, t * CHIP_NODES : (t + 1) * CHIP_NODES] for t in range(TOKS)]

    def forward_head(h, carry):
        rows = pl.ds(pl.multiple_of(h * HEAD_DIM, HEAD_DIM), HEAD_DIM)
        query, key, value = parts(query_s, rows), parts(key_s, rows), parts(value_s, rows)
        all_probs = []
        mixed = []
        for t in range(TOKS):
            scores = [
                jnp.sum(query[t] * key[u], axis=0, keepdims=True) * score_scale
                for u in range(TOKS)
            ]
            top = jnp.maximum(
                jnp.maximum(scores[0], scores[1]), jnp.maximum(scores[2], scores[3])
            )
            raised = [jnp.exp(s - top) for s in scores]
            total = raised[0] + raised[1] + raised[2] + raised[3]
            probs = [r / total for r in raised]
            all_probs += probs
            low = [p.astype(BF).astype(F32) for p in probs]
            mixed.append(
                low[0] * value[0] + low[1] * value[1] + low[2] * value[2] + low[3] * value[3]
            )
        probs_s[h] = jnp.concatenate(all_probs, axis=0)
        mixed_s[rows, :] = jnp.concatenate(mixed, axis=1).astype(BF)
        return carry

    lax.fori_loop(0, HEADS, forward_head, 0)
    loads[3].wait()
    residual = (tokens.astype(F32) + dot(out_w[...], mixed_s[...])).astype(BF)
    second_norm, second_inv = normalize(residual.astype(F32))
    normed_b = second_norm.astype(BF)

    root = math.sqrt(2.0 / math.pi)
    groups = FF_CHUNK // (2 * GROUP)

    def ffn_chunk(i, carry):
        rows = pl.ds(pl.multiple_of(i * FF_CHUNK, FF_CHUNK), FF_CHUNK)
        pre = dot(up_w[rows, :], normed_b)
        grad_act = dot(down_w[rows, :], scaled)
        square = pre * pre
        gate = 0.5 + 0.5 * jnp.tanh(pre * (root + (root * 0.044715) * square))
        activated = pre * gate
        slope = gate + activated * (1.0 - gate) * (
            2.0 * root + (6.0 * root * 0.044715) * square
        )
        at = pl.ds(i * groups, groups)
        act_s[at] = activated.astype(BF).reshape(groups, 2, GROUP, width)
        pre_s[at] = (grad_act * slope).astype(BF).reshape(groups, 2, GROUP, width)
        return carry

    loads[4].wait()
    loads[5].wait()
    lax.fori_loop(0, FF // FF_CHUNK, ffn_chunk, 0)

    half = FF // 2
    grad_down = dot_rows(act_s[:, own].reshape(half, width), scaled)
    result[:, 2 * GROUP : 3 * GROUP, :] = grad_down.astype(BF).reshape(CHIPS, GROUP, D)
    grad_up = dot_rows(pre_s[:, own].reshape(half, width), normed_b)
    result[:, GROUP : 2 * GROUP, :] = grad_up.astype(BF).reshape(CHIPS, GROUP, D)

    loads[6].wait()
    grad_normed = dot(up_t[...], pre_s[...].reshape(FF, width))
    grad_resid = (
        scaled.astype(F32)
        + second_inv
        * (
            grad_normed
            - jnp.mean(grad_normed, axis=0, keepdims=True)
            - second_norm * jnp.mean(grad_normed * second_norm, axis=0, keepdims=True)
        )
    ).astype(BF)
    gr_s[...] = grad_resid.reshape(GROUP, 2, GROUP, width)
    loads[7].wait()
    gmix_s[...] = dot(out_t[...], grad_resid).astype(BF)

    def backward_head(h, carry):
        rows = pl.ds(pl.multiple_of(h * HEAD_DIM, HEAD_DIM), HEAD_DIM)
        query, key, value = parts(query_s, rows), parts(key_s, rows), parts(value_s, rows)
        grad_mixed = parts(gmix_s, rows)
        saved = probs_s[h]
        prob = lambda t, u: saved[t * TOKS + u : t * TOKS + u + 1, :]
        weights = []
        grad_query = []
        for t in range(TOKS):
            grad_probs = [
                jnp.sum(grad_mixed[t] * value[u], axis=0, keepdims=True) for u in range(TOKS)
            ]
            inner = sum(prob(t, u) * grad_probs[u] for u in range(TOKS))
            weight = [
                (prob(t, u) * (grad_probs[u] - inner) * score_scale).astype(BF).astype(F32)
                for u in range(TOKS)
            ]
            weights.append(weight)
            grad_query.append(sum(weight[u] * key[u] for u in range(TOKS)))
        grad_key = [sum(weights[t][u] * query[t] for t in range(TOKS)) for u in range(TOKS)]
        grad_value = [
            sum(prob(t, u).astype(BF).astype(F32) * grad_mixed[t] for t in range(TOKS))
            for u in range(TOKS)
        ]
        at = pl.ds(h * 2, 2)
        for ref, pieces in ((gq_s, grad_query), (gk_s, grad_key), (gv_s, grad_value)):
            ref[at] = jnp.concatenate(pieces, axis=1).astype(BF).reshape(2, 2, GROUP, width)
        return carry

    lax.fori_loop(0, HEADS, backward_head, 0)
    quarter = D // 2
    stacked = jnp.concatenate(
        [ref[:, own].reshape(quarter, width) for ref in (gq_s, gk_s, gv_s)], axis=0
    )
    count = GROUP * 3
    result[:count, 0:GROUP, :] = dot_rows(stacked, normed_a).astype(BF).reshape(count, GROUP, D)
    sum_out = dot_rows(gr_s[:, own].reshape(quarter, width), mixed_s[...])
    result[count:, 0:GROUP, :] = sum_out.astype(BF).reshape(GROUP, GROUP, D)


def layer(place, first, later, counted, owners, *weights):
    width = TOKS * CHIP_NODES
    square = pltpu.VMEM((D, width), BF)
    grouped = pltpu.VMEM((GROUP, 2, GROUP, width), BF)
    wide = pltpu.VMEM((CHIPS, 2, GROUP, width), BF)
    vmem = pl.BlockSpec(memory_space=pltpu.VMEM)
    hbm = pl.BlockSpec(memory_space=pltpu.HBM)
    return pl.pallas_call(
        layer_kernel,
        out_shape=jax.ShapeDtypeStruct((CHIPS, 3 * GROUP, D), BF),
        in_specs=[pl.BlockSpec(memory_space=pltpu.SMEM)] + [vmem] * 4 + [hbm] * 8,
        out_specs=vmem,
        scratch_shapes=[
            square, square, square, square,
            pltpu.VMEM((HEADS, TOKS * TOKS, CHIP_NODES), F32),
            wide, wide, square, grouped, grouped, grouped, grouped,
            *[pltpu.VMEM(w.shape, BF) for w in weights],
            pltpu.SemaphoreType.DMA((len(weights),)),
        ],
        compiler_params=params(36),
        name="layer",
    )(place, first, later, counted, owners, *[in_hbm(w) for w in weights])


def in_hbm(array):
    return pltpu.with_memory_space_constraint(array, pltpu.HBM)


def exchange(array, axes):
    return lax.all_to_all(array, axes, split_axis=0, concat_axis=0, tiled=True)


def on_device(
    features, edge_tiles, block_lists, send_lists, train_ids, owners, cotangent,
    query_weight, key_weight, value_weight, out_weight, up_weight, down_weight,
):
    ids = train_ids.reshape(1, TRAIN)
    named = (owners == jnp.arange(CHIPS * 2, dtype=jnp.int32)[None]).astype(F32)
    counts = jnp.sum(named, axis=0, keepdims=True)
    incoming = exchange(pack(send_lists, features), WIDE)
    first_rows = exchange(pick(ids, [features], cotangent), NARROW_AXES)
    incoming, first_rows, counts, up_t, out_t = lax.optimization_barrier(
        (incoming, first_rows, counts, up_weight.T, out_weight.T)
    )
    step = functools.partial(apply, block_lists, send_lists, edge_tiles)
    current = features
    hops = None
    fields = []
    for hop in range(HOPS):
        if hop == 0:
            once, outgoing, degree = step(current, incoming, counts)
        else:
            once, outgoing = step(current, incoming, degree, hop=hop)
        incoming = exchange(outgoing, WIDE)
        if hop == 0:
            counted = incoming
        results = step(once, incoming, degree, previous=current, hops=hops, hop=hop)
        current, hops = results[0], results[1]
        fields.append(current)
        if hop < HOPS - 1:
            incoming = exchange(results[2], WIDE)
    later_rows = exchange(pick(ids, fields), NARROW_AXES)

    place = jnp.stack([lax.axis_index("c"), lax.axis_index("x")]).astype(jnp.int32)
    partial = layer(
        place, first_rows, later_rows, counted, owners.reshape(TOKS, CHIP_NODES),
        query_weight, key_weight, value_weight, out_weight, out_t, up_weight, up_t, down_weight,
    )
    gathered = exchange(partial, ALL_CHIPS)
    sums = jnp.sum(gathered.astype(F32), axis=0)
    return (hops, sums[:GROUP], sums[GROUP : 2 * GROUP], sums[2 * GROUP :])


def solution(mesh):
    split = Mesh(mesh.devices.reshape(4, 4, 4, 2), ("z", "y", "x", "c"))
    rows = P(WIDE + NARROW_AXES, None)
    in_specs = (
        P(NARROW_AXES, WIDE),
        P(WIDE, None, None, None),
        P(WIDE, None),
        P(WIDE, None, None),
        P(WIDE),
        P(WIDE, None),
        P(None, NARROW_AXES, WIDE),
        P(), P(), P(), P(), P(), P(),
    )
    out_specs = (P(None, NARROW_AXES, WIDE), rows, rows, rows)
    return jax.shard_map(
        on_device, mesh=split, in_specs=in_specs, out_specs=out_specs, check_vma=False
    )
```

time: 236 us -> 219 us (0.928)
  blocking collectives: 89 us -> 113 us
  local copies, waits for them, and re-layouts: 24.4 us -> 11.2 us
  starting transfers between devices: 28.3 us -> 16 us
  other arithmetic: 9.38 us -> 0.73 us
  Pallas kernels: 55.4 us -> 51.4 us
  waiting for transfers between devices: 27.9 us -> 25 us
    all_to_all x4 -> x6, blocking collectives: 89 us -> 113 us  [exchange(): return lax.all_to_all(array, axes, split_axis=0, concat_axis=0, tiled=True)]
    unnamed x22 -> x24, local copies, waits for them, and re-layouts: 23 us -> 10.5 us
    all_to_all x6 -> x3, starting transfers between devices: 28.3 us -> 16 us  [exchange(): return lax.all_to_all(array, axes, split_axis=0, concat_axis=0, tiled=True)]
    reduce_sum x3 -> x0, other arithmetic: 8.07 us -> none  [the longest x1 7.42 us: on_device(): degree = jnp.sum(edge_tiles, axis=(1, 2), dtype=F32)]
    pallas_call x1, Pallas kernels: 18.4 us -> 14.6 us  [layer(): pl.pallas_call(layer_kernel, out_shape=jax.ShapeDtypeStruct((CHIPS, 3 * G...]
    all_to_all x6 -> x3, waiting for transfers between devices: 27.9 us -> 25 us  [exchange(): return lax.all_to_all(array, axes, split_axis=0, concat_axis=0, tiled=True)]
    pallas_call x3 -> x2, Pallas kernels: 5.02 us -> 4.09 us  [pick(): pl.pallas_call(functools.partial(pick_kernel, with_grads=grads is not Non...]
  transfers between devices with their start and end apart: 6 -> 3, of which waited for: 5 -> 3; matrix products, arithmetic and copies ran while one was open for 7% -> 2% of each run, Pallas kernels for 7% -> 1%
where the time goes in v2:
time: 219 us; the launch traced here: 218 us
  blocking collectives  113 us (52%)
  Pallas kernels  51.4 us (23%)
  waiting for transfers between devices  25 us (11%)
  starting transfers between devices  16 us (7%)
  local copies, waits for them, and re-layouts  11.2 us (5%)
    all_to_all x6, blocking collectives, exchange(): return lax.all_to_all(array, axes, split_axis=0, concat_axis=0, tiled=True)  113 us
    pallas_call x6, Pallas kernels, apply(): pl.pallas_call(functools.partial(apply_kernel, second=second and hop + 1,...  29.8 us
    all_to_all x3, waiting for transfers between devices, exchange(): return lax.all_to_all(array, axes, split_axis=0, concat_axis=0, tiled=True)  25 us
    all_to_all x3, starting transfers between devices, exchange(): return lax.all_to_all(array, axes, split_axis=0, concat_axis=0, tiled=True)  16 us
    pallas_call x1, Pallas kernels, layer(): pl.pallas_call(layer_kernel, out_shape=jax.ShapeDtypeStruct((CHIPS, 3 * G...  14.6 us
    unnamed x24, local copies, waits for them, and re-layouts  10.5 us
  transfers between devices with their start and end apart: 3, of which 3 were waited for; matrix products, arithmetic and copies ran while one was open for 2% of the time, Pallas kernels for 1%

profile of v2, /device:TPU:0, one launch (start us, length us, event | category | flops | bytes accessed | tf_op | source)
XLA Modules:
  0.0 218.4 jit_solution(15504087277672902721)
XLA Ops:
  0.6 0.0 copy-start.1
  0.6 0.0 copy-start.3
  0.7 0.0 copy-start.2
  0.7 0.8 copy.50.sends.refs_1_.refs_7_
  1.5 2.9 %pack.1 = bf16[16,128,128]{2,1,0:T(8,128)(2,1)} custom-call(s32[1,16,2]{2,1,0:T(8,128)S(1)} %copy.50.sends.refs_1_.refs_7_, bf16[64,4096]{1,0:T(8,128)(2,1)} %refs_6_.1), custom_call_target="tpu_custom_call" | custom-call | tf_op jit(solution)/shard_map/pack/pallas_call | solution.py:71
  4.4 8.1 %all-to-all-start = ((bf16[16,128,128]{2,1,0:T(8,128)(2,1)}), bf16[16,128,128]{2,1,0:T(8,128)(2,1)S(1)}, u32[]{:S(2)}, u32[]{:S(2)}) async-start(bf16[16,128,128]{2,1,0:T(8,128)(2,1)} %pack.1), calls=%async_computation | async-start | bytes 1048576 | tf_op jit(solution)/shard_map/all_to_all | solution.py:423
  12.4 0.0 copy-done.1
  12.4 0.0 copy-done.3
  12.5 0.0 copy-done.2
  12.5 1.5 pick_1_320.1
  14.0 10.0 %all-to-all-done.refs_4_ = bf16[16,128,128]{2,1,0:T(8,128)(2,1)S(1)} async-done(((bf16[16,128,128]{2,1,0:T(8,128)(2,1)}), bf16[16,128,128]{2,1,0:T(8,128)(2,1)S(1)}, u32[]{:S(2)}, u32[]{:S(2)}) %all-to-all-start) | async-done | bytes 524320 | tf_op jit(solution)/shard_map/all_to_all | solution.py:423
  24.0 4.3 %all-to-all-start.1 = ((bf16[8,320,128]{2,1,0:T(8,128)(2,1)}), bf16[8,320,128]{2,1,0:T(8,128)(2,1)S(1)}, u32[]{:S(2)}, u32[]{:S(2)}) async-start(bf16[8,320,128]{2,1,0:T(8,128)(2,1)} %pick_1_320.1), calls=%async_computation.1 | async-start | bytes 1310720 | tf_op jit(solution)/shard_map/all_to_all | solution.py:423
  28.3 0.0 copy-start.5
  28.3 0.0 copy-start.6
  28.3 0.0 copy-start.4
  28.3 4.0 %copy.36 = bf16[2048,512]{0,1:T(8,128)(2,1)} copy(bf16[2048,512]{1,0:T(8,128)(2,1)} %up_h.1) | data formatting | bytes 4194304 | tf_op args[11]
  32.3 0.0 copy-done.5
  32.3 1.0 copy.37
  33.3 0.0 copy-done.6
  33.3 0.1 copy.49.refs_0_
  33.4 0.0 copy-done.4
  33.4 0.1 convert_reduce_fusion.1
  33.6 6.5 %all-to-all-done.1.first = bf16[8,320,128]{2,1,0:T(8,128)(2,1)S(1)} async-done(((bf16[8,320,128]{2,1,0:T(8,128)(2,1)}), bf16[8,320,128]{2,1,0:T(8,128)(2,1)S(1)}, u32[]{:S(2)}, u32[]{:S(2)}) %all-to-all-start.1) | async-done | bytes 655392 | tf_op jit(solution)/shard_map/all_to_all | solution.py:423
  40.0 0.0 copy-start
  40.0 4.6 %copy-done = bf16[32,12,128,128]{3,2,1,0:T(8,128)(2,1)S(1)} copy-done((bf16[32,12,128,128]{3,2,1,0:T(8,128)(2,1)S(1)}, bf16[32,12,128,128]{3,2,1,0:T(8,128)(2,1)}, u32[]{:S(2)}) %copy-start) | copy-done | bytes 12582936
  44.6 0.0 slice-start
  44.6 0.0 slice-start.1
  44.6 4.8 %apply_first_0.1 = (bf16[64,4096]{1,0:T(8,128)(2,1)S(1)}, bf16[16,144,128]{2,1,0:T(8,128)(2,1)S(1)}, f32[32,128]{1,0:T(8,128)S(1)}) custom-call(s32[32,12]{1,0:T(8,128)S(1)} %copy.49.refs_0_, s32[1,16,2]{2,1,0:T(8,128)S(1)} %copy.50.sends.refs_1_.refs_7_, bf16[32,12,128,128]{3,2,1,0:T(8,128)(2,1)S(1)} %copy-done, bf16[64,4096]{1,0:T(8,128)(2,1)S(1)} %copy-done.1, ...), custom_call_target="tpu_custom_call" | custom-call | tf_op jit(solution)/shard_map/apply_first_0/pallas_call | solution.py:178
  49.4 15.0 %all_to_all.45.refs_4_.counted = bf16[16,144,128]{2,1,0:T(8,128)(2,1)S(1)} all-to-all(bf16[16,144,128]{2,1,0:T(8,128)(2,1)S(1)} %get-tuple-element.27), channel_id=1, replica_groups=mesh['z'=4,'y'=4,'x'=4,'c'=2] {'z','y'}, dimensions={0} | all-to-all | bytes 1179648 | tf_op jit(solution)/shard_map/all_to_all | solution.py:423
  64.4 0.0 slice-start.2
  64.4 5.4 %apply_second_0.1 = (bf16[64,4096]{1,0:T(8,128)(2,1)S(1)}, bf16[3,64,4096]{2,1,0:T(8,128)(2,1)}, bf16[16,128,128]{2,1,0:T(8,128)(2,1)S(1)}) custom-call(s32[32,12]{1,0:T(8,128)S(1)} %copy.49.refs_0_, s32[1,16,2]{2,1,0:T(8,128)S(1)} %copy.50.sends.refs_1_.refs_7_, bf16[32,12,128,128]{3,2,1,0:T(8,128)(2,1)S(1)} %copy-done, ...), custom_call_target="tpu_custom_call" | custom-call | tf_op jit(solution)/shard_map/apply_second_0/pallas_call | solution.py:178
  69.9 13.2 %all_to_all.46.refs_4_ = bf16[16,128,128]{2,1,0:T(8,128)(2,1)S(1)} all-to-all(bf16[16,128,128]{2,1,0:T(8,128)(2,1)S(1)} %get-tuple-element.30), channel_id=1, replica_groups=mesh['z'=4,'y'=4,'x'=4,'c'=2] {'z','y'}, dimensions={0} | all-to-all | bytes 1048576 | tf_op jit(solution)/shard_map/all_to_all | solution.py:423
  83.1 0.0 slice-done
  83.1 0.0 slice-done.1
  83.1 0.0 slice-done.2
  83.1 4.5 %apply_first_1.1 = (bf16[64,4096]{1,0:T(8,128)(2,1)S(1)}, bf16[16,128,128]{2,1,0:T(8,128)(2,1)S(1)}) custom-call(s32[32,12]{1,0:T(8,128)S(1)} %copy.49.refs_0_, s32[1,16,2]{2,1,0:T(8,128)S(1)} %copy.50.sends.refs_1_.refs_7_, bf16[32,12,128,128]{3,2,1,0:T(8,128)(2,1)S(1)} %bitcast.9, bf16[64,4096]{1,0:T(8,128)(2,1)S(1)} %get-tuple-element.29.refs_3_.refs_6_.refs_0_, ...), custom_call_target="tpu_custom_call" | custom-call | tf_op jit(solution)/shard_map/apply_first_1/pallas_call | solution.py:178
  87.6 13.1 %all_to_all.47.refs_4_ = bf16[16,128,128]{2,1,0:T(8,128)(2,1)S(1)} all-to-all(bf16[16,128,128]{2,1,0:T(8,128)(2,1)S(1)} %get-tuple-element.32), channel_id=1, replica_groups=mesh['z'=4,'y'=4,'x'=4,'c'=2] {'z','y'}, dimensions={0} | all-to-all | bytes 1048576 | tf_op jit(solution)/shard_map/all_to_all | solution.py:423
  100.8 5.3 %apply_second_1.1 = (bf16[64,4096]{1,0:T(8,128)(2,1)S(1)}, bf16[3,64,4096]{2,1,0:T(8,128)(2,1)}, bf16[16,128,128]{2,1,0:T(8,128)(2,1)S(1)}) custom-call(s32[32,12]{1,0:T(8,128)S(1)} %copy.49.refs_0_, s32[1,16,2]{2,1,0:T(8,128)S(1)} %copy.50.sends.refs_1_.refs_7_, bf16[32,12,128,128]{3,2,1,0:T(8,128)(2,1)S(1)} %bitcast.9, ...), custom_call_target="tpu_custom_call", output_to_operand_aliasing={{1}: (7, {})} | custom-call | tf_op jit(solution)/shard_map/apply_second_1/pallas_call | solution.py:178
  106.1 13.1 %all_to_all.48.refs_4_ = bf16[16,128,128]{2,1,0:T(8,128)(2,1)S(1)} all-to-all(bf16[16,128,128]{2,1,0:T(8,128)(2,1)S(1)} %get-tuple-element.35), channel_id=1, replica_groups=mesh['z'=4,'y'=4,'x'=4,'c'=2] {'z','y'}, dimensions={0} | all-to-all | bytes 1048576 | tf_op jit(solution)/shard_map/all_to_all | solution.py:423
  119.2 4.5 %apply_first_2.1 = (bf16[64,4096]{1,0:T(8,128)(2,1)S(1)}, bf16[16,128,128]{2,1,0:T(8,128)(2,1)S(1)}) custom-call(s32[32,12]{1,0:T(8,128)S(1)} %copy.49.refs_0_, s32[1,16,2]{2,1,0:T(8,128)S(1)} %copy.50.sends.refs_1_.refs_7_, bf16[32,12,128,128]{3,2,1,0:T(8,128)(2,1)S(1)} %bitcast.9, bf16[64,4096]{1,0:T(8,128)(2,1)S(1)} %get-tuple-element.34.refs_3_.refs_6_.refs_1_, ...), custom_call_target="tpu_custom_call" | custom-call | tf_op jit(solution)/shard_map/apply_first_2/pallas_call | solution.py:178
  123.7 13.1 %all_to_all.49.refs_4_ = bf16[16,128,128]{2,1,0:T(8,128)(2,1)S(1)} all-to-all(bf16[16,128,128]{2,1,0:T(8,128)(2,1)S(1)} %get-tuple-element.37), channel_id=1, replica_groups=mesh['z'=4,'y'=4,'x'=4,'c'=2] {'z','y'}, dimensions={0} | all-to-all | bytes 1048576 | tf_op jit(solution)/shard_map/all_to_all | solution.py:423
  136.8 5.3 %apply_second_2.1 = (bf16[64,4096]{1,0:T(8,128)(2,1)S(1)}, bf16[3,64,4096]{2,1,0:T(8,128)(2,1)}) custom-call(s32[32,12]{1,0:T(8,128)S(1)} %copy.49.refs_0_, s32[1,16,2]{2,1,0:T(8,128)S(1)} %copy.50.sends.refs_1_.refs_7_, bf16[32,12,128,128]{3,2,1,0:T(8,128)(2,1)S(1)} %bitcast.9, ...), custom_call_target="tpu_custom_call", output_to_operand_aliasing={{1}: (7, {})} | custom-call | tf_op jit(solution)/shard_map/apply_second_2/pallas_call | solution.py:178
  142.1 2.6 %pick_3_192.1 = bf16[8,192,128]{2,1,0:T(8,128)(2,1)} custom-call(s32[1,512]{1,0:T(1,128)S(1)} %bitcast.11, bf16[64,4096]{1,0:T(8,128)(2,1)S(1)} %get-tuple-element.29.refs_3_.refs_6_.refs_0_, bf16[64,4096]{1,0:T(8,128)(2,1)S(1)} %get-tuple-element.34.refs_3_.refs_6_.refs_1_, bf16[64,4096]{1,0:T(8,128)(2,1)S(1)} %get-tuple-element.41.refs_2_), custom_call_target="tpu_custom_call" | custom-call | tf_op jit(solution)/shard_map/pick_3_192/pallas_call | solution.py:215
  144.6 3.6 %all-to-all-start.7 = ((bf16[8,192,128]{2,1,0:T(8,128)(2,1)}), bf16[8,192,128]{2,1,0:T(8,128)(2,1)S(1)}, u32[]{:S(2)}, u32[]{:S(2)}) async-start(bf16[8,192,128]{2,1,0:T(8,128)(2,1)} %pick_3_192.1), calls=%async_computation.7 | async-start | bytes 786432 | tf_op jit(solution)/shard_map/all_to_all | solution.py:423
  148.3 0.1 pad_add_fusion.place
  148.4 8.6 %all-to-all-done.7.later = bf16[8,192,128]{2,1,0:T(8,128)(2,1)S(1)} async-done(((bf16[8,192,128]{2,1,0:T(8,128)(2,1)}), bf16[8,192,128]{2,1,0:T(8,128)(2,1)S(1)}, u32[]{:S(2)}, u32[]{:S(2)}) %all-to-all-start.7) | async-done | bytes 393248 | tf_op jit(solution)/shard_map/all_to_all | solution.py:423
  157.0 14.6 %layer.1 = bf16[64,48,512]{2,1,0:T(8,128)(2,1)S(1)} custom-call(s32[2]{0:T(128)S(1)} %pad_add_fusion.place, bf16[8,320,128]{2,1,0:T(8,128)(2,1)S(1)} %all-to-all-done.1.first, bf16[8,192,128]{2,1,0:T(8,128)(2,1)S(1)} %all-to-all-done.7.later, bf16[16,144,128]{2,1,0:T(8,128)(2,1)S(1)} %all_to_all.45.refs_4_.counted, s32[4,128]{1,0:T(4,128)S(1)} %bitcast.13, ...), custom_call_target="tpu_custom_call" | custom-call | tf_op jit(solution)/shard_map/layer/pallas_call | solution.py:401
  171.6 45.6 %all_to_all.50 = bf16[64,48,512]{2,1,0:T(8,128)(2,1)S(1)} all-to-all(bf16[64,48,512]{2,1,0:T(8,128)(2,1)S(1)} %layer.1), channel_id=1, replica_groups=mesh['z'=4,'y'=4,'x'=4,'c'=2] {'z','y','x'}, dimensions={0} | all-to-all | bytes 6291456 | tf_op jit(solution)/shard_map/all_to_all | solution.py:423
  217.2 0.5 convert_reduce_fusion
  217.7 0.6 fusion
  (1 shorter events, 0.0 us)
Async XLA Ops:
  0.6 11.8 %copy-start.1 = (bf16[64,4096]{1,0:T(8,128)(2,1)S(1)}, bf16[64,4096]{1,0:T(8,128)(2,1)}, u32[]{:S(2)}) copy-start(bf16[64,4096]{1,0:T(8,128)(2,1)} %refs_6_.1) | copy-start | bytes 1572868
  0.6 11.8 %copy-start.3 = (s32[512]{0:T(512)S(1)}, s32[512]{0:T(512)}, u32[]{:S(2)}) copy-start(s32[512]{0:T(512)} %param.17) | copy-start | bytes 6148
  0.7 11.8 %copy-start.2 = (bf16[4,64,512]{2,1,0:T(8,128)(2,1)S(1)}, bf16[4,64,512]{2,1,0:T(8,128)(2,1)}, u32[]{:S(2)}) copy-start(bf16[4,64,512]{2,1,0:T(8,128)(2,1)} %refs_1_.7) | copy-start | bytes 786436
  4.4 19.6 %all-to-all-start = ((bf16[16,128,128]{2,1,0:T(8,128)(2,1)}), bf16[16,128,128]{2,1,0:T(8,128)(2,1)S(1)}, u32[]{:S(2)}, u32[]{:S(2)}) async-start(bf16[16,128,128]{2,1,0:T(8,128)(2,1)} %pack.1), calls=%async_computation | async-start | bytes 1048576 | tf_op jit(solution)/shard_map/all_to_all | solution.py:423
  24.0 16.1 %all-to-all-start.1 = ((bf16[8,320,128]{2,1,0:T(8,128)(2,1)}), bf16[8,320,128]{2,1,0:T(8,128)(2,1)S(1)}, u32[]{:S(2)}, u32[]{:S(2)}) async-start(bf16[8,320,128]{2,1,0:T(8,128)(2,1)} %pick_1_320.1), calls=%async_computation.1 | async-start | bytes 1310720 | tf_op jit(solution)/shard_map/all_to_all | solution.py:423
  28.3 4.0 %copy-start.5 = (bf16[512,512]{1,0:T(8,128)(2,1)S(1)}, bf16[512,512]{1,0:T(8,128)(2,1)}, u32[]{:S(2)}) copy-start(bf16[512,512]{1,0:T(8,128)(2,1)} %out_h.1) | copy-start | bytes 1572868
  28.3 5.0 %copy-start.6 = (s32[32,12]{0,1:T(8,128)S(1)}, s32[32,12]{0,1:T(8,128)}, u32[]{:S(2)}) copy-start(s32[32,12]{0,1:T(8,128)} %param.15) | copy-start | bytes 4612
  28.3 5.1 %copy-start.4 = (s32[512,1]{0,1:T(1,128)S(1)}, s32[512,1]{0,1:T(1,128)}, u32[]{:S(2)}) copy-start(s32[512,1]{0,1:T(1,128)} %param.18) | copy-start | bytes 6148
  40.0 4.6 %copy-start = (bf16[32,12,128,128]{3,2,1,0:T(8,128)(2,1)S(1)}, bf16[32,12,128,128]{3,2,1,0:T(8,128)(2,1)}, u32[]{:S(2)}) copy-start(bf16[32,12,128,128]{3,2,1,0:T(8,128)(2,1)} %refs_2_.11) | copy-start | bytes 37748740
  44.6 38.5 %slice-start = ((s8[12582912]{0:T(1024)(128)(4,1)}), s8[4194304]{0:T(1024)(128)(4,1)S(1)}, s32[]{:S(2)}) async-start(s8[12582912]{0:T(1024)(128)(4,1)} %bitcast.8), calls=%async_computation.9 | async-start | bytes 8388608
  44.6 38.5 %slice-start.1 = ((s8[12582912]{0:T(1024)(128)(4,1)}), s8[4194304]{0:T(1024)(128)(4,1)S(1)}, s32[]{:S(2)}) async-start(s8[12582912]{0:T(1024)(128)(4,1)} %bitcast.8), calls=%async_computation.10 | async-start | bytes 8388608
  64.4 18.7 %slice-start.2 = ((s8[12582912]{0:T(1024)(128)(4,1)}), s8[4194304]{0:T(1024)(128)(4,1)S(1)}, s32[]{:S(2)}) async-start(s8[12582912]{0:T(1024)(128)(4,1)} %bitcast.8), calls=%async_computation.11 | async-start | bytes 8388608
  144.6 12.3 %all-to-all-start.7 = ((bf16[8,192,128]{2,1,0:T(8,128)(2,1)}), bf16[8,192,128]{2,1,0:T(8,128)(2,1)S(1)}, u32[]{:S(2)}, u32[]{:S(2)}) async-start(bf16[8,192,128]{2,1,0:T(8,128)(2,1)} %pick_3_192.1), calls=%async_computation.7 | async-start | bytes 786432 | tf_op jit(solution)/shard_map/all_to_all | solution.py:423

commit v3 on v2

v3 whole, which is shorter than its diff:
```python
import functools
import math

import jax
import jax.numpy as jnp
from jax import lax
from jax.experimental import pallas as pl
from jax.experimental.pallas import tpu as pltpu
from jax.sharding import Mesh, PartitionSpec as P

D = 512
FF = 2048
HEADS = 8
HEAD_DIM = 64
HOPS = 3
TOKS = 4
BLK = 128
K = 12
SEND = 2
NB = 32
PARTS = 16
FEATS = 64
NODES = NB * BLK
TRAIN = 512
OWNERS = 128
QUAD = 4
QUAD_NODES = 256
NARROW = 8
DESTS = 32
GROUP = 16
UNROLL = 4
FF_CHUNK = 256
EPSILON = 1e-05

BF = jnp.bfloat16
F32 = jnp.float32
WIDE = ("z", "y")
NARROW_AXES = ("xh", "xl", "c")
QUADS = ("z", "y", "xh")
CHUNK = 4


def params(limit_mib):
    return pltpu.CompilerParams(vmem_limit_bytes=limit_mib * 1024 * 1024)


def dot(left, right):
    return jnp.dot(left, right, preferred_element_type=F32)


def dot_rows(left, right):
    return lax.dot_general(left, right, (((1,), (1,)), ((), ())), preferred_element_type=F32)


def pack_kernel(sends, field, outgoing, sems):
    copies = []
    for slot in range(PARTS * SEND):
        start = pl.multiple_of(sends[0, slot // SEND, slot % SEND] * BLK, BLK)
        rows = (slot % SEND) * FEATS
        copies.append(
            pltpu.make_async_copy(
                field.at[:, pl.ds(start, BLK)],
                outgoing.at[slot // SEND, rows : rows + FEATS, :],
                sems.at[slot],
            )
        )
    for copy in copies:
        copy.start()
    for copy in copies:
        copy.wait()


def pack(sends, field):
    return pl.pallas_call(
        pack_kernel,
        out_shape=jax.ShapeDtypeStruct((PARTS, SEND * FEATS, BLK), BF),
        in_specs=[
            pl.BlockSpec(memory_space=pltpu.SMEM),
            pl.BlockSpec(memory_space=pltpu.HBM),
        ],
        scratch_shapes=[pltpu.SemaphoreType.DMA((PARTS * SEND,))],
        compiler_params=params(4),
        name="pack",
    )(sends, in_hbm(field))


def picked_columns(ids, fields):
    id_row = ids[...]
    total = None
    for b in range(NB):
        rows = lax.broadcasted_iota(jnp.int32, (BLK, TRAIN), 0) + b * BLK
        chosen = jnp.where(rows == id_row, 1.0, 0.0).astype(BF)
        block = jnp.concatenate([field[:, b * BLK : (b + 1) * BLK] for field in fields], axis=0)
        term = dot(block, chosen)
        total = term if total is None else total + term
    return total.astype(BF)


def apply_kernel(*refs, second, first, last, picking):
    refs = list(refs)
    lists, sends, tiles_h, field, incoming = refs[:5]
    refs = refs[5:]
    degree = None if first else refs.pop(0)
    previous = refs.pop(0) if second else None
    aliased = second and refs.pop(0)
    ids = refs.pop(0) if picking else None
    others = [refs.pop(0) for _ in range(picking - 1)] if picking else []
    result = refs.pop(0)
    hops = refs.pop(0) if second else None
    outgoing = None if last else refs.pop(0)
    rows_out = refs.pop(0) if picking else None
    degree_out = refs.pop(0) if first else None
    pool, fresh, tiles, sems = refs
    loads = [
        pltpu.make_async_copy(
            tiles_h.at[pl.ds(i * CHUNK, CHUNK)], tiles.at[pl.ds(i * CHUNK, CHUNK)], sems.at[i]
        )
        for i in range(NB // CHUNK)
    ]
    for load in loads:
        load.start()

    for j in range(NB):
        pool[j] = field[:, j * BLK : (j + 1) * BLK]
    for j in range(PARTS * SEND):
        rows = (j % SEND) * FEATS
        pool[NB + j] = incoming[j // SEND, rows : rows + FEATS, :]

    def one_block(b, carry):
        picked = jnp.concatenate([pool[lists[b, k]] for k in range(K)], axis=1)
        if first:
            picked = jnp.concatenate([picked, jnp.ones((GROUP, K * BLK), BF)], axis=0)
        summed = dot(picked, tiles[b].reshape(K * BLK, BLK))
        if first:
            share = summed[FEATS : FEATS + 1, :]
            degree_out[pl.ds(b, 1), :] = share
            summed = summed[:FEATS, :]
        else:
            share = degree[pl.ds(b, 1), :]
        value = (summed / share).astype(BF)
        cols = pl.ds(pl.multiple_of(b * BLK, BLK), BLK)
        if second:
            value = (
                0.5 * previous[:, cols].astype(F32) + pool[b].astype(F32) + value.astype(F32)
            ).astype(BF)
        result[:, cols] = value
        fresh[b] = value
        return carry

    for i, load in enumerate(loads):
        load.wait()
        lax.fori_loop(i * CHUNK, (i + 1) * CHUNK, one_block, 0, unroll=UNROLL)
    if second:
        store = pltpu.make_async_copy(result, hops.at[second - 1], sems.at[NB // CHUNK])
        store.start()
    if not last:
        for slot in range(PARTS * SEND):
            rows = (slot % SEND) * FEATS
            outgoing[slot // SEND, rows : rows + FEATS, :] = fresh[
                sends[0, slot // SEND, slot % SEND]
            ]
    if picking:
        picked = picked_columns(ids, [*others, result])
        if last:
            for n in range(NARROW):
                half = n // QUAD
                rows_out[n] = picked[:, half * QUAD_NODES : (half + 1) * QUAD_NODES]
        else:
            rows_out[...] = picked
    if second:
        store.wait()


def apply(lists, sends, tiles, field, incoming, degree=None, previous=None, hops=None, hop=0, ids=None, others=()):
    second = previous is not None
    last = second and hop == HOPS - 1
    first = hop == 0 and not second
    smem = pl.BlockSpec(memory_space=pltpu.SMEM)
    vmem = pl.BlockSpec(memory_space=pltpu.VMEM)
    hbm = pl.BlockSpec(memory_space=pltpu.HBM)
    operands = [lists, sends, in_hbm(tiles), field, incoming]
    in_specs = [smem, smem, hbm, vmem, vmem]
    if not first:
        operands.append(degree)
        in_specs.append(vmem)
    out_shape = [jax.ShapeDtypeStruct((FEATS, NODES), BF)]
    out_specs = [vmem]
    aliases = {}
    if second:
        operands.append(previous)
        in_specs.append(vmem)
        if hops is None:
            operands.append(sends)
            in_specs.append(smem)
        else:
            aliases = {len(operands): 1}
            operands.append(hops)
            in_specs.append(hbm)
        out_shape.append(jax.ShapeDtypeStruct((HOPS, FEATS, NODES), BF))
        out_specs.append(hbm)
    if ids is not None:
        operands += [ids, *others]
        in_specs += [vmem] * (1 + len(others))
    if not last:
        out_shape.append(jax.ShapeDtypeStruct((PARTS, SEND * FEATS, BLK), BF))
        out_specs.append(vmem)
    if ids is not None:
        rows = FEATS * (1 + len(others))
        shape = (NARROW, rows, QUAD_NODES) if last else (rows, TRAIN)
        out_shape.append(jax.ShapeDtypeStruct(shape, BF))
        out_specs.append(vmem)
    if first:
        out_shape.append(jax.ShapeDtypeStruct((NB, BLK), F32))
        out_specs.append(vmem)
    scratch = [
        pltpu.VMEM((2 * NB, FEATS, BLK), BF),
        pltpu.VMEM((NB, FEATS, BLK), BF),
        pltpu.VMEM(tiles.shape, BF),
        pltpu.SemaphoreType.DMA((NB // CHUNK + 1,)),
    ]
    return pl.pallas_call(
        functools.partial(
            apply_kernel, second=second and hop + 1, first=first, last=last,
            picking=0 if ids is None else 1 + len(others),
        ),
        out_shape=out_shape,
        in_specs=in_specs,
        out_specs=out_specs,
        scratch_shapes=scratch,
        input_output_aliases=aliases,
        compiler_params=params(28),
        name=f"apply_{'second' if second else 'first'}_{hop}",
    )(*operands)


def layer_kernel(
    place, early_h, grads_h, final, counts, owners,
    query_h, key_h, value_h, out_h, out_th, up_h, up_th, down_h,
    result, query_s, key_s, value_s, mixed_s, probs_s, act_s, pre_s, gmix_s, gq_s, gk_s, gv_s, gr_s,
    query_w, key_w, value_w, out_w, out_t, up_w, up_t, down_w, early, grads, sems,
):
    own = place[0]
    mine = pl.ds(pl.multiple_of(place[1] * QUAD_NODES, QUAD_NODES), QUAD_NODES)
    pairs = (
        (query_h, query_w), (key_h, key_w), (value_h, value_w), (out_h, out_w),
        (up_h, up_w), (down_h, down_w), (up_th, up_t), (out_th, out_t),
        (early_h.at[:, :, mine], early), (grads_h.at[:, :, mine], grads),
    )
    loads = [
        pltpu.make_async_copy(source, target, sems.at[index])
        for index, (source, target) in enumerate(pairs)
    ]
    for index in (8, 0, 1, 2, 9, 3, 4, 5, 6, 7):
        loads[index].start()
    width = TOKS * QUAD_NODES
    loads[8].wait()
    tokens = jnp.concatenate(
        [early[:, t * FEATS : (t + 1) * FEATS, :].reshape(D, QUAD_NODES) for t in range(HOPS)]
        + [final[...].reshape(D, QUAD_NODES)],
        axis=1,
    )

    def normalize(hidden):
        center = hidden - jnp.mean(hidden, axis=0, keepdims=True)
        inverse = lax.rsqrt(jnp.mean(center * center, axis=0, keepdims=True) + EPSILON)
        return center * inverse, inverse

    normed_a = normalize(tokens.astype(F32))[0].astype(BF)
    loads[0].wait()
    query_s[...] = dot(query_w[...], normed_a).astype(BF)
    loads[1].wait()
    key_s[...] = dot(key_w[...], normed_a).astype(BF)
    loads[2].wait()
    value_s[...] = dot(value_w[...], normed_a).astype(BF)
    score_scale = 1.0 / math.sqrt(HEAD_DIM)

    def columns(half):
        return [
            pl.ds(pl.multiple_of(t * QUAD_NODES + half * BLK, BLK), BLK) for t in range(TOKS)
        ]

    def parts(ref, rows, cols):
        return [ref[rows, c].astype(F32) for c in cols]

    def forward_head(step, carry):
        h = step // 2
        cols = columns(step % 2)
        rows = pl.ds(pl.multiple_of(h * HEAD_DIM, HEAD_DIM), HEAD_DIM)
        query, key, value = [parts(ref, rows, cols) for ref in (query_s, key_s, value_s)]
        all_probs = []
        for t in range(TOKS):
            scores = [
                jnp.sum(query[t] * key[u], axis=0, keepdims=True) * score_scale
                for u in range(TOKS)
            ]
            top = jnp.maximum(
                jnp.maximum(scores[0], scores[1]), jnp.maximum(scores[2], scores[3])
            )
            raised = [jnp.exp(s - top) for s in scores]
            total = raised[0] + raised[1] + raised[2] + raised[3]
            probs = [r / total for r in raised]
            all_probs += probs
            low = [p.astype(BF).astype(F32) for p in probs]
            mixed_s[rows, cols[t]] = (
                low[0] * value[0] + low[1] * value[1] + low[2] * value[2] + low[3] * value[3]
            ).astype(BF)
        probs_s[step] = jnp.concatenate(all_probs, axis=0)
        return carry

    lax.fori_loop(0, 2 * HEADS, forward_head, 0)
    loads[3].wait()
    residual = (tokens.astype(F32) + dot(out_w[...], mixed_s[...])).astype(BF)
    second_norm, second_inv = normalize(residual.astype(F32))
    normed_b = second_norm.astype(BF)

    root = math.sqrt(2.0 / math.pi)
    groups = FF_CHUNK // (QUAD * GROUP)

    loads[9].wait()
    named = lax.broadcasted_iota(jnp.int32, (OWNERS, QUAD_NODES), 0) == owners[:, mine]
    by_owner = jnp.concatenate([1.0 / counts[...]] * (QUAD_NODES // OWNERS), axis=1)
    row_scale = jnp.sum(jnp.where(named, by_owner, 0.0), axis=0, keepdims=True)
    scaled = jnp.concatenate(
        [
            (
                grads[:, t * FEATS : (t + 1) * FEATS, :].reshape(D, QUAD_NODES).astype(F32)
                * row_scale
            ).astype(BF)
            for t in range(TOKS)
        ],
        axis=1,
    )

    def ffn_chunk(i, carry):
        rows = pl.ds(pl.multiple_of(i * FF_CHUNK, FF_CHUNK), FF_CHUNK)
        pre = dot(up_w[rows, :], normed_b)
        grad_act = dot(down_w[rows, :], scaled)
        square = pre * pre
        gate = 0.5 + 0.5 * jnp.tanh(pre * (root + (root * 0.044715) * square))
        activated = pre * gate
        slope = gate + activated * (1.0 - gate) * (
            2.0 * root + (6.0 * root * 0.044715) * square
        )
        at = pl.ds(i * groups, groups)
        act_s[at] = activated.astype(BF).reshape(groups, QUAD, GROUP, width)
        pre_s[at] = (grad_act * slope).astype(BF).reshape(groups, QUAD, GROUP, width)
        return carry

    loads[4].wait()
    loads[5].wait()
    lax.fori_loop(0, FF // FF_CHUNK, ffn_chunk, 0)

    share = FF // QUAD
    grad_down = dot_rows(act_s[:, own].reshape(share, width), scaled)
    result[:, 2 * GROUP : 3 * GROUP, :] = grad_down.astype(BF).reshape(DESTS, GROUP, D)
    grad_up = dot_rows(pre_s[:, own].reshape(share, width), normed_b)
    result[:, GROUP : 2 * GROUP, :] = grad_up.astype(BF).reshape(DESTS, GROUP, D)

    loads[6].wait()
    grad_normed = dot(up_t[...], pre_s[...].reshape(FF, width))
    grad_resid = (
        scaled.astype(F32)
        + second_inv
        * (
            grad_normed
            - jnp.mean(grad_normed, axis=0, keepdims=True)
            - second_norm * jnp.mean(grad_normed * second_norm, axis=0, keepdims=True)
        )
    ).astype(BF)
    gr_s[...] = grad_resid.reshape(HEADS, QUAD, GROUP, width)
    loads[7].wait()
    gmix_s[...] = dot(out_t[...], grad_resid).astype(BF)

    def backward_head(step, carry):
        h = step // 2
        cols = columns(step % 2)
        rows = pl.ds(pl.multiple_of(h * HEAD_DIM, HEAD_DIM), HEAD_DIM)
        query, key, value, grad_mixed = [
            parts(ref, rows, cols) for ref in (query_s, key_s, value_s, gmix_s)
        ]
        saved = probs_s[step]
        prob = lambda t, u: saved[t * TOKS + u : t * TOKS + u + 1, :]
        weights = []
        grad_query = []
        for t in range(TOKS):
            grad_probs = [
                jnp.sum(grad_mixed[t] * value[u], axis=0, keepdims=True) for u in range(TOKS)
            ]
            inner = sum(prob(t, u) * grad_probs[u] for u in range(TOKS))
            weight = [
                (prob(t, u) * (grad_probs[u] - inner) * score_scale).astype(BF).astype(F32)
                for u in range(TOKS)
            ]
            weights.append(weight)
            grad_query.append(sum(weight[u] * key[u] for u in range(TOKS)))
        grad_key = [sum(weights[t][u] * query[t] for t in range(TOKS)) for u in range(TOKS)]
        grad_value = [
            sum(prob(t, u).astype(BF).astype(F32) * grad_mixed[t] for t in range(TOKS))
            for u in range(TOKS)
        ]
        for ref, pieces in ((gq_s, grad_query), (gk_s, grad_key), (gv_s, grad_value)):
            for t in range(TOKS):
                ref[h, :, :, cols[t]] = pieces[t].astype(BF).reshape(QUAD, GROUP, BLK)
        return carry

    lax.fori_loop(0, 2 * HEADS, backward_head, 0)
    share = D // QUAD
    stacked = jnp.concatenate(
        [ref[:, own].reshape(share, width) for ref in (gq_s, gk_s, gv_s)], axis=0
    )
    count = HEADS * 3
    result[:count, 0:GROUP, :] = dot_rows(stacked, normed_a).astype(BF).reshape(count, GROUP, D)
    sum_out = dot_rows(gr_s[:, own].reshape(share, width), mixed_s[...])
    result[count:, 0:GROUP, :] = sum_out.astype(BF).reshape(HEADS, GROUP, D)


def in_hbm(array):
    return pltpu.with_memory_space_constraint(array, pltpu.HBM)


def layer(place, early, grads, final, counts, owners, *weights):
    width = TOKS * QUAD_NODES
    square = pltpu.VMEM((D, width), BF)
    grouped = pltpu.VMEM((HEADS, QUAD, GROUP, width), BF)
    wide = pltpu.VMEM((DESTS, QUAD, GROUP, width), BF)
    vmem = pl.BlockSpec(memory_space=pltpu.VMEM)
    hbm = pl.BlockSpec(memory_space=pltpu.HBM)
    smem = pl.BlockSpec(memory_space=pltpu.SMEM)
    return pl.pallas_call(
        layer_kernel,
        out_shape=jax.ShapeDtypeStruct((DESTS, 3 * GROUP, D), BF),
        in_specs=[smem, hbm, hbm, vmem, vmem, vmem] + [hbm] * 8,
        out_specs=vmem,
        scratch_shapes=[
            square, square, square, square,
            pltpu.VMEM((2 * HEADS, TOKS * TOKS, BLK), F32),
            wide, wide, square, grouped, grouped, grouped, grouped,
            *[pltpu.VMEM(w.shape, BF) for w in weights],
            pltpu.VMEM((NARROW, HOPS * FEATS, QUAD_NODES), BF),
            pltpu.VMEM((NARROW, TOKS * FEATS, QUAD_NODES), BF),
            pltpu.SemaphoreType.DMA((len(weights) + 2,)),
        ],
        compiler_params=params(58),
        name="layer",
    )(
        place, in_hbm(early), in_hbm(grads), final, counts, owners,
        *[in_hbm(w) for w in weights],
    )


def exchange(array, axes):
    return lax.all_to_all(array, axes, split_axis=0, concat_axis=0, tiled=True)


def on_device(
    features, edge_tiles, block_lists, send_lists, train_ids, owners, cotangent,
    query_weight, key_weight, value_weight, out_weight, up_weight, down_weight,
):
    ids = train_ids.reshape(1, TRAIN)
    grads = lax.all_gather(cotangent.reshape(TOKS * FEATS, TRAIN), NARROW_AXES)
    named = (owners == jnp.arange(OWNERS, dtype=jnp.int32)[None]).astype(F32)
    counts = lax.psum(
        jnp.broadcast_to(jnp.sum(named, axis=0)[:, None], (OWNERS, OWNERS)), WIDE
    )
    incoming = exchange(pack(send_lists, features), WIDE)
    incoming, up_t, out_t = lax.optimization_barrier((incoming, up_weight.T, out_weight.T))
    step = functools.partial(apply, block_lists, send_lists, edge_tiles)
    current = features
    hops = None
    fields = [features]
    for hop in range(HOPS):
        if hop == 0:
            once, outgoing, degree = step(current, incoming)
        else:
            once, outgoing = step(current, incoming, degree, hop=hop)
        incoming = exchange(outgoing, WIDE)
        results = step(
            once, incoming, degree, previous=current, hops=hops, hop=hop,
            ids=None if hop == 0 else ids,
            others=tuple(fields) if hop == HOPS - 2 else (),
        )
        current, hops = results[0], results[1]
        fields.append(current)
        if hop == HOPS - 2:
            early = lax.all_gather(results[3], NARROW_AXES)
        if hop < HOPS - 1:
            incoming = exchange(results[2], WIDE)
    final = exchange(results[2], NARROW_AXES)

    place = jnp.stack(
        [2 * lax.axis_index("xl") + lax.axis_index("c"), lax.axis_index("xh")]
    ).astype(jnp.int32)
    partial = layer(
        place, early, grads, final, counts, owners.reshape(1, TRAIN),
        query_weight, key_weight, value_weight, out_weight, out_t, up_weight, up_t, down_weight,
    )
    gathered = exchange(partial, QUADS)
    sums = jnp.sum(gathered.astype(F32), axis=0)
    return (hops, sums[:GROUP], sums[GROUP : 2 * GROUP], sums[2 * GROUP :])


def solution(mesh):
    split = Mesh(mesh.devices.reshape(4, 4, 2, 2, 2), ("z", "y", "xh", "xl", "c"))
    rows = P(WIDE + NARROW_AXES, None)
    in_specs = (
        P(NARROW_AXES, WIDE),
        P(WIDE, None, None, None),
        P(WIDE, None),
        P(WIDE, None, None),
        P(WIDE),
        P(WIDE, None),
        P(None, NARROW_AXES, WIDE),
        P(), P(), P(), P(), P(), P(),
    )
    out_specs = (P(None, NARROW_AXES, WIDE), rows, rows, rows)
    return jax.shard_map(
        on_device, mesh=split, in_specs=in_specs, out_specs=out_specs, check_vma=False
    )
```

time: 219 us -> 221 us (level)
  Pallas kernels: 51.4 us -> 72.7 us
  blocking collectives: 113 us -> 95.7 us
  between operations: 0.81 us -> 15.6 us
  waiting for transfers between devices: 25 us -> 14.5 us
  local copies, waits for them, and re-layouts: 11.2 us -> 7.47 us
  starting transfers between devices: 16 us -> 12.6 us
    all_to_all x6, blocking collectives: 113 us -> 95.7 us  [exchange(): return lax.all_to_all(array, axes, split_axis=0, concat_axis=0, tiled=True)]
    pallas_call x6, Pallas kernels: 29.8 us -> 42.2 us  [apply(): pl.pallas_call(functools.partial(apply_kernel, second=second and hop + 1,...]
    all_to_all x3 -> x2, waiting for transfers between devices: 25 us -> 13.9 us  [exchange(): return lax.all_to_all(array, axes, split_axis=0, concat_axis=0, tiled=True)]
    pallas_call x3 -> x1, Pallas kernels: 18.7 us -> 27.8 us  [layer(): pl.pallas_call(layer_kernel, out_shape=jax.ShapeDtypeStruct((DESTS, 3 * G...]
    unnamed x24 -> x14, local copies, waits for them, and re-layouts: 10.5 us -> 6.13 us
    all_to_all x3 -> x2, starting transfers between devices: 16 us -> 12.5 us  [exchange(): return lax.all_to_all(array, axes, split_axis=0, concat_axis=0, tiled=True)]
  transfers between devices with their start and end apart: 3 -> 5, of which waited for: 3 -> 2; matrix products, arithmetic and copies ran while one was open for 2% -> 3% of each run, Pallas kernels for 1% -> 20%
where the time goes in v3:
time: 221 us; the launch traced here: 220 us
  blocking collectives  95.7 us (43%)
  Pallas kernels  72.7 us (33%)
  between operations  15.6 us (7%)
  waiting for transfers between devices  14.5 us (7%)
  starting transfers between devices  12.6 us (6%)
  local copies, waits for them, and re-layouts  7.47 us (3%)
    all_to_all x6, blocking collectives, exchange(): return lax.all_to_all(array, axes, split_axis=0, concat_axis=0, tiled=True)  95.7 us
    pallas_call x6, Pallas kernels, apply(): pl.pallas_call(functools.partial(apply_kernel, second=second and hop + 1,...  42.2 us
    pallas_call x1, Pallas kernels, layer(): pl.pallas_call(layer_kernel, out_shape=jax.ShapeDtypeStruct((DESTS, 3 * G...  27.8 us
    all_to_all x2, waiting for transfers between devices, exchange(): return lax.all_to_all(array, axes, split_axis=0, concat_axis=0, tiled=True)  13.9 us
    all_to_all x2, starting transfers between devices, exchange(): return lax.all_to_all(array, axes, split_axis=0, concat_axis=0, tiled=True)  12.5 us
    unnamed x14, local copies, waits for them, and re-layouts  6.13 us
  transfers between devices with their start and end apart: 5, of which 2 were waited for; matrix products, arithmetic and copies ran while one was open for 3% of the time, Pallas kernels for 20%

profile of v3, /device:TPU:0, one launch (start us, length us, event | category | flops | bytes accessed | tf_op | source)
XLA Modules:
  0.0 220.3 jit_solution(7557831411949676064)
XLA Ops:
  8.0 0.0 copy-start.4
  8.0 0.0 copy-start.2
  8.0 0.0 all-reduce.2.cloned.1.call-start
  8.1 1.0 convert_reduce_fusion.1
  9.0 0.7 broadcast_in_dim.2
  9.7 0.0 all-reduce.2.cloned.1.call-update
  9.8 0.0 all-gather.4.cloned.1.call-start
  9.8 0.5 all-gather.4.cloned.1.call-update
  10.3 0.8 copy.66.sends.refs_1_.refs_7_
  11.1 2.8 %pack.1 = bf16[16,128,128]{2,1,0:T(8,128)(2,1)} custom-call(s32[1,16,2]{2,1,0:T(8,128)S(1)} %copy.66.sends.refs_1_.refs_7_, bf16[64,4096]{1,0:T(8,128)(2,1)} %refs_9_.1), custom_call_target="tpu_custom_call" | custom-call | tf_op jit(solution)/shard_map/pack/pallas_call | solution.py:74
  13.9 8.2 %all-to-all-start = ((bf16[16,128,128]{2,1,0:T(8,128)(2,1)}), bf16[16,128,128]{2,1,0:T(8,128)(2,1)S(1)}, u32[]{:S(2)}, u32[]{:S(2)}) async-start(bf16[16,128,128]{2,1,0:T(8,128)(2,1)} %pack.1), calls=%async_computation | async-start | bytes 1048576 | tf_op jit(solution)/shard_map/all_to_all | solution.py:452
  22.1 0.0 all-gather.6.cloned.1.call-start
  22.2 0.0 copy-done.4
  22.2 0.1 copy.65.refs_0_
  22.3 0.0 copy-done.2
  22.3 0.0 copy-start
  22.3 2.5 %copy.52 = bf16[2048,512]{0,1:T(8,128)(2,1)} copy(bf16[2048,512]{1,0:T(8,128)(2,1)S(1)} %copy-done.2) | data formatting | bytes 4194304 | tf_op args[11]
  24.8 2.1 copy.53
  26.8 7.0 %all-to-all-done.refs_4_ = bf16[16,128,128]{2,1,0:T(8,128)(2,1)S(1)} async-done(((bf16[16,128,128]{2,1,0:T(8,128)(2,1)}), bf16[16,128,128]{2,1,0:T(8,128)(2,1)S(1)}, u32[]{:S(2)}, u32[]{:S(2)}) %all-to-all-start) | async-done | bytes 524320 | tf_op jit(solution)/shard_map/all_to_all | solution.py:452
  33.8 0.0 copy-done
  33.8 6.4 %apply_first_0.1 = (bf16[64,4096]{1,0:T(8,128)(2,1)S(1)}, bf16[16,128,128]{2,1,0:T(8,128)(2,1)S(1)}, f32[32,128]{1,0:T(8,128)S(1)}) custom-call(s32[32,12]{1,0:T(8,128)S(1)} %copy.65.refs_0_, s32[1,16,2]{2,1,0:T(8,128)S(1)} %copy.66.sends.refs_1_.refs_7_, bf16[32,12,128,128]{3,2,1,0:T(8,128)(2,1)} %refs_2_.11, bf16[64,4096]{1,0:T(8,128)(2,1)S(1)} %copy-done, ...), custom_call_target="tpu_custom_call" | custom-call | tf_op jit(solution)/shard_map/apply_first_0/pallas_call | solution.py:221
  40.2 14.1 %all_to_all.40.refs_4_ = bf16[16,128,128]{2,1,0:T(8,128)(2,1)S(1)} all-to-all(bf16[16,128,128]{2,1,0:T(8,128)(2,1)S(1)} %get-tuple-element.25), channel_id=1, replica_groups=mesh['z'=4,'y'=4,'xh'=2,'xl'=2,'c'=2] {'z','y'}, dimensions={0} | all-to-all | bytes 1048576 | tf_op jit(solution)/shard_map/all_to_all | solution.py:452
  54.3 7.1 %apply_second_0.1 = (bf16[64,4096]{1,0:T(8,128)(2,1)S(1)}, bf16[3,64,4096]{2,1,0:T(8,128)(2,1)}, bf16[16,128,128]{2,1,0:T(8,128)(2,1)S(1)}) custom-call(s32[32,12]{1,0:T(8,128)S(1)} %copy.65.refs_0_, s32[1,16,2]{2,1,0:T(8,128)S(1)} %copy.66.sends.refs_1_.refs_7_, bf16[32,12,128,128]{3,2,1,0:T(8,128)(2,1)} %refs_2_.11, ...), custom_call_target="tpu_custom_call" | custom-call | tf_op jit(solution)/shard_map/apply_second_0/pallas_call | solution.py:221
  61.3 13.3 %all_to_all.41.refs_4_ = bf16[16,128,128]{2,1,0:T(8,128)(2,1)S(1)} all-to-all(bf16[16,128,128]{2,1,0:T(8,128)(2,1)S(1)} %get-tuple-element.28), channel_id=1, replica_groups=mesh['z'=4,'y'=4,'xh'=2,'xl'=2,'c'=2] {'z','y'}, dimensions={0} | all-to-all | bytes 1048576 | tf_op jit(solution)/shard_map/all_to_all | solution.py:452
  74.7 0.0 copy-start.1
  74.7 6.2 %apply_first_1.1 = (bf16[64,4096]{1,0:T(8,128)(2,1)S(1)}, bf16[16,128,128]{2,1,0:T(8,128)(2,1)S(1)}) custom-call(s32[32,12]{1,0:T(8,128)S(1)} %copy.65.refs_0_, s32[1,16,2]{2,1,0:T(8,128)S(1)} %copy.66.sends.refs_1_.refs_7_, bf16[32,12,128,128]{3,2,1,0:T(8,128)(2,1)} %refs_2_.11, bf16[64,4096]{1,0:T(8,128)(2,1)S(1)} %get-tuple-element.27.refs_3_.refs_6_.refs_10_, ...), custom_call_target="tpu_custom_call" | custom-call | tf_op jit(solution)/shard_map/apply_first_1/pallas_call | solution.py:221
  80.8 13.2 %all_to_all.42.refs_4_ = bf16[16,128,128]{2,1,0:T(8,128)(2,1)S(1)} all-to-all(bf16[16,128,128]{2,1,0:T(8,128)(2,1)S(1)} %get-tuple-element.30), channel_id=1, replica_groups=mesh['z'=4,'y'=4,'xh'=2,'xl'=2,'c'=2] {'z','y'}, dimensions={0} | all-to-all | bytes 1048576 | tf_op jit(solution)/shard_map/all_to_all | solution.py:452
  94.1 0.0 copy-done.1
  94.1 8.5 %apply_second_1.1 = (bf16[64,4096]{1,0:T(8,128)(2,1)S(1)}, bf16[3,64,4096]{2,1,0:T(8,128)(2,1)}, bf16[16,128,128]{2,1,0:T(8,128)(2,1)S(1)}, bf16[192,512]{1,0:T(8,128)(2,1)}) custom-call(s32[32,12]{1,0:T(8,128)S(1)} %copy.65.refs_0_, s32[1,16,2]{2,1,0:T(8,128)S(1)} %copy.66.sends.refs_1_.refs_7_, ...), custom_call_target="tpu_custom_call", output_to_operand_aliasing={{1}: (7, {})} | custom-call | tf_op jit(solution)/shard_map/apply_second_1/pallas_call | solution.py:221
  102.5 0.0 all-gather.6.cloned.1.call-update
  102.6 13.1 %all_to_all.43.refs_4_ = bf16[16,128,128]{2,1,0:T(8,128)(2,1)S(1)} all-to-all(bf16[16,128,128]{2,1,0:T(8,128)(2,1)S(1)} %get-tuple-element.33), channel_id=1, replica_groups=mesh['z'=4,'y'=4,'xh'=2,'xl'=2,'c'=2] {'z','y'}, dimensions={0} | all-to-all | bytes 1048576 | tf_op jit(solution)/shard_map/all_to_all | solution.py:452
  115.7 6.3 %apply_first_2.1 = (bf16[64,4096]{1,0:T(8,128)(2,1)S(1)}, bf16[16,128,128]{2,1,0:T(8,128)(2,1)S(1)}) custom-call(s32[32,12]{1,0:T(8,128)S(1)} %copy.65.refs_0_, s32[1,16,2]{2,1,0:T(8,128)S(1)} %copy.66.sends.refs_1_.refs_7_, bf16[32,12,128,128]{3,2,1,0:T(8,128)(2,1)} %refs_2_.11, bf16[64,4096]{1,0:T(8,128)(2,1)S(1)} %get-tuple-element.32.refs_3_.refs_6_, ...), custom_call_target="tpu_custom_call" | custom-call | tf_op jit(solution)/shard_map/apply_first_2/pallas_call | solution.py:221
  122.0 13.1 %all_to_all.44.refs_4_ = bf16[16,128,128]{2,1,0:T(8,128)(2,1)S(1)} all-to-all(bf16[16,128,128]{2,1,0:T(8,128)(2,1)S(1)} %get-tuple-element.35), channel_id=1, replica_groups=mesh['z'=4,'y'=4,'xh'=2,'xl'=2,'c'=2] {'z','y'}, dimensions={0} | all-to-all | bytes 1048576 | tf_op jit(solution)/shard_map/all_to_all | solution.py:452
  135.0 7.8 %apply_second_2.1 = (bf16[64,4096]{1,0:T(8,128)(2,1)}, bf16[3,64,4096]{2,1,0:T(8,128)(2,1)}, bf16[8,64,256]{2,1,0:T(8,128)(2,1)}) custom-call(s32[32,12]{1,0:T(8,128)S(1)} %copy.65.refs_0_, s32[1,16,2]{2,1,0:T(8,128)S(1)} %copy.66.sends.refs_1_.refs_7_, bf16[32,12,128,128]{3,2,1,0:T(8,128)(2,1)} %refs_2_.11, ...), custom_call_target="tpu_custom_call", output_to_operand_aliasing={{1}: (7, {})} | custom-call | tf_op jit(solution)/shard_map/apply_second_2/pallas_call | solution.py:221
  142.9 4.3 %all-to-all-start.6 = ((bf16[8,64,256]{2,1,0:T(8,128)(2,1)}), bf16[8,64,256]{2,1,0:T(8,128)(2,1)S(1)}, u32[]{:S(2)}, u32[]{:S(2)}) async-start(bf16[8,64,256]{2,1,0:T(8,128)(2,1)} %get-tuple-element.39), calls=%async_computation.6 | async-start | bytes 524288 | tf_op jit(solution)/shard_map/all_to_all | solution.py:452
  147.1 0.6 pad_add_fusion.place
  147.7 0.0 all-reduce.2.cloned.1.call-done.counts
  147.7 7.0 %all-to-all-done.6.final = bf16[8,64,256]{2,1,0:T(8,128)(2,1)S(1)} async-done(((bf16[8,64,256]{2,1,0:T(8,128)(2,1)}), bf16[8,64,256]{2,1,0:T(8,128)(2,1)S(1)}, u32[]{:S(2)}, u32[]{:S(2)}) %all-to-all-start.6) | async-done | bytes 262176 | tf_op jit(solution)/shard_map/all_to_all | solution.py:452
  154.7 0.0 copy-start.3
  154.7 0.0 all-gather.4.cloned.1.call-done.grads_h
  154.7 0.0 all-gather.6.cloned.1.call-done
  154.7 0.7 copy-done.3
  155.4 27.8 %layer.1 = bf16[32,48,512]{2,1,0:T(8,128)(2,1)} custom-call(s32[2]{0:T(128)} %pad_add_fusion.place, bf16[8,192,512]{2,1,0:T(8,128)(2,1)} %bitcast.13, bf16[8,256,512]{2,1,0:T(8,128)(2,1)} %all-gather.4.cloned.1.call-done.grads_h, bf16[8,64,256]{2,1,0:T(8,128)(2,1)} %copy-done.3, f32[128,128]{1,0:T(8,128)} %all-reduce.2.cloned.1.call-done.counts, ...), custom_call_target="tpu_custom_call" | custom-call | tf_op jit(solution)/shard_map/layer/pallas_call | solution.py:429
  183.2 28.8 %all_to_all.45 = bf16[32,48,512]{2,1,0:T(8,128)(2,1)S(1)} all-to-all(bf16[32,48,512]{2,1,0:T(8,128)(2,1)} %layer.1), channel_id=1, replica_groups=mesh['z'=4,'y'=4,'xh'=2,'xl'=2,'c'=2] {'z','y','xh'}, dimensions={0} | all-to-all | bytes 3145728 | tf_op jit(solution)/shard_map/all_to_all | solution.py:452
  212.0 0.2 convert_reduce_fusion
  212.3 0.6 fusion
Async XLA Ops:
  8.0 14.2 %copy-start.4 = (s32[32,12]{0,1:T(8,128)S(1)}, s32[32,12]{0,1:T(8,128)}, u32[]{:S(2)}) copy-start(s32[32,12]{0,1:T(8,128)} %param.15) | copy-start | bytes 4612
  8.0 14.3 %copy-start.2 = (bf16[2048,512]{1,0:T(8,128)(2,1)S(1)}, bf16[2048,512]{1,0:T(8,128)(2,1)}, u32[]{:S(2)}) copy-start(bf16[2048,512]{1,0:T(8,128)(2,1)} %up_h.1) | copy-start | bytes 6291460
  8.0 139.7 %all-reduce.2.cloned.1.call-start = ((), (), s32[]{:S(2)}) async-start(), calls=%async_computation.9 | async-start | bytes 131072 | tf_op jit(solution)/shard_map/psum | solution.py:462
  9.8 144.9 %all-gather.4.cloned.1.call-start = ((), (), s32[]{:S(2)}) async-start(), calls=%async_computation.8 | async-start | bytes 2359296 | tf_op jit(solution)/shard_map/all_gather | solution.py:460
  13.9 19.9 %all-to-all-start = ((bf16[16,128,128]{2,1,0:T(8,128)(2,1)}), bf16[16,128,128]{2,1,0:T(8,128)(2,1)S(1)}, u32[]{:S(2)}, u32[]{:S(2)}) async-start(bf16[16,128,128]{2,1,0:T(8,128)(2,1)} %pack.1), calls=%async_computation | async-start | bytes 1048576 | tf_op jit(solution)/shard_map/all_to_all | solution.py:452
  22.1 132.6 %all-gather.6.cloned.1.call-start = ((), (), s32[]{:S(2)}) async-start(), calls=%async_computation.10 | async-start | bytes 1769472 | tf_op jit(solution)/shard_map/all_gather | solution.py:485
  22.3 11.5 %copy-start = (bf16[64,4096]{1,0:T(8,128)(2,1)S(1)}, bf16[64,4096]{1,0:T(8,128)(2,1)}, u32[]{:S(2)}) copy-start(bf16[64,4096]{1,0:T(8,128)(2,1)} %refs_9_.1) | copy-start | bytes 1572868
  74.7 19.4 %copy-start.1 = (s32[512]{0:T(512)S(1)}, s32[512]{0:T(512)}, u32[]{:S(2)}) copy-start(s32[512]{0:T(512)} %param.17) | copy-start | bytes 6148
  142.9 11.8 %all-to-all-start.6 = ((bf16[8,64,256]{2,1,0:T(8,128)(2,1)}), bf16[8,64,256]{2,1,0:T(8,128)(2,1)S(1)}, u32[]{:S(2)}, u32[]{:S(2)}) async-start(bf16[8,64,256]{2,1,0:T(8,128)(2,1)} %get-tuple-element.39), calls=%async_computation.6 | async-start | bytes 524288 | tf_op jit(solution)/shard_map/all_to_all | solution.py:452
  154.7 0.7 copy-start.3
Sparse Core Ops, SparseCore 0:
  12.0 86.8 all-reduce.1
Sparse Core Ops, SparseCore 1:
  12.0 27.7 all-gather.3
  102.7 21.7 all-gather.5

commit v4 on v3

--- a/solution.py
+++ b/solution.py
@@ -28,8 +28,9 @@
 NARROW = 8
 DESTS = 32
 GROUP = 16
-UNROLL = 4
-FF_CHUNK = 256
+UNROLL = 8
+PICK_BLOCKS = 4
+FF_CHUNK = 512
 EPSILON = 1e-05
 
 BF = jnp.bfloat16
@@ -37,7 +38,6 @@
 WIDE = ("z", "y")
 NARROW_AXES = ("xh", "xl", "c")
 QUADS = ("z", "y", "xh")
-CHUNK = 4
 
 
 def params(limit_mib):
@@ -52,7 +52,7 @@
     return lax.dot_general(left, right, (((1,), (1,)), ((), ())), preferred_element_type=F32)
 
 
-def pack_kernel(sends, field, outgoing, sems):
+def pack_kernel(sends, field, owners, outgoing, counts, sems):
     copies = []
     for slot in range(PARTS * SEND):
         start = pl.multiple_of(sends[0, slot // SEND, slot % SEND] * BLK, BLK)
@@ -66,39 +66,51 @@
         )
     for copy in copies:
         copy.start()
+    named = lax.broadcasted_iota(jnp.int32, (OWNERS, TRAIN), 0) == owners[...]
+    count = jnp.sum(jnp.where(named, 1.0, 0.0), axis=1, keepdims=True)
+    counts[...] = jnp.broadcast_to(count, (OWNERS, OWNERS))
     for copy in copies:
         copy.wait()
 
 
-def pack(sends, field):
+def pack(sends, field, owners):
     return pl.pallas_call(
         pack_kernel,
-        out_shape=jax.ShapeDtypeStruct((PARTS, SEND * FEATS, BLK), BF),
+        out_shape=[
+            jax.ShapeDtypeStruct((PARTS, SEND * FEATS, BLK), BF),
+            jax.ShapeDtypeStruct((OWNERS, OWNERS), F32),
+        ],
         in_specs=[
             pl.BlockSpec(memory_space=pltpu.SMEM),
             pl.BlockSpec(memory_space=pltpu.HBM),
+            pl.BlockSpec(memory_space=pltpu.VMEM),
         ],
         scratch_shapes=[pltpu.SemaphoreType.DMA((PARTS * SEND,))],
         compiler_params=params(4),
         name="pack",
-    )(sends, in_hbm(field))
+    )(sends, in_hbm(field), owners)
 
 
 def picked_columns(ids, fields):
     id_row = ids[...]
-    total = None
-    for b in range(NB):
-        rows = lax.broadcasted_iota(jnp.int32, (BLK, TRAIN), 0) + b * BLK
-        chosen = jnp.where(rows == id_row, 1.0, 0.0).astype(BF)
-        block = jnp.concatenate([field[:, b * BLK : (b + 1) * BLK] for field in fields], axis=0)
-        term = dot(block, chosen)
-        total = term if total is None else total + term
-    return total.astype(BF)
-
-
-def apply_kernel(*refs, second, first, last, picking):
+
+    def add_blocks(i, total):
+        for j in range(PICK_BLOCKS):
+            b = i * PICK_BLOCKS + j
+            rows = lax.broadcasted_iota(jnp.int32, (BLK, TRAIN), 0) + b * BLK
+            chosen = jnp.where(rows == id_row, 1.0, 0.0).astype(BF)
+            cols = pl.ds(pl.multiple_of(b * BLK, BLK), BLK)
+            block = jnp.concatenate([field[:, cols] for field in fields], axis=0)
+            total = total + dot(block, chosen)
+        return total
+
+    start = jnp.zeros((FEATS * len(fields), TRAIN), F32)
+    return lax.fori_loop(0, NB // PICK_BLOCKS, add_blocks, start).astype(BF)
+
+
+def apply_kernel(*refs, second, first, last, picking, stage):
     refs = list(refs)
-    lists, sends, tiles_h, field, incoming = refs[:5]
+    lists, sends, tiles, field, incoming = refs[:5]
     refs = refs[5:]
     degree = None if first else refs.pop(0)
     previous = refs.pop(0) if second else None
@@ -110,15 +122,16 @@
     outgoing = None if last else refs.pop(0)
     rows_out = refs.pop(0) if picking else None
     degree_out = refs.pop(0) if first else None
-    pool, fresh, tiles, sems = refs
-    loads = [
-        pltpu.make_async_copy(
-            tiles_h.at[pl.ds(i * CHUNK, CHUNK)], tiles.at[pl.ds(i * CHUNK, CHUNK)], sems.at[i]
-        )
-        for i in range(NB // CHUNK)
-    ]
-    for load in loads:
-        load.start()
+    tiles_h, tiles = (tiles, refs.pop(0)) if stage else (None, tiles)
+    pool, fresh, sems = refs
+
+    def load(i):
+        blocks = pl.ds(i * UNROLL, UNROLL)
+        return pltpu.make_async_copy(tiles_h.at[blocks], tiles.at[blocks], sems.at[i])
+
+    if stage:
+        for i in range(NB // UNROLL):
+            load(i).start()
 
     for j in range(NB):
         pool[j] = field[:, j * BLK : (j + 1) * BLK]
@@ -126,7 +139,7 @@
         rows = (j % SEND) * FEATS
         pool[NB + j] = incoming[j // SEND, rows : rows + FEATS, :]
 
-    def one_block(b, carry):
+    def one_block(b):
         picked = jnp.concatenate([pool[lists[b, k]] for k in range(K)], axis=1)
         if first:
             picked = jnp.concatenate([picked, jnp.ones((GROUP, K * BLK), BF)], axis=0)
@@ -145,13 +158,17 @@
             ).astype(BF)
         result[:, cols] = value
         fresh[b] = value
+
+    def some_blocks(i, carry):
+        if stage:
+            load(i).wait()
+        for j in range(UNROLL):
+            one_block(i * UNROLL + j)
         return carry
 
-    for i, load in enumerate(loads):
-        load.wait()
-        lax.fori_loop(i * CHUNK, (i + 1) * CHUNK, one_block, 0, unroll=UNROLL)
+    lax.fori_loop(0, NB // UNROLL, some_blocks, 0)
     if second:
-        store = pltpu.make_async_copy(result, hops.at[second - 1], sems.at[NB // CHUNK])
+        store = pltpu.make_async_copy(result, hops.at[second - 1], sems.at[0])
         store.start()
     if not last:
         for slot in range(PARTS * SEND):
@@ -171,15 +188,15 @@
         store.wait()
 
 
-def apply(lists, sends, tiles, field, incoming, degree=None, previous=None, hops=None, hop=0, ids=None, others=()):
+def apply(lists, sends, tiles, field, incoming, degree=None, previous=None, hops=None, hop=0, ids=None, others=(), stage=False):
     second = previous is not None
     last = second and hop == HOPS - 1
     first = hop == 0 and not second
     smem = pl.BlockSpec(memory_space=pltpu.SMEM)
     vmem = pl.BlockSpec(memory_space=pltpu.VMEM)
     hbm = pl.BlockSpec(memory_space=pltpu.HBM)
-    operands = [lists, sends, in_hbm(tiles), field, incoming]
-    in_specs = [smem, smem, hbm, vmem, vmem]
+    operands = [lists, sends, in_hbm(tiles) if stage else in_vmem(tiles), field, incoming]
+    in_specs = [smem, smem, hbm if stage else vmem, vmem, vmem]
     if not first:
         operands.append(degree)
         in_specs.append(vmem)
@@ -212,23 +229,25 @@
     if first:
         out_shape.append(jax.ShapeDtypeStruct((NB, BLK), F32))
         out_specs.append(vmem)
+    if stage:
+        out_shape.append(pltpu.VMEM(tiles.shape, BF))
+        out_specs.append(vmem)
     scratch = [
         pltpu.VMEM((2 * NB, FEATS, BLK), BF),
         pltpu.VMEM((NB, FEATS, BLK), BF),
-        pltpu.VMEM(tiles.shape, BF),
-        pltpu.SemaphoreType.DMA((NB // CHUNK + 1,)),
+        pltpu.SemaphoreType.DMA((NB // UNROLL,)),
     ]
     return pl.pallas_call(
         functools.partial(
             apply_kernel, second=second and hop + 1, first=first, last=last,
-            picking=0 if ids is None else 1 + len(others),
+            picking=0 if ids is None else 1 + len(others), stage=stage,
         ),
         out_shape=out_shape,
         in_specs=in_specs,
         out_specs=out_specs,
         scratch_shapes=scratch,
         input_output_aliases=aliases,
-        compiler_params=params(28),
+        compiler_params=params(8),
         name=f"apply_{'second' if second else 'first'}_{hop}",
     )(*operands)
 
@@ -414,6 +433,10 @@
     result[count:, 0:GROUP, :] = sum_out.astype(BF).reshape(HEADS, GROUP, D)
 
 
+def in_vmem(array):
+    return pltpu.with_memory_space_constraint(array, pltpu.VMEM)
+
+
 def in_hbm(array):
     return pltpu.with_memory_space_constraint(array, pltpu.HBM)
 
@@ -440,7 +463,7 @@
             pltpu.VMEM((NARROW, TOKS * FEATS, QUAD_NODES), BF),
             pltpu.SemaphoreType.DMA((len(weights) + 2,)),
         ],
-        compiler_params=params(58),
+        compiler_params=params(44),
         name="layer",
     )(
         place, in_hbm(early), in_hbm(grads), final, counts, owners,
@@ -458,24 +481,27 @@
 ):
     ids = train_ids.reshape(1, TRAIN)
     grads = lax.all_gather(cotangent.reshape(TOKS * FEATS, TRAIN), NARROW_AXES)
-    named = (owners == jnp.arange(OWNERS, dtype=jnp.int32)[None]).astype(F32)
-    counts = lax.psum(
-        jnp.broadcast_to(jnp.sum(named, axis=0)[:, None], (OWNERS, OWNERS)), WIDE
-    )
-    incoming = exchange(pack(send_lists, features), WIDE)
+    owner_row = owners.reshape(1, TRAIN)
+    outgoing, counts = pack(send_lists, features, owner_row)
+    counts = lax.psum(counts, WIDE)
+    incoming = exchange(outgoing, WIDE)
     incoming, up_t, out_t = lax.optimization_barrier((incoming, up_weight.T, out_weight.T))
-    step = functools.partial(apply, block_lists, send_lists, edge_tiles)
+    step = functools.partial(apply, block_lists, send_lists)
     current = features
     hops = None
     fields = [features]
     for hop in range(HOPS):
         if hop == 0:
-            once, outgoing, degree = step(current, incoming)
+            once, outgoing, degree, tiles = step(edge_tiles, current, incoming, stage=True)
+        elif hop == HOPS - 1:
+            once, outgoing, tiles = step(
+                edge_tiles, current, incoming, degree, hop=hop, stage=True
+            )
         else:
-            once, outgoing = step(current, incoming, degree, hop=hop)
+            once, outgoing = step(tiles, current, incoming, degree, hop=hop)
         incoming = exchange(outgoing, WIDE)
         results = step(
-            once, incoming, degree, previous=current, hops=hops, hop=hop,
+            tiles, once, incoming, degree, previous=current, hops=hops, hop=hop,
             ids=None if hop == 0 else ids,
             others=tuple(fields) if hop == HOPS - 2 else (),
         )
@@ -491,7 +517,7 @@
         [2 * lax.axis_index("xl") + lax.axis_index("c"), lax.axis_index("xh")]
     ).astype(jnp.int32)
     partial = layer(
-        place, early, grads, final, counts, owners.reshape(1, TRAIN),
+        place, early, grads, final, counts, owner_row,
         query_weight, key_weight, value_weight, out_weight, out_t, up_weight, up_t, down_weight,
     )
     gathered = exchange(partial, QUADS)

time: 221 us -> 210 us (0.950)
  Pallas kernels: 72.7 us -> 64.2 us
    pallas_call x6, Pallas kernels: 42.2 us -> 37.1 us  [apply(): pl.pallas_call(functools.partial(apply_kernel, second=second and hop + 1,...]
    pallas_call x1, Pallas kernels: 27.8 us -> 24.3 us  [layer(): pl.pallas_call(layer_kernel, out_shape=jax.ShapeDtypeStruct((DESTS, 3 * G...]
    unnamed x14 -> x18, local copies, waits for them, and re-layouts: 6.13 us -> 7.45 us
  transfers between devices with their start and end apart: 5 -> 5, of which waited for: 2 -> 2; matrix products, arithmetic and copies ran while one was open for 3% -> 2% of each run, Pallas kernels for 20% -> 18%
where the time goes in v4:
time: 210 us
  blocking collectives  94.2 us (45%)
  Pallas kernels  64.2 us (31%)
  between operations  15.6 us (7%)
  waiting for transfers between devices  14.4 us (7%)
  starting transfers between devices  12.8 us (6%)
  local copies, waits for them, and re-layouts  8.09 us (4%)
    all_to_all x6, blocking collectives, exchange(): return lax.all_to_all(array, axes, split_axis=0, concat_axis=0, tiled=True)  94.2 us
    pallas_call x6, Pallas kernels, apply(): pl.pallas_call(functools.partial(apply_kernel, second=second and hop + 1,...  37.1 us
    pallas_call x1, Pallas kernels, layer(): pl.pallas_call(layer_kernel, out_shape=jax.ShapeDtypeStruct((DESTS, 3 * G...  24.3 us
    all_to_all x2, waiting for transfers between devices, exchange(): return lax.all_to_all(array, axes, split_axis=0, concat_axis=0, tiled=True)  13.9 us
    all_to_all x2, starting transfers between devices, exchange(): return lax.all_to_all(array, axes, split_axis=0, concat_axis=0, tiled=True)  12.7 us
    unnamed x18, local copies, waits for them, and re-layouts  7.45 us
  transfers between devices with their start and end apart: 5, of which 2 were waited for; matrix products, arithmetic and copies ran while one was open for 2% of the time, Pallas kernels for 18%

profile of v4, /device:TPU:0, one launch (start us, length us, event | category | flops | bytes accessed | tf_op | source)
XLA Modules:
  0.0 209.6 jit_solution(7797738869327569917)
XLA Ops:
  8.0 0.0 all-reduce.2.cloned.1.call-start
  8.0 0.8 copy.50.sends.refs_1_.refs_7_
  8.8 0.0 copy-start.2
  8.8 0.7 copy-done.2
  9.5 2.9 %pack.1 = (bf16[16,128,128]{2,1,0:T(8,128)(2,1)}, f32[128,128]{1,0:T(8,128)}) custom-call(s32[1,16,2]{2,1,0:T(8,128)S(1)} %copy.50.sends.refs_1_.refs_7_, bf16[64,4096]{1,0:T(8,128)(2,1)} %refs_9_.1, s32[1,512]{1,0:T(1,128)S(1)} %bitcast.8), custom_call_target="tpu_custom_call" | custom-call | tf_op jit(solution)/shard_map/pack/pallas_call | solution.py:77
  12.3 0.0 all-reduce.2.cloned.1.call-update
  12.4 0.0 all-gather.4.cloned.1.call-start
  12.4 0.5 all-gather.4.cloned.1.call-update
  12.9 8.2 %all-to-all-start = ((bf16[16,128,128]{2,1,0:T(8,128)(2,1)}), bf16[16,128,128]{2,1,0:T(8,128)(2,1)S(1)}, u32[]{:S(2)}, u32[]{:S(2)}) async-start(bf16[16,128,128]{2,1,0:T(8,128)(2,1)} %get-tuple-element.27), calls=%async_computation | async-start | bytes 1048576 | tf_op jit(solution)/shard_map/all_to_all | solution.py:475
  21.1 0.0 copy-start.5
  21.1 0.0 copy-start.6
  21.1 0.0 copy-start
  21.2 0.0 all-gather.6.cloned.1.call-start
  21.2 4.1 %copy.36 = bf16[2048,512]{0,1:T(8,128)(2,1)} copy(bf16[2048,512]{1,0:T(8,128)(2,1)} %up_h.1) | data formatting | bytes 4194304 | tf_op args[11]
  25.3 0.0 copy-done.5
  25.3 1.0 copy.37
  26.3 0.0 copy-done.6
  26.3 0.1 copy.49.refs_0_
  26.4 6.4 %all-to-all-done.refs_4_ = bf16[16,128,128]{2,1,0:T(8,128)(2,1)S(1)} async-done(((bf16[16,128,128]{2,1,0:T(8,128)(2,1)}), bf16[16,128,128]{2,1,0:T(8,128)(2,1)S(1)}, u32[]{:S(2)}, u32[]{:S(2)}) %all-to-all-start) | async-done | bytes 524320 | tf_op jit(solution)/shard_map/all_to_all | solution.py:475
  32.8 0.0 copy-done
  32.8 6.7 %apply_first_0.1 = (bf16[64,4096]{1,0:T(8,128)(2,1)S(1)}, bf16[16,128,128]{2,1,0:T(8,128)(2,1)S(1)}, f32[32,128]{1,0:T(8,128)S(1)}, bf16[32,12,128,128]{3,2,1,0:T(8,128)(2,1)S(1)}) custom-call(s32[32,12]{1,0:T(8,128)S(1)} %copy.49.refs_0_, s32[1,16,2]{2,1,0:T(8,128)S(1)} %copy.50.sends.refs_1_.refs_7_, bf16[32,12,128,128]{3,2,1,0:T(8,128)(2,1)} %refs_2_.3, ...), custom_call_target="tpu_custom_call" | custom-call | tf_op jit(solution)/shard_map/apply_first_0/pallas_call | solution.py:240
  39.5 13.7 %all_to_all.40.refs_4_ = bf16[16,128,128]{2,1,0:T(8,128)(2,1)S(1)} all-to-all(bf16[16,128,128]{2,1,0:T(8,128)(2,1)S(1)} %get-tuple-element.31), channel_id=1, replica_groups=mesh['z'=4,'y'=4,'xh'=2,'xl'=2,'c'=2] {'z','y'}, dimensions={0} | all-to-all | bytes 1048576 | tf_op jit(solution)/shard_map/all_to_all | solution.py:475
  53.2 5.0 %apply_second_0.1 = (bf16[64,4096]{1,0:T(8,128)(2,1)S(1)}, bf16[3,64,4096]{2,1,0:T(8,128)(2,1)}, bf16[16,128,128]{2,1,0:T(8,128)(2,1)S(1)}) custom-call(s32[32,12]{1,0:T(8,128)S(1)} %copy.49.refs_0_, s32[1,16,2]{2,1,0:T(8,128)S(1)} %copy.50.sends.refs_1_.refs_7_, bf16[32,12,128,128]{3,2,1,0:T(8,128)(2,1)S(1)} %get-tuple-element.29.refs_2_, ...), custom_call_target="tpu_custom_call" | custom-call | tf_op jit(solution)/shard_map/apply_second_0/pallas_call | solution.py:240
  58.2 13.2 %all_to_all.41.refs_4_ = bf16[16,128,128]{2,1,0:T(8,128)(2,1)S(1)} all-to-all(bf16[16,128,128]{2,1,0:T(8,128)(2,1)S(1)} %get-tuple-element.34), channel_id=1, replica_groups=mesh['z'=4,'y'=4,'xh'=2,'xl'=2,'c'=2] {'z','y'}, dimensions={0} | all-to-all | bytes 1048576 | tf_op jit(solution)/shard_map/all_to_all | solution.py:475
  71.4 0.0 copy-start.4
  71.4 4.1 %apply_first_1.1 = (bf16[64,4096]{1,0:T(8,128)(2,1)S(1)}, bf16[16,128,128]{2,1,0:T(8,128)(2,1)S(1)}) custom-call(s32[32,12]{1,0:T(8,128)S(1)} %copy.49.refs_0_, s32[1,16,2]{2,1,0:T(8,128)S(1)} %copy.50.sends.refs_1_.refs_7_, bf16[32,12,128,128]{3,2,1,0:T(8,128)(2,1)S(1)} %get-tuple-element.29.refs_2_, ...), custom_call_target="tpu_custom_call" | custom-call | tf_op jit(solution)/shard_map/apply_first_1/pallas_call | solution.py:240
  75.5 13.1 %all_to_all.42.refs_4_ = bf16[16,128,128]{2,1,0:T(8,128)(2,1)S(1)} all-to-all(bf16[16,128,128]{2,1,0:T(8,128)(2,1)S(1)} %get-tuple-element.36), channel_id=1, replica_groups=mesh['z'=4,'y'=4,'xh'=2,'xl'=2,'c'=2] {'z','y'}, dimensions={0} | all-to-all | bytes 1048576 | tf_op jit(solution)/shard_map/all_to_all | solution.py:475
  88.6 0.0 copy-done.4
  88.6 7.9 %apply_second_1.1 = (bf16[64,4096]{1,0:T(8,128)(2,1)S(1)}, bf16[3,64,4096]{2,1,0:T(8,128)(2,1)}, bf16[16,128,128]{2,1,0:T(8,128)(2,1)S(1)}, bf16[192,512]{1,0:T(8,128)(2,1)}) custom-call(s32[32,12]{1,0:T(8,128)S(1)} %copy.49.refs_0_, s32[1,16,2]{2,1,0:T(8,128)S(1)} %copy.50.sends.refs_1_.refs_7_, ...), custom_call_target="tpu_custom_call", output_to_operand_aliasing={{1}: (7, {})} | custom-call | tf_op jit(solution)/shard_map/apply_second_1/pallas_call | solution.py:240
  96.5 0.0 all-gather.6.cloned.1.call-update
  96.6 13.1 %all_to_all.43.refs_4_ = bf16[16,128,128]{2,1,0:T(8,128)(2,1)S(1)} all-to-all(bf16[16,128,128]{2,1,0:T(8,128)(2,1)S(1)} %get-tuple-element.39), channel_id=1, replica_groups=mesh['z'=4,'y'=4,'xh'=2,'xl'=2,'c'=2] {'z','y'}, dimensions={0} | all-to-all | bytes 1048576 | tf_op jit(solution)/shard_map/all_to_all | solution.py:475
  109.6 6.5 %apply_first_2.1 = (bf16[64,4096]{1,0:T(8,128)(2,1)S(1)}, bf16[16,128,128]{2,1,0:T(8,128)(2,1)S(1)}, bf16[32,12,128,128]{3,2,1,0:T(8,128)(2,1)S(1)}) custom-call(s32[32,12]{1,0:T(8,128)S(1)} %copy.49.refs_0_, s32[1,16,2]{2,1,0:T(8,128)S(1)} %copy.50.sends.refs_1_.refs_7_, bf16[32,12,128,128]{3,2,1,0:T(8,128)(2,1)} %refs_2_.3, ...), custom_call_target="tpu_custom_call" | custom-call | tf_op jit(solution)/shard_map/apply_first_2/pallas_call | solution.py:240
  116.2 13.1 %all_to_all.44.refs_4_ = bf16[16,128,128]{2,1,0:T(8,128)(2,1)S(1)} all-to-all(bf16[16,128,128]{2,1,0:T(8,128)(2,1)S(1)} %get-tuple-element.42), channel_id=1, replica_groups=mesh['z'=4,'y'=4,'xh'=2,'xl'=2,'c'=2] {'z','y'}, dimensions={0} | all-to-all | bytes 1048576 | tf_op jit(solution)/shard_map/all_to_all | solution.py:475
  129.3 0.0 copy-start.3
  129.3 6.8 %apply_second_2.1 = (bf16[64,4096]{1,0:T(8,128)(2,1)}, bf16[3,64,4096]{2,1,0:T(8,128)(2,1)}, bf16[8,64,256]{2,1,0:T(8,128)(2,1)}) custom-call(s32[32,12]{1,0:T(8,128)S(1)} %copy.49.refs_0_, s32[1,16,2]{2,1,0:T(8,128)S(1)} %copy.50.sends.refs_1_.refs_7_, bf16[32,12,128,128]{3,2,1,0:T(8,128)(2,1)S(1)} %get-tuple-element.40.refs_2_, ...), custom_call_target="tpu_custom_call", output_to_operand_aliasing={{1}: (7, {})} | custom-call | tf_op jit(solution)/shard_map/apply_second_2/pallas_call | solution.py:240
  136.1 4.5 %all-to-all-start.6 = ((bf16[8,64,256]{2,1,0:T(8,128)(2,1)}), bf16[8,64,256]{2,1,0:T(8,128)(2,1)S(1)}, u32[]{:S(2)}, u32[]{:S(2)}) async-start(bf16[8,64,256]{2,1,0:T(8,128)(2,1)} %get-tuple-element.46), calls=%async_computation.6 | async-start | bytes 524288 | tf_op jit(solution)/shard_map/all_to_all | solution.py:475
  140.6 0.1 pad_add_fusion.place
  140.7 0.0 all-reduce.2.cloned.1.call-done.counts
  140.7 7.5 %all-to-all-done.6.final = bf16[8,64,256]{2,1,0:T(8,128)(2,1)S(1)} async-done(((bf16[8,64,256]{2,1,0:T(8,128)(2,1)}), bf16[8,64,256]{2,1,0:T(8,128)(2,1)S(1)}, u32[]{:S(2)}, u32[]{:S(2)}) %all-to-all-start.6) | async-done | bytes 262176 | tf_op jit(solution)/shard_map/all_to_all | solution.py:475
  148.1 0.0 all-gather.4.cloned.1.call-done.grads_h
  148.1 0.0 all-gather.6.cloned.1.call-done
  148.1 0.0 copy-done.3
  148.1 0.0 copy-start.1
  148.1 0.8 copy-done.1
  149.0 24.3 %layer.1 = bf16[32,48,512]{2,1,0:T(8,128)(2,1)S(1)} custom-call(s32[2]{0:T(128)S(1)} %pad_add_fusion.place, bf16[8,192,512]{2,1,0:T(8,128)(2,1)} %bitcast.14, bf16[8,256,512]{2,1,0:T(8,128)(2,1)} %all-gather.4.cloned.1.call-done.grads_h, bf16[8,64,256]{2,1,0:T(8,128)(2,1)S(1)} %all-to-all-done.6.final, f32[128,128]{1,0:T(8,128)S(1)} %copy-done.1, ...), custom_call_target="tpu_custom_call" | custom-call | tf_op jit(solution)/shard_map/layer/pallas_call | solution.py:452
  173.3 28.1 %all_to_all.45 = bf16[32,48,512]{2,1,0:T(8,128)(2,1)S(1)} all-to-all(bf16[32,48,512]{2,1,0:T(8,128)(2,1)S(1)} %layer.1), channel_id=1, replica_groups=mesh['z'=4,'y'=4,'xh'=2,'xl'=2,'c'=2] {'z','y','xh'}, dimensions={0} | all-to-all | bytes 3145728 | tf_op jit(solution)/shard_map/all_to_all | solution.py:475
  201.3 0.2 convert_reduce_fusion
  201.6 0.6 fusion
Async XLA Ops:
  8.0 132.7 %all-reduce.2.cloned.1.call-start = ((), (), s32[]{:S(2)}) async-start(), calls=%async_computation.9 | async-start | bytes 131072 | tf_op jit(solution)/shard_map/psum | solution.py:486
  8.8 0.7 copy-start.2
  12.4 135.8 %all-gather.4.cloned.1.call-start = ((), (), s32[]{:S(2)}) async-start(), calls=%async_computation.8 | async-start | bytes 2359296 | tf_op jit(solution)/shard_map/all_gather | solution.py:483
  12.9 19.8 %all-to-all-start = ((bf16[16,128,128]{2,1,0:T(8,128)(2,1)}), bf16[16,128,128]{2,1,0:T(8,128)(2,1)S(1)}, u32[]{:S(2)}, u32[]{:S(2)}) async-start(bf16[16,128,128]{2,1,0:T(8,128)(2,1)} %get-tuple-element.27), calls=%async_computation | async-start | bytes 1048576 | tf_op jit(solution)/shard_map/all_to_all | solution.py:475
  21.1 4.1 %copy-start.5 = (bf16[512,512]{1,0:T(8,128)(2,1)S(1)}, bf16[512,512]{1,0:T(8,128)(2,1)}, u32[]{:S(2)}) copy-start(bf16[512,512]{1,0:T(8,128)(2,1)} %out_h.1) | copy-start | bytes 1572868
  21.1 5.1 %copy-start.6 = (s32[32,12]{0,1:T(8,128)S(1)}, s32[32,12]{0,1:T(8,128)}, u32[]{:S(2)}) copy-start(s32[32,12]{0,1:T(8,128)} %param.15) | copy-start | bytes 4612
  21.1 11.6 %copy-start = (bf16[64,4096]{1,0:T(8,128)(2,1)S(1)}, bf16[64,4096]{1,0:T(8,128)(2,1)}, u32[]{:S(2)}) copy-start(bf16[64,4096]{1,0:T(8,128)(2,1)} %refs_9_.1) | copy-start | bytes 1572868
  21.2 127.0 %all-gather.6.cloned.1.call-start = ((), (), s32[]{:S(2)}) async-start(), calls=%async_computation.10 | async-start | bytes 1769472 | tf_op jit(solution)/shard_map/all_gather | solution.py:511
  71.4 17.2 %copy-start.4 = (s32[512]{0:T(512)S(1)}, s32[512]{0:T(512)}, u32[]{:S(2)}) copy-start(s32[512]{0:T(512)} %param.17) | copy-start | bytes 6148
  129.3 18.9 %copy-start.3 = (s32[512,1]{0,1:T(1,128)S(1)}, s32[512,1]{0,1:T(1,128)}, u32[]{:S(2)}) copy-start(s32[512,1]{0,1:T(1,128)} %param.18) | copy-start | bytes 6148
  136.1 12.0 %all-to-all-start.6 = ((bf16[8,64,256]{2,1,0:T(8,128)(2,1)}), bf16[8,64,256]{2,1,0:T(8,128)(2,1)S(1)}, u32[]{:S(2)}, u32[]{:S(2)}) async-start(bf16[8,64,256]{2,1,0:T(8,128)(2,1)} %get-tuple-element.46), calls=%async_computation.6 | async-start | bytes 524288 | tf_op jit(solution)/shard_map/all_to_all | solution.py:475
  148.1 0.8 copy-start.1
Sparse Core Ops, SparseCore 0:
  12.5 85.4 all-reduce.1
Sparse Core Ops, SparseCore 1:
  14.6 27.7 all-gather.3
  96.6 21.9 all-gather.5

commit v5 on v4

--- a/solution.py
+++ b/solution.py
@@ -28,7 +28,9 @@
 NARROW = 8
 DESTS = 32
 GROUP = 16
-UNROLL = 8
+UNROLL = 16
+CHUNK = 4
+IN_FLIGHT = 3
 PICK_BLOCKS = 4
 FF_CHUNK = 512
 EPSILON = 1e-05
@@ -52,7 +54,13 @@
     return lax.dot_general(left, right, (((1,), (1,)), ((), ())), preferred_element_type=F32)
 
 
-def pack_kernel(sends, field, owners, outgoing, counts, sems):
+def block_columns(b):
+    return pl.ds(b * BLK if isinstance(b, int) else pl.multiple_of(b * BLK, BLK), BLK)
+
+
+def pack_kernel(sends, field, owners_h, outgoing, counts, owners, sems):
+    names = pltpu.make_async_copy(owners_h, owners, sems.at[PARTS * SEND])
+    names.start()
     copies = []
     for slot in range(PARTS * SEND):
         start = pl.multiple_of(sends[0, slot // SEND, slot % SEND] * BLK, BLK)
@@ -66,6 +74,7 @@
         )
     for copy in copies:
         copy.start()
+    names.wait()
     named = lax.broadcasted_iota(jnp.int32, (OWNERS, TRAIN), 0) == owners[...]
     count = jnp.sum(jnp.where(named, 1.0, 0.0), axis=1, keepdims=True)
     counts[...] = jnp.broadcast_to(count, (OWNERS, OWNERS))
@@ -83,29 +92,28 @@
         in_specs=[
             pl.BlockSpec(memory_space=pltpu.SMEM),
             pl.BlockSpec(memory_space=pltpu.HBM),
-            pl.BlockSpec(memory_space=pltpu.VMEM),
+            pl.BlockSpec(memory_space=pltpu.HBM),
         ],
-        scratch_shapes=[pltpu.SemaphoreType.DMA((PARTS * SEND,))],
+        scratch_shapes=[
+            pltpu.VMEM((1, TRAIN), jnp.int32),
+            pltpu.SemaphoreType.DMA((PARTS * SEND + 1,)),
+        ],
         compiler_params=params(4),
         name="pack",
-    )(sends, in_hbm(field), owners)
+    )(sends, in_hbm(field), in_hbm(owners))
 
 
 def picked_columns(ids, fields):
     id_row = ids[...]
-
-    def add_blocks(i, total):
-        for j in range(PICK_BLOCKS):
-            b = i * PICK_BLOCKS + j
-            rows = lax.broadcasted_iota(jnp.int32, (BLK, TRAIN), 0) + b * BLK
-            chosen = jnp.where(rows == id_row, 1.0, 0.0).astype(BF)
-            cols = pl.ds(pl.multiple_of(b * BLK, BLK), BLK)
-            block = jnp.concatenate([field[:, cols] for field in fields], axis=0)
-            total = total + dot(block, chosen)
-        return total
-
-    start = jnp.zeros((FEATS * len(fields), TRAIN), F32)
-    return lax.fori_loop(0, NB // PICK_BLOCKS, add_blocks, start).astype(BF)
+    span = PICK_BLOCKS * BLK
+    total = None
+    for start in range(0, NODES, span):
+        rows = lax.broadcasted_iota(jnp.int32, (span, TRAIN), 0) + start
+        chosen = jnp.where(rows == id_row, 1.0, 0.0).astype(BF)
+        block = jnp.concatenate([field[:, start : start + span] for field in fields], axis=0)
+        term = dot(block, chosen)
+        total = term if total is None else total + term
+    return total.astype(BF)
 
 
 def apply_kernel(*refs, second, first, last, picking, stage):
@@ -126,11 +134,17 @@
     pool, fresh, sems = refs
 
     def load(i):
-        blocks = pl.ds(i * UNROLL, UNROLL)
+        blocks = pl.ds(i * CHUNK, CHUNK)
         return pltpu.make_async_copy(tiles_h.at[blocks], tiles.at[blocks], sems.at[i])
 
+    def store(i):
+        cols = pl.ds(pl.multiple_of(i * UNROLL * BLK, UNROLL * BLK), UNROLL * BLK)
+        return pltpu.make_async_copy(
+            result.at[:, cols], hops.at[second - 1, :, cols], sems.at[i]
+        )
+
     if stage:
-        for i in range(NB // UNROLL):
+        for i in range(IN_FLIGHT):
             load(i).start()
 
     for j in range(NB):
@@ -151,7 +165,7 @@
         else:
             share = degree[pl.ds(b, 1), :]
         value = (summed / share).astype(BF)
-        cols = pl.ds(pl.multiple_of(b * BLK, BLK), BLK)
+        cols = block_columns(b)
         if second:
             value = (
                 0.5 * previous[:, cols].astype(F32) + pool[b].astype(F32) + value.astype(F32)
@@ -160,16 +174,21 @@
         fresh[b] = value
 
     def some_blocks(i, carry):
-        if stage:
-            load(i).wait()
         for j in range(UNROLL):
             one_block(i * UNROLL + j)
+        if second:
+            store(i).start()
         return carry
 
-    lax.fori_loop(0, NB // UNROLL, some_blocks, 0)
-    if second:
-        store = pltpu.make_async_copy(result, hops.at[second - 1], sems.at[0])
-        store.start()
+    if stage:
+        for i in range(NB // CHUNK):
+            load(i).wait()
+            if i + IN_FLIGHT < NB // CHUNK:
+                load(i + IN_FLIGHT).start()
+            for j in range(CHUNK):
+                one_block(i * CHUNK + j)
+    else:
+        lax.fori_loop(0, NB // UNROLL, some_blocks, 0)
     if not last:
         for slot in range(PARTS * SEND):
             rows = (slot % SEND) * FEATS
@@ -185,7 +204,8 @@
         else:
             rows_out[...] = picked
     if second:
-        store.wait()
+        for i in range(NB // UNROLL):
+            store(i).wait()
 
 
 def apply(lists, sends, tiles, field, incoming, degree=None, previous=None, hops=None, hop=0, ids=None, others=(), stage=False):
@@ -235,7 +255,7 @@
     scratch = [
         pltpu.VMEM((2 * NB, FEATS, BLK), BF),
         pltpu.VMEM((NB, FEATS, BLK), BF),
-        pltpu.SemaphoreType.DMA((NB // UNROLL,)),
+        pltpu.SemaphoreType.DMA((NB // CHUNK,)),
     ]
     return pl.pallas_call(
         functools.partial(
@@ -253,10 +273,10 @@
 
 
 def layer_kernel(
-    place, early_h, grads_h, final, counts, owners,
+    place, early_h, grads_h, final, counts_h, owners_h,
     query_h, key_h, value_h, out_h, out_th, up_h, up_th, down_h,
     result, query_s, key_s, value_s, mixed_s, probs_s, act_s, pre_s, gmix_s, gq_s, gk_s, gv_s, gr_s,
-    query_w, key_w, value_w, out_w, out_t, up_w, up_t, down_w, early, grads, sems,
+    query_w, key_w, value_w, out_w, out_t, up_w, up_t, down_w, early, grads, counts, owners, sems,
 ):
     own = place[0]
     mine = pl.ds(pl.multiple_of(place[1] * QUAD_NODES, QUAD_NODES), QUAD_NODES)
@@ -264,12 +284,13 @@
         (query_h, query_w), (key_h, key_w), (value_h, value_w), (out_h, out_w),
         (up_h, up_w), (down_h, down_w), (up_th, up_t), (out_th, out_t),
         (early_h.at[:, :, mine], early), (grads_h.at[:, :, mine], grads),
+        (counts_h, counts), (owners_h, owners),
     )
     loads = [
         pltpu.make_async_copy(source, target, sems.at[index])
         for index, (source, target) in enumerate(pairs)
     ]
-    for index in (8, 0, 1, 2, 9, 3, 4, 5, 6, 7):
+    for index in (8, 0, 1, 2, 10, 11, 9, 3, 4, 5, 6, 7):
         loads[index].start()
     width = TOKS * QUAD_NODES
     loads[8].wait()
@@ -336,6 +357,8 @@
     groups = FF_CHUNK // (QUAD * GROUP)
 
     loads[9].wait()
+    loads[10].wait()
+    loads[11].wait()
     named = lax.broadcasted_iota(jnp.int32, (OWNERS, QUAD_NODES), 0) == owners[:, mine]
     by_owner = jnp.concatenate([1.0 / counts[...]] * (QUAD_NODES // OWNERS), axis=1)
     row_scale = jnp.sum(jnp.where(named, by_owner, 0.0), axis=0, keepdims=True)
@@ -452,7 +475,7 @@
     return pl.pallas_call(
         layer_kernel,
         out_shape=jax.ShapeDtypeStruct((DESTS, 3 * GROUP, D), BF),
-        in_specs=[smem, hbm, hbm, vmem, vmem, vmem] + [hbm] * 8,
+        in_specs=[smem, hbm, hbm, vmem, hbm, hbm] + [hbm] * 8,
         out_specs=vmem,
         scratch_shapes=[
             square, square, square, square,
@@ -461,14 +484,31 @@
             *[pltpu.VMEM(w.shape, BF) for w in weights],
             pltpu.VMEM((NARROW, HOPS * FEATS, QUAD_NODES), BF),
             pltpu.VMEM((NARROW, TOKS * FEATS, QUAD_NODES), BF),
-            pltpu.SemaphoreType.DMA((len(weights) + 2,)),
+            pltpu.VMEM((OWNERS, OWNERS), F32),
+            pltpu.VMEM((1, TRAIN), jnp.int32),
+            pltpu.SemaphoreType.DMA((len(weights) + 4,)),
         ],
         compiler_params=params(44),
         name="layer",
     )(
-        place, in_hbm(early), in_hbm(grads), final, counts, owners,
+        place, in_hbm(early), in_hbm(grads), final, in_hbm(counts), in_hbm(owners),
         *[in_hbm(w) for w in weights],
     )
+
+
+def sum_kernel(gathered, *outs):
+    total = jnp.sum(gathered[...].astype(F32), axis=0)
+    for index, out in enumerate(outs):
+        out[...] = total[index * GROUP : (index + 1) * GROUP]
+
+
+def sum_parts(gathered):
+    return pl.pallas_call(
+        sum_kernel,
+        out_shape=[jax.ShapeDtypeStruct((GROUP, D), F32)] * 3,
+        compiler_params=params(8),
+        name="sum_parts",
+    )(gathered)
 
 
 def exchange(array, axes):
@@ -521,8 +561,7 @@
         query_weight, key_weight, value_weight, out_weight, out_t, up_weight, up_t, down_weight,
     )
     gathered = exchange(partial, QUADS)
-    sums = jnp.sum(gathered.astype(F32), axis=0)
-    return (hops, sums[:GROUP], sums[GROUP : 2 * GROUP], sums[2 * GROUP :])
+    return (hops, *sum_parts(gathered))
 
 
 def solution(mesh):

time: 210 us -> 205 us (0.976)
  Pallas kernels: 64.2 us -> 61.3 us
  local copies, waits for them, and re-layouts: 8.09 us -> 5.93 us
    pallas_call x6, Pallas kernels: 37.1 us -> 33.3 us  [apply(): pl.pallas_call(functools.partial(apply_kernel, second=second and hop + 1,...]
    unnamed x18 -> x12, local copies, waits for them, and re-layouts: 7.45 us -> 5.93 us
  transfers between devices with their start and end apart: 5 -> 5, of which waited for: 2 -> 2; matrix products, arithmetic and copies ran while one was open for 2% -> 3% of each run, Pallas kernels for 18% -> 16%
where the time goes in v5:
time: 205 us; the launch traced here: 204 us
  blocking collectives  94.3 us (46%)
  Pallas kernels  61.3 us (30%)
  between operations  15.6 us (8%)
  waiting for transfers between devices  14.4 us (7%)
  starting transfers between devices  12.7 us (6%)
  local copies, waits for them, and re-layouts  5.93 us (3%)
    all_to_all x6, blocking collectives, exchange(): return lax.all_to_all(array, axes, split_axis=0, concat_axis=0, tiled=True)  94.3 us
    pallas_call x6, Pallas kernels, apply(): pl.pallas_call(functools.partial(apply_kernel, second=second and hop + 1,...  33.3 us
    pallas_call x1, Pallas kernels, layer(): pl.pallas_call(layer_kernel, out_shape=jax.ShapeDtypeStruct((DESTS, 3 * G...  24.3 us
    all_to_all x2, waiting for transfers between devices, exchange(): return lax.all_to_all(array, axes, split_axis=0, concat_axis=0, tiled=True)  13.9 us
    all_to_all x2, starting transfers between devices, exchange(): return lax.all_to_all(array, axes, split_axis=0, concat_axis=0, tiled=True)  12.6 us
    unnamed x12, local copies, waits for them, and re-layouts  5.93 us
  transfers between devices with their start and end apart: 5, of which 2 were waited for; matrix products, arithmetic and copies ran while one was open for 3% of the time, Pallas kernels for 16%

profile of v5, /device:TPU:0, one launch (start us, length us, event | category | flops | bytes accessed | tf_op | source)
XLA Modules:
  0.0 204.3 jit_solution(8238220361659760856)
XLA Ops:
  8.0 0.0 all-reduce.2.cloned.1.call-start
  8.0 0.8 copy.50.sends.refs_1_.refs_7_
  8.8 2.9 %pack.1 = (bf16[16,128,128]{2,1,0:T(8,128)(2,1)}, f32[128,128]{1,0:T(8,128)}) custom-call(s32[1,16,2]{2,1,0:T(8,128)S(1)} %copy.50.sends.refs_1_.refs_7_, bf16[64,4096]{1,0:T(8,128)(2,1)} %refs_9_.1, s32[1,512]{1,0:T(1,128)} %bitcast.14), custom_call_target="tpu_custom_call" | custom-call | tf_op jit(solution)/shard_map/pack/pallas_call | solution.py:86
  11.7 0.0 all-reduce.2.cloned.1.call-update
  11.7 0.0 all-gather.4.cloned.1.call-start
  11.8 0.5 all-gather.4.cloned.1.call-update
  12.3 8.0 %all-to-all-start = ((bf16[16,128,128]{2,1,0:T(8,128)(2,1)}), bf16[16,128,128]{2,1,0:T(8,128)(2,1)S(1)}, u32[]{:S(2)}, u32[]{:S(2)}) async-start(bf16[16,128,128]{2,1,0:T(8,128)(2,1)} %get-tuple-element.30), calls=%async_computation | async-start | bytes 1048576 | tf_op jit(solution)/shard_map/all_to_all | solution.py:515
  20.4 0.0 copy-start.2
  20.4 0.0 copy-start.3
  20.4 0.0 copy-start
  20.4 0.0 all-gather.6.cloned.1.call-start
  20.4 4.1 %copy.36 = bf16[2048,512]{0,1:T(8,128)(2,1)} copy(bf16[2048,512]{1,0:T(8,128)(2,1)} %up_h.1) | data formatting | bytes 4194304 | tf_op args[11]
  24.5 0.0 copy-done.2
  24.5 1.0 copy.37
  25.5 0.0 copy-done.3
  25.5 0.1 copy.49.refs_0_
  25.6 6.4 %all-to-all-done.refs_4_ = bf16[16,128,128]{2,1,0:T(8,128)(2,1)S(1)} async-done(((bf16[16,128,128]{2,1,0:T(8,128)(2,1)}), bf16[16,128,128]{2,1,0:T(8,128)(2,1)S(1)}, u32[]{:S(2)}, u32[]{:S(2)}) %all-to-all-start) | async-done | bytes 524320 | tf_op jit(solution)/shard_map/all_to_all | solution.py:515
  32.0 0.0 copy-done
  32.0 6.8 %apply_first_0.1 = (bf16[64,4096]{1,0:T(8,128)(2,1)S(1)}, bf16[16,128,128]{2,1,0:T(8,128)(2,1)S(1)}, f32[32,128]{1,0:T(8,128)S(1)}, bf16[32,12,128,128]{3,2,1,0:T(8,128)(2,1)S(1)}) custom-call(s32[32,12]{1,0:T(8,128)S(1)} %copy.49.refs_0_, s32[1,16,2]{2,1,0:T(8,128)S(1)} %copy.50.sends.refs_1_.refs_7_, bf16[32,12,128,128]{3,2,1,0:T(8,128)(2,1)} %refs_2_.3, ...), custom_call_target="tpu_custom_call" | custom-call | tf_op jit(solution)/shard_map/apply_first_0/pallas_call | solution.py:260
  38.8 13.7 %all_to_all.40.refs_4_ = bf16[16,128,128]{2,1,0:T(8,128)(2,1)S(1)} all-to-all(bf16[16,128,128]{2,1,0:T(8,128)(2,1)S(1)} %get-tuple-element.34), channel_id=1, replica_groups=mesh['z'=4,'y'=4,'xh'=2,'xl'=2,'c'=2] {'z','y'}, dimensions={0} | all-to-all | bytes 1048576 | tf_op jit(solution)/shard_map/all_to_all | solution.py:515
  52.5 4.7 %apply_second_0.1 = (bf16[64,4096]{1,0:T(8,128)(2,1)S(1)}, bf16[3,64,4096]{2,1,0:T(8,128)(2,1)}, bf16[16,128,128]{2,1,0:T(8,128)(2,1)S(1)}) custom-call(s32[32,12]{1,0:T(8,128)S(1)} %copy.49.refs_0_, s32[1,16,2]{2,1,0:T(8,128)S(1)} %copy.50.sends.refs_1_.refs_7_, bf16[32,12,128,128]{3,2,1,0:T(8,128)(2,1)S(1)} %get-tuple-element.32.refs_2_, ...), custom_call_target="tpu_custom_call" | custom-call | tf_op jit(solution)/shard_map/apply_second_0/pallas_call | solution.py:260
  57.2 13.2 %all_to_all.41.refs_4_ = bf16[16,128,128]{2,1,0:T(8,128)(2,1)S(1)} all-to-all(bf16[16,128,128]{2,1,0:T(8,128)(2,1)S(1)} %get-tuple-element.37), channel_id=1, replica_groups=mesh['z'=4,'y'=4,'xh'=2,'xl'=2,'c'=2] {'z','y'}, dimensions={0} | all-to-all | bytes 1048576 | tf_op jit(solution)/shard_map/all_to_all | solution.py:515
  70.4 0.0 copy-start.1
  70.4 3.9 %apply_first_1.1 = (bf16[64,4096]{1,0:T(8,128)(2,1)S(1)}, bf16[16,128,128]{2,1,0:T(8,128)(2,1)S(1)}) custom-call(s32[32,12]{1,0:T(8,128)S(1)} %copy.49.refs_0_, s32[1,16,2]{2,1,0:T(8,128)S(1)} %copy.50.sends.refs_1_.refs_7_, bf16[32,12,128,128]{3,2,1,0:T(8,128)(2,1)S(1)} %get-tuple-element.32.refs_2_, ...), custom_call_target="tpu_custom_call" | custom-call | tf_op jit(solution)/shard_map/apply_first_1/pallas_call | solution.py:260
  74.4 13.1 %all_to_all.42.refs_4_ = bf16[16,128,128]{2,1,0:T(8,128)(2,1)S(1)} all-to-all(bf16[16,128,128]{2,1,0:T(8,128)(2,1)S(1)} %get-tuple-element.39), channel_id=1, replica_groups=mesh['z'=4,'y'=4,'xh'=2,'xl'=2,'c'=2] {'z','y'}, dimensions={0} | all-to-all | bytes 1048576 | tf_op jit(solution)/shard_map/all_to_all | solution.py:515
  87.5 0.0 copy-done.1
  87.5 5.6 %apply_second_1.1 = (bf16[64,4096]{1,0:T(8,128)(2,1)S(1)}, bf16[3,64,4096]{2,1,0:T(8,128)(2,1)}, bf16[16,128,128]{2,1,0:T(8,128)(2,1)S(1)}, bf16[192,512]{1,0:T(8,128)(2,1)}) custom-call(s32[32,12]{1,0:T(8,128)S(1)} %copy.49.refs_0_, s32[1,16,2]{2,1,0:T(8,128)S(1)} %copy.50.sends.refs_1_.refs_7_, ...), custom_call_target="tpu_custom_call", output_to_operand_aliasing={{1}: (7, {})} | custom-call | tf_op jit(solution)/shard_map/apply_second_1/pallas_call | solution.py:260
  93.1 0.0 all-gather.6.cloned.1.call-update
  93.1 13.1 %all_to_all.43.refs_4_ = bf16[16,128,128]{2,1,0:T(8,128)(2,1)S(1)} all-to-all(bf16[16,128,128]{2,1,0:T(8,128)(2,1)S(1)} %get-tuple-element.42), channel_id=1, replica_groups=mesh['z'=4,'y'=4,'xh'=2,'xl'=2,'c'=2] {'z','y'}, dimensions={0} | all-to-all | bytes 1048576 | tf_op jit(solution)/shard_map/all_to_all | solution.py:515
  106.2 6.7 %apply_first_2.1 = (bf16[64,4096]{1,0:T(8,128)(2,1)S(1)}, bf16[16,128,128]{2,1,0:T(8,128)(2,1)S(1)}, bf16[32,12,128,128]{3,2,1,0:T(8,128)(2,1)S(1)}) custom-call(s32[32,12]{1,0:T(8,128)S(1)} %copy.49.refs_0_, s32[1,16,2]{2,1,0:T(8,128)S(1)} %copy.50.sends.refs_1_.refs_7_, bf16[32,12,128,128]{3,2,1,0:T(8,128)(2,1)} %refs_2_.3, ...), custom_call_target="tpu_custom_call" | custom-call | tf_op jit(solution)/shard_map/apply_first_2/pallas_call | solution.py:260
  112.9 13.1 %all_to_all.44.refs_4_ = bf16[16,128,128]{2,1,0:T(8,128)(2,1)S(1)} all-to-all(bf16[16,128,128]{2,1,0:T(8,128)(2,1)S(1)} %get-tuple-element.45), channel_id=1, replica_groups=mesh['z'=4,'y'=4,'xh'=2,'xl'=2,'c'=2] {'z','y'}, dimensions={0} | all-to-all | bytes 1048576 | tf_op jit(solution)/shard_map/all_to_all | solution.py:515
  125.9 5.6 %apply_second_2.1 = (bf16[64,4096]{1,0:T(8,128)(2,1)}, bf16[3,64,4096]{2,1,0:T(8,128)(2,1)}, bf16[8,64,256]{2,1,0:T(8,128)(2,1)}) custom-call(s32[32,12]{1,0:T(8,128)S(1)} %copy.49.refs_0_, s32[1,16,2]{2,1,0:T(8,128)S(1)} %copy.50.sends.refs_1_.refs_7_, bf16[32,12,128,128]{3,2,1,0:T(8,128)(2,1)S(1)} %get-tuple-element.43.refs_2_, ...), custom_call_target="tpu_custom_call", output_to_operand_aliasing={{1}: (7, {})} | custom-call | tf_op jit(solution)/shard_map/apply_second_2/pallas_call | solution.py:260
  131.6 4.5 %all-to-all-start.6 = ((bf16[8,64,256]{2,1,0:T(8,128)(2,1)}), bf16[8,64,256]{2,1,0:T(8,128)(2,1)S(1)}, u32[]{:S(2)}, u32[]{:S(2)}) async-start(bf16[8,64,256]{2,1,0:T(8,128)(2,1)} %get-tuple-element.49), calls=%async_computation.6 | async-start | bytes 524288 | tf_op jit(solution)/shard_map/all_to_all | solution.py:515
  136.1 0.1 pad_add_fusion.place
  136.2 0.0 all-reduce.2.cloned.1.call-done.counts_h
  136.2 7.5 %all-to-all-done.6.final = bf16[8,64,256]{2,1,0:T(8,128)(2,1)S(1)} async-done(((bf16[8,64,256]{2,1,0:T(8,128)(2,1)}), bf16[8,64,256]{2,1,0:T(8,128)(2,1)S(1)}, u32[]{:S(2)}, u32[]{:S(2)}) %all-to-all-start.6) | async-done | bytes 262176 | tf_op jit(solution)/shard_map/all_to_all | solution.py:515
  143.7 0.0 all-gather.4.cloned.1.call-done.grads_h
  143.7 0.0 all-gather.6.cloned.1.call-done
  143.7 24.3 %layer.1 = bf16[32,48,512]{2,1,0:T(8,128)(2,1)S(1)} custom-call(s32[2]{0:T(128)S(1)} %pad_add_fusion.place, bf16[8,192,512]{2,1,0:T(8,128)(2,1)} %bitcast.12, bf16[8,256,512]{2,1,0:T(8,128)(2,1)} %all-gather.4.cloned.1.call-done.grads_h, bf16[8,64,256]{2,1,0:T(8,128)(2,1)S(1)} %all-to-all-done.6.final, f32[128,128]{1,0:T(8,128)} %all-reduce.2.cloned.1.call-done.counts_h, ...), custom_call_target="tpu_custom_call" | custom-call | tf_op jit(solution)/shard_map/layer/pallas_call | solution.py:475
  168.0 28.1 %all_to_all.45.gathered = bf16[32,48,512]{2,1,0:T(8,128)(2,1)S(1)} all-to-all(bf16[32,48,512]{2,1,0:T(8,128)(2,1)S(1)} %layer.1), channel_id=1, replica_groups=mesh['z'=4,'y'=4,'xh'=2,'xl'=2,'c'=2] {'z','y','xh'}, dimensions={0} | all-to-all | bytes 3145728 | tf_op jit(solution)/shard_map/all_to_all | solution.py:515
  196.0 0.8 sum_parts.1
Async XLA Ops:
  8.0 128.2 %all-reduce.2.cloned.1.call-start = ((), (), s32[]{:S(2)}) async-start(), calls=%async_computation.9 | async-start | bytes 131072 | tf_op jit(solution)/shard_map/psum | solution.py:526
  11.7 131.9 %all-gather.4.cloned.1.call-start = ((), (), s32[]{:S(2)}) async-start(), calls=%async_computation.8 | async-start | bytes 2359296 | tf_op jit(solution)/shard_map/all_gather | solution.py:523
  12.3 19.7 %all-to-all-start = ((bf16[16,128,128]{2,1,0:T(8,128)(2,1)}), bf16[16,128,128]{2,1,0:T(8,128)(2,1)S(1)}, u32[]{:S(2)}, u32[]{:S(2)}) async-start(bf16[16,128,128]{2,1,0:T(8,128)(2,1)} %get-tuple-element.30), calls=%async_computation | async-start | bytes 1048576 | tf_op jit(solution)/shard_map/all_to_all | solution.py:515
  20.4 4.1 %copy-start.2 = (bf16[512,512]{1,0:T(8,128)(2,1)S(1)}, bf16[512,512]{1,0:T(8,128)(2,1)}, u32[]{:S(2)}) copy-start(bf16[512,512]{1,0:T(8,128)(2,1)} %out_h.1) | copy-start | bytes 1572868
  20.4 5.1 %copy-start.3 = (s32[32,12]{0,1:T(8,128)S(1)}, s32[32,12]{0,1:T(8,128)}, u32[]{:S(2)}) copy-start(s32[32,12]{0,1:T(8,128)} %param.15) | copy-start | bytes 4612
  20.4 11.6 %copy-start = (bf16[64,4096]{1,0:T(8,128)(2,1)S(1)}, bf16[64,4096]{1,0:T(8,128)(2,1)}, u32[]{:S(2)}) copy-start(bf16[64,4096]{1,0:T(8,128)(2,1)} %refs_9_.1) | copy-start | bytes 1572868
  20.4 123.3 %all-gather.6.cloned.1.call-start = ((), (), s32[]{:S(2)}) async-start(), calls=%async_computation.10 | async-start | bytes 1769472 | tf_op jit(solution)/shard_map/all_gather | solution.py:551
  70.4 17.1 %copy-start.1 = (s32[512]{0:T(512)S(1)}, s32[512]{0:T(512)}, u32[]{:S(2)}) copy-start(s32[512]{0:T(512)} %param.17) | copy-start | bytes 6148
  131.6 12.1 %all-to-all-start.6 = ((bf16[8,64,256]{2,1,0:T(8,128)(2,1)}), bf16[8,64,256]{2,1,0:T(8,128)(2,1)S(1)}, u32[]{:S(2)}, u32[]{:S(2)}) async-start(bf16[8,64,256]{2,1,0:T(8,128)(2,1)} %get-tuple-element.49), calls=%async_computation.6 | async-start | bytes 524288 | tf_op jit(solution)/shard_map/all_to_all | solution.py:515
Sparse Core Ops, SparseCore 0:
  12.0 85.3 all-reduce.1
Sparse Core Ops, SparseCore 1:
  13.9 27.6 all-gather.3
  93.2 21.8 all-gather.5

commit v6 on v5

--- a/solution.py
+++ b/solution.py
@@ -63,7 +63,7 @@
     names.start()
     copies = []
     for slot in range(PARTS * SEND):
-        start = pl.multiple_of(sends[0, slot // SEND, slot % SEND] * BLK, BLK)
+        start = pl.multiple_of(sends[0, slot % SEND, slot // SEND] * BLK, BLK)
         rows = (slot % SEND) * FEATS
         copies.append(
             pltpu.make_async_copy(
@@ -100,7 +100,7 @@
         ],
         compiler_params=params(4),
         name="pack",
-    )(sends, in_hbm(field), in_hbm(owners))
+    )(in_hbm(sends), in_hbm(field), in_hbm(owners))
 
 
 def picked_columns(ids, fields):
@@ -120,6 +120,7 @@
     refs = list(refs)
     lists, sends, tiles, field, incoming = refs[:5]
     refs = refs[5:]
+    up_h, out_h = (refs.pop(0), refs.pop(0)) if first else (None, None)
     degree = None if first else refs.pop(0)
     previous = refs.pop(0) if second else None
     aliased = second and refs.pop(0)
@@ -131,7 +132,16 @@
     rows_out = refs.pop(0) if picking else None
     degree_out = refs.pop(0) if first else None
     tiles_h, tiles = (tiles, refs.pop(0)) if stage else (None, tiles)
-    pool, fresh, sems = refs
+    up_t, out_t = (refs.pop(0), refs.pop(0)) if first else (None, None)
+    pool, fresh, sems = refs[:3]
+    if first:
+        up_w, out_w = refs[3:]
+        weights = [
+            pltpu.make_async_copy(up_h, up_w, sems.at[NB // CHUNK]),
+            pltpu.make_async_copy(out_h, out_w, sems.at[NB // CHUNK + 1]),
+        ]
+        for weight in weights:
+            weight.start()
 
     def load(i):
         blocks = pl.ds(i * CHUNK, CHUNK)
@@ -147,6 +157,12 @@
         for i in range(IN_FLIGHT):
             load(i).start()
 
+    if first:
+        for weight in weights:
+            weight.wait()
+        for i in range(0, FF, D):
+            up_t[:, i : i + D] = jnp.transpose(up_w[i : i + D, :])
+        out_t[...] = jnp.transpose(out_w[...])
     for j in range(NB):
         pool[j] = field[:, j * BLK : (j + 1) * BLK]
     for j in range(PARTS * SEND):
@@ -154,7 +170,7 @@
         pool[NB + j] = incoming[j // SEND, rows : rows + FEATS, :]
 
     def one_block(b):
-        picked = jnp.concatenate([pool[lists[b, k]] for k in range(K)], axis=1)
+        picked = jnp.concatenate([pool[lists[k, b]] for k in range(K)], axis=1)
         if first:
             picked = jnp.concatenate([picked, jnp.ones((GROUP, K * BLK), BF)], axis=0)
         summed = dot(picked, tiles[b].reshape(K * BLK, BLK))
@@ -193,7 +209,7 @@
         for slot in range(PARTS * SEND):
             rows = (slot % SEND) * FEATS
             outgoing[slot // SEND, rows : rows + FEATS, :] = fresh[
-                sends[0, slot // SEND, slot % SEND]
+                sends[0, slot % SEND, slot // SEND]
             ]
     if picking:
         picked = picked_columns(ids, [*others, result])
@@ -208,16 +224,22 @@
             store(i).wait()
 
 
-def apply(lists, sends, tiles, field, incoming, degree=None, previous=None, hops=None, hop=0, ids=None, others=(), stage=False):
+def apply(
+    lists, sends, tiles, field, incoming, degree=None, previous=None, hops=None, hop=0, ids=None, others=(), stage=False,
+    weights=(),
+):
     second = previous is not None
     last = second and hop == HOPS - 1
     first = hop == 0 and not second
     smem = pl.BlockSpec(memory_space=pltpu.SMEM)
     vmem = pl.BlockSpec(memory_space=pltpu.VMEM)
     hbm = pl.BlockSpec(memory_space=pltpu.HBM)
-    operands = [lists, sends, in_hbm(tiles) if stage else in_vmem(tiles), field, incoming]
+    operands = [in_hbm(lists), in_hbm(sends), in_hbm(tiles) if stage else in_vmem(tiles), field, incoming]
     in_specs = [smem, smem, hbm if stage else vmem, vmem, vmem]
-    if not first:
+    if first:
+        operands += [in_hbm(w) for w in weights]
+        in_specs += [hbm, hbm]
+    else:
         operands.append(degree)
         in_specs.append(vmem)
     out_shape = [jax.ShapeDtypeStruct((FEATS, NODES), BF)]
@@ -252,10 +274,14 @@
     if stage:
         out_shape.append(pltpu.VMEM(tiles.shape, BF))
         out_specs.append(vmem)
+    if first:
+        out_shape += [jax.ShapeDtypeStruct(w.shape[::-1], BF) for w in weights]
+        out_specs += [vmem, vmem]
     scratch = [
         pltpu.VMEM((2 * NB, FEATS, BLK), BF),
         pltpu.VMEM((NB, FEATS, BLK), BF),
-        pltpu.SemaphoreType.DMA((NB // CHUNK,)),
+        pltpu.SemaphoreType.DMA((NB // CHUNK + 2,)),
+        *[pltpu.VMEM(w.shape, BF) for w in weights],
     ]
     return pl.pallas_call(
         functools.partial(
@@ -267,51 +293,133 @@
         out_specs=out_specs,
         scratch_shapes=scratch,
         input_output_aliases=aliases,
-        compiler_params=params(8),
+        compiler_params=params(12 if first else 8),
         name=f"apply_{'second' if second else 'first'}_{hop}",
     )(*operands)
 
 
-def layer_kernel(
-    place, early_h, grads_h, final, counts_h, owners_h,
-    query_h, key_h, value_h, out_h, out_th, up_h, up_th, down_h,
-    result, query_s, key_s, value_s, mixed_s, probs_s, act_s, pre_s, gmix_s, gq_s, gk_s, gv_s, gr_s,
-    query_w, key_w, value_w, out_w, out_t, up_w, up_t, down_w, early, grads, counts, owners, sems,
-):
-    own = place[0]
-    mine = pl.ds(pl.multiple_of(place[1] * QUAD_NODES, QUAD_NODES), QUAD_NODES)
-    pairs = (
-        (query_h, query_w), (key_h, key_w), (value_h, value_w), (out_h, out_w),
-        (up_h, up_w), (down_h, down_w), (up_th, up_t), (out_th, out_t),
-        (early_h.at[:, :, mine], early), (grads_h.at[:, :, mine], grads),
-        (counts_h, counts), (owners_h, owners),
-    )
-    loads = [
+def normalize(hidden):
+    center = hidden - jnp.mean(hidden, axis=0, keepdims=True)
+    inverse = lax.rsqrt(jnp.mean(center * center, axis=0, keepdims=True) + EPSILON)
+    return center * inverse, inverse
+
+
+def copies_of(pairs, sems):
+    return [
         pltpu.make_async_copy(source, target, sems.at[index])
         for index, (source, target) in enumerate(pairs)
     ]
-    for index in (8, 0, 1, 2, 10, 11, 9, 3, 4, 5, 6, 7):
-        loads[index].start()
+
+
+def early_kernel(
+    place, early_h, grads_h, counts_h, owners_h, query_h, key_h, value_h,
+    tokens_h, normed_h, query_oh, key_oh, value_oh, scaled_h,
+    early, grads, counts, owners, query_w, key_w, value_w,
+    tokens_s, normed_s, query_s, key_s, value_s, scaled_s, sems,
+):
+    mine = pl.ds(pl.multiple_of(place[1] * QUAD_NODES, QUAD_NODES), QUAD_NODES)
+    loads = copies_of(
+        (
+            (early_h.at[:, :, mine], early), (query_h, query_w), (key_h, key_w),
+            (value_h, value_w), (counts_h, counts), (owners_h, owners),
+            (grads_h.at[:, :, mine], grads),
+        ),
+        sems,
+    )
+    stores = copies_of(
+        (
+            (tokens_s, tokens_h), (normed_s, normed_h), (query_s, query_oh),
+            (key_s, key_oh), (value_s, value_oh), (scaled_s, scaled_h),
+        ),
+        sems.at[pl.ds(len(loads), 6)],
+    )
+    for load in loads:
+        load.start()
+    loads[0].wait()
+    for t in range(HOPS):
+        cols = slice(t * QUAD_NODES, (t + 1) * QUAD_NODES)
+        tokens = early[:, t * FEATS : (t + 1) * FEATS, :].reshape(D, QUAD_NODES)
+        tokens_s[:, cols] = tokens
+        normed_s[:, cols] = normalize(tokens.astype(F32))[0].astype(BF)
+    stores[0].start()
+    stores[1].start()
+    for index, (weight, target) in enumerate(
+        ((query_w, query_s), (key_w, key_s), (value_w, value_s))
+    ):
+        loads[1 + index].wait()
+        target[...] = dot(weight[...], normed_s[...]).astype(BF)
+        stores[2 + index].start()
+    for load in loads[4:]:
+        load.wait()
+    named = lax.broadcasted_iota(jnp.int32, (OWNERS, QUAD_NODES), 0) == owners[:, mine]
+    by_owner = jnp.concatenate([1.0 / counts[...]] * (QUAD_NODES // OWNERS), axis=1)
+    row_scale = jnp.sum(jnp.where(named, by_owner, 0.0), axis=0, keepdims=True)
+    for t in range(TOKS):
+        rows = grads[:, t * FEATS : (t + 1) * FEATS, :].reshape(D, QUAD_NODES)
+        scaled_s[:, t * QUAD_NODES : (t + 1) * QUAD_NODES] = (
+            rows.astype(F32) * row_scale
+        ).astype(BF)
+    stores[5].start()
+    for store in stores:
+        store.wait()
+
+
+def early_part(place, early, grads, counts, owners, *weights):
+    hbm = pl.BlockSpec(memory_space=pltpu.HBM)
+    smem = pl.BlockSpec(memory_space=pltpu.SMEM)
+    shapes = [(D, HOPS * QUAD_NODES)] * 5 + [(D, TOKS * QUAD_NODES)]
+    return pl.pallas_call(
+        early_kernel,
+        out_shape=[pltpu.HBM(shape, BF) for shape in shapes],
+        in_specs=[smem] + [hbm] * 7,
+        out_specs=[hbm] * 6,
+        scratch_shapes=[
+            pltpu.VMEM((NARROW, HOPS * FEATS, QUAD_NODES), BF),
+            pltpu.VMEM((NARROW, TOKS * FEATS, QUAD_NODES), BF),
+            pltpu.VMEM((OWNERS, OWNERS), F32),
+            pltpu.VMEM((1, TRAIN), jnp.int32),
+            *[pltpu.VMEM(w.shape, BF) for w in weights],
+            *[pltpu.VMEM(shape, BF) for shape in shapes],
+            pltpu.SemaphoreType.DMA((13,)),
+        ],
+        compiler_params=params(24),
+        name="early",
+    )(place, *[in_hbm(array) for array in (early, grads, counts, owners, *weights)])
+
+
+def layer_kernel(
+    final, tokens_h, normed_h, query_ih, key_ih, value_ih, scaled_h, place,
+    query_h, key_h, value_h, out_h, out_th, up_h, up_th, down_h,
+    result, query_s, key_s, value_s, mixed_s, probs_s, act_s, pre_s, gmix_s, gq_s, gk_s, gv_s, gr_s,
+    query_w, key_w, value_w, out_w, out_t, up_w, up_t, down_w, tokens_s, normed_s, scaled_s, sems,
+):
+    own = place[0]
     width = TOKS * QUAD_NODES
-    loads[8].wait()
-    tokens = jnp.concatenate(
-        [early[:, t * FEATS : (t + 1) * FEATS, :].reshape(D, QUAD_NODES) for t in range(HOPS)]
-        + [final[...].reshape(D, QUAD_NODES)],
-        axis=1,
-    )
-
-    def normalize(hidden):
-        center = hidden - jnp.mean(hidden, axis=0, keepdims=True)
-        inverse = lax.rsqrt(jnp.mean(center * center, axis=0, keepdims=True) + EPSILON)
-        return center * inverse, inverse
-
-    normed_a = normalize(tokens.astype(F32))[0].astype(BF)
-    loads[0].wait()
-    query_s[...] = dot(query_w[...], normed_a).astype(BF)
-    loads[1].wait()
-    key_s[...] = dot(key_w[...], normed_a).astype(BF)
-    loads[2].wait()
-    value_s[...] = dot(value_w[...], normed_a).astype(BF)
+    known = slice(0, HOPS * QUAD_NODES)
+    added = slice(HOPS * QUAD_NODES, width)
+    loads = copies_of(
+        (
+            (query_h, query_w), (key_h, key_w), (value_h, value_w),
+            (query_ih, query_s.at[:, known]), (key_ih, key_s.at[:, known]),
+            (value_ih, value_s.at[:, known]), (out_h, out_w), (tokens_h, tokens_s.at[:, known]),
+            (up_h, up_w), (down_h, down_w), (scaled_h, scaled_s), (up_th, up_t),
+            (out_th, out_t), (normed_h, normed_s.at[:, known]),
+        ),
+        sems,
+    )
+    for load in loads:
+        load.start()
+    last = final[...].reshape(D, QUAD_NODES)
+    tokens_s[:, added] = last
+    last = normalize(last.astype(F32))[0].astype(BF)
+    normed_s[:, added] = last
+    for index, (weight, target) in enumerate(
+        ((query_w, query_s), (key_w, key_s), (value_w, value_s))
+    ):
+        loads[index].wait()
+        target[:, added] = dot(weight[...], last).astype(BF)
+    for load in loads[3:6]:
+        load.wait()
     score_scale = 1.0 / math.sqrt(HEAD_DIM)
 
     def columns(half):
@@ -348,35 +456,19 @@
         return carry
 
     lax.fori_loop(0, 2 * HEADS, forward_head, 0)
-    loads[3].wait()
-    residual = (tokens.astype(F32) + dot(out_w[...], mixed_s[...])).astype(BF)
+    loads[6].wait()
+    loads[7].wait()
+    residual = (tokens_s[...].astype(F32) + dot(out_w[...], mixed_s[...])).astype(BF)
     second_norm, second_inv = normalize(residual.astype(F32))
     normed_b = second_norm.astype(BF)
 
     root = math.sqrt(2.0 / math.pi)
     groups = FF_CHUNK // (QUAD * GROUP)
-
-    loads[9].wait()
-    loads[10].wait()
-    loads[11].wait()
-    named = lax.broadcasted_iota(jnp.int32, (OWNERS, QUAD_NODES), 0) == owners[:, mine]
-    by_owner = jnp.concatenate([1.0 / counts[...]] * (QUAD_NODES // OWNERS), axis=1)
-    row_scale = jnp.sum(jnp.where(named, by_owner, 0.0), axis=0, keepdims=True)
-    scaled = jnp.concatenate(
-        [
-            (
-                grads[:, t * FEATS : (t + 1) * FEATS, :].reshape(D, QUAD_NODES).astype(F32)
-                * row_scale
-            ).astype(BF)
-            for t in range(TOKS)
-        ],
-        axis=1,
-    )
 
     def ffn_chunk(i, carry):
         rows = pl.ds(pl.multiple_of(i * FF_CHUNK, FF_CHUNK), FF_CHUNK)
         pre = dot(up_w[rows, :], normed_b)
-        grad_act = dot(down_w[rows, :], scaled)
+        grad_act = dot(down_w[rows, :], scaled_s[...])
         square = pre * pre
         gate = 0.5 + 0.5 * jnp.tanh(pre * (root + (root * 0.044715) * square))
         activated = pre * gate
@@ -388,20 +480,20 @@
         pre_s[at] = (grad_act * slope).astype(BF).reshape(groups, QUAD, GROUP, width)
         return carry
 
-    loads[4].wait()
-    loads[5].wait()
+    for load in loads[8:11]:
+        load.wait()
     lax.fori_loop(0, FF // FF_CHUNK, ffn_chunk, 0)
 
     share = FF // QUAD
-    grad_down = dot_rows(act_s[:, own].reshape(share, width), scaled)
+    grad_down = dot_rows(act_s[:, own].reshape(share, width), scaled_s[...])
     result[:, 2 * GROUP : 3 * GROUP, :] = grad_down.astype(BF).reshape(DESTS, GROUP, D)
     grad_up = dot_rows(pre_s[:, own].reshape(share, width), normed_b)
     result[:, GROUP : 2 * GROUP, :] = grad_up.astype(BF).reshape(DESTS, GROUP, D)
 
-    loads[6].wait()
+    loads[11].wait()
     grad_normed = dot(up_t[...], pre_s[...].reshape(FF, width))
     grad_resid = (
-        scaled.astype(F32)
+        scaled_s[...].astype(F32)
         + second_inv
         * (
             grad_normed
@@ -410,7 +502,7 @@
         )
     ).astype(BF)
     gr_s[...] = grad_resid.reshape(HEADS, QUAD, GROUP, width)
-    loads[7].wait()
+    loads[12].wait()
     gmix_s[...] = dot(out_t[...], grad_resid).astype(BF)
 
     def backward_head(step, carry):
@@ -451,7 +543,8 @@
         [ref[:, own].reshape(share, width) for ref in (gq_s, gk_s, gv_s)], axis=0
     )
     count = HEADS * 3
-    result[:count, 0:GROUP, :] = dot_rows(stacked, normed_a).astype(BF).reshape(count, GROUP, D)
+    loads[13].wait()
+    result[:count, 0:GROUP, :] = dot_rows(stacked, normed_s[...]).astype(BF).reshape(count, GROUP, D)
     sum_out = dot_rows(gr_s[:, own].reshape(share, width), mixed_s[...])
     result[count:, 0:GROUP, :] = sum_out.astype(BF).reshape(HEADS, GROUP, D)
 
@@ -464,7 +557,7 @@
     return pltpu.with_memory_space_constraint(array, pltpu.HBM)
 
 
-def layer(place, early, grads, final, counts, owners, *weights):
+def layer(final, known, place, *weights):
     width = TOKS * QUAD_NODES
     square = pltpu.VMEM((D, width), BF)
     grouped = pltpu.VMEM((HEADS, QUAD, GROUP, width), BF)
@@ -475,25 +568,19 @@
     return pl.pallas_call(
         layer_kernel,
         out_shape=jax.ShapeDtypeStruct((DESTS, 3 * GROUP, D), BF),
-        in_specs=[smem, hbm, hbm, vmem, hbm, hbm] + [hbm] * 8,
+        in_specs=[vmem] + [hbm] * 6 + [smem] + [hbm] * 8,
         out_specs=vmem,
         scratch_shapes=[
             square, square, square, square,
             pltpu.VMEM((2 * HEADS, TOKS * TOKS, BLK), F32),
             wide, wide, square, grouped, grouped, grouped, grouped,
             *[pltpu.VMEM(w.shape, BF) for w in weights],
-            pltpu.VMEM((NARROW, HOPS * FEATS, QUAD_NODES), BF),
-            pltpu.VMEM((NARROW, TOKS * FEATS, QUAD_NODES), BF),
-            pltpu.VMEM((OWNERS, OWNERS), F32),
-            pltpu.VMEM((1, TRAIN), jnp.int32),
-            pltpu.SemaphoreType.DMA((len(weights) + 4,)),
+            square, square, square,
+            pltpu.SemaphoreType.DMA((14,)),
         ],
-        compiler_params=params(44),
+        compiler_params=params(48),
         name="layer",
-    )(
-        place, in_hbm(early), in_hbm(grads), final, in_hbm(counts), in_hbm(owners),
-        *[in_hbm(w) for w in weights],
-    )
+    )(final, *[in_hbm(k) for k in known], place, *[in_hbm(w) for w in weights])
 
 
 def sum_kernel(gathered, *outs):
@@ -522,17 +609,19 @@
     ids = train_ids.reshape(1, TRAIN)
     grads = lax.all_gather(cotangent.reshape(TOKS * FEATS, TRAIN), NARROW_AXES)
     owner_row = owners.reshape(1, TRAIN)
-    outgoing, counts = pack(send_lists, features, owner_row)
+    send_slots = jnp.transpose(send_lists, (0, 2, 1))
+    outgoing, counts = pack(send_slots, features, owner_row)
     counts = lax.psum(counts, WIDE)
     incoming = exchange(outgoing, WIDE)
-    incoming, up_t, out_t = lax.optimization_barrier((incoming, up_weight.T, out_weight.T))
-    step = functools.partial(apply, block_lists, send_lists)
+    step = functools.partial(apply, jnp.transpose(block_lists), send_slots)
     current = features
     hops = None
     fields = [features]
     for hop in range(HOPS):
         if hop == 0:
-            once, outgoing, degree, tiles = step(edge_tiles, current, incoming, stage=True)
+            once, outgoing, degree, tiles, up_t, out_t = step(
+                edge_tiles, current, incoming, stage=True, weights=(up_weight, out_weight)
+            )
         elif hop == HOPS - 1:
             once, outgoing, tiles = step(
                 edge_tiles, current, incoming, degree, hop=hop, stage=True
@@ -552,12 +641,14 @@
         if hop < HOPS - 1:
             incoming = exchange(results[2], WIDE)
     final = exchange(results[2], NARROW_AXES)
-
     place = jnp.stack(
         [2 * lax.axis_index("xl") + lax.axis_index("c"), lax.axis_index("xh")]
     ).astype(jnp.int32)
+    known = early_part(
+        place, early, grads, counts, owner_row, query_weight, key_weight, value_weight
+    )
     partial = layer(
-        place, early, grads, final, counts, owner_row,
+        final, known, place,
         query_weight, key_weight, value_weight, out_weight, out_t, up_weight, up_t, down_weight,
     )
     gathered = exchange(partial, QUADS)

time: 205 us -> 204 us (level)
  blocking collectives: 94.3 us -> 116 us
  waiting for transfers between devices: 14.4 us -> 2.44 us
  starting transfers between devices: 12.7 us -> 4.53 us
  local copies, waits for them, and re-layouts: 5.93 us -> 0.02 us
  Pallas kernels: 61.3 us -> 65.3 us
    all_to_all x6 -> x7, blocking collectives: 94.3 us -> 116 us  [exchange(): return lax.all_to_all(array, axes, split_axis=0, concat_axis=0, tiled=True)]
    all_to_all x2 -> x1, waiting for transfers between devices: 13.9 us -> 1.87 us  [exchange(): return lax.all_to_all(array, axes, split_axis=0, concat_axis=0, tiled=True)]
    all_to_all x2 -> x1, starting transfers between devices: 12.6 us -> 4.41 us  [exchange(): return lax.all_to_all(array, axes, split_axis=0, concat_axis=0, tiled=True)]
    unnamed x12 -> x8, local copies, waits for them, and re-layouts: 5.93 us -> 0.02 us
    pallas_call x0 -> x1, Pallas kernels: none -> 5.56 us  [early_part(): pl.pallas_call(early_kernel, out_shape=[pltpu.HBM(shape, BF) for shape in...]
  transfers between devices with their start and end apart: 5 -> 4, of which waited for: 2 -> 1; matrix products, arithmetic and copies ran while one was open for 3% -> 0% of each run, Pallas kernels for 16% -> 19%
where the time goes in v6:
time: 204 us; the launch traced here: 203 us
  blocking collectives  116 us (57%)
  Pallas kernels  65.3 us (32%)
  between operations  15.6 us (8%)
  starting transfers between devices  4.53 us (2%)
  waiting for transfers between devices  2.44 us (1%)
    all_to_all x7, blocking collectives, exchange(): return lax.all_to_all(array, axes, split_axis=0, concat_axis=0, tiled=True)  116 us
    pallas_call x6, Pallas kernels, apply(): pl.pallas_call(functools.partial(apply_kernel, second=second and hop + 1,...  33.8 us
    pallas_call x1, Pallas kernels, layer(): pl.pallas_call(layer_kernel, out_shape=jax.ShapeDtypeStruct((DESTS, 3 * G...  22.3 us
    pallas_call x1, Pallas kernels, early_part(): pl.pallas_call(early_kernel, out_shape=[pltpu.HBM(shape, BF) for shape in...  5.56 us
    all_to_all x1, starting transfers between devices, exchange(): return lax.all_to_all(array, axes, split_axis=0, concat_axis=0, tiled=True)  4.41 us
  transfers between devices with their start and end apart: 4, of which 1 were waited for; matrix products, arithmetic and copies ran while one was open for 0% of the time, Pallas kernels for 19%

profile of v6, /device:TPU:0, one launch (start us, length us, event | category | flops | bytes accessed | tf_op | source)
XLA Modules:
  0.0 203.4 jit_solution(4433978464501402990)
XLA Ops:
  8.0 0.0 copy-start
  8.0 0.0 all-reduce.2.cloned.1.call-start
  8.1 2.8 %pack.1 = (bf16[16,128,128]{2,1,0:T(8,128)(2,1)S(1)}, f32[128,128]{1,0:T(8,128)}) custom-call(s32[1,2,16]{2,1,0:T(2,128)} %bitcast.18, bf16[64,4096]{1,0:T(8,128)(2,1)} %refs_9_.1, s32[1,512]{1,0:T(1,128)} %bitcast.26), custom_call_target="tpu_custom_call" | custom-call | tf_op jit(solution)/shard_map/pack/pallas_call | solution.py:86
  10.8 0.0 all-reduce.2.cloned.1.call-update
  10.8 0.0 all-gather.4.cloned.1.call-start
  10.9 0.5 all-gather.4.cloned.1.call-update
  11.4 0.0 all-gather.6.cloned.1.call-start
  11.5 19.7 %all_to_all.40.refs_4_ = bf16[16,128,128]{2,1,0:T(8,128)(2,1)S(1)} all-to-all(bf16[16,128,128]{2,1,0:T(8,128)(2,1)S(1)} %get-tuple-element.35), channel_id=1, replica_groups=mesh['z'=4,'y'=4,'xh'=2,'xl'=2,'c'=2] {'z','y'}, dimensions={0} | all-to-all | bytes 1048576 | tf_op jit(solution)/shard_map/all_to_all | solution.py:602
  31.1 0.0 copy-done
  31.1 7.7 %apply_first_0.1 = (bf16[64,4096]{1,0:T(8,128)(2,1)S(1)}, bf16[16,128,128]{2,1,0:T(8,128)(2,1)S(1)}, f32[32,128]{1,0:T(8,128)S(1)}, bf16[32,12,128,128]{3,2,1,0:...) custom-call(s32[12,32]{1,0:T(8,128)} %bitcast.11, s32[1,2,16]{2,1,0:T(2,128)} %bitcast.19, ...), custom_call_target="tpu_custom_call" | custom-call | tf_op jit(solution)/shard_map/apply_first_0/pallas_call | solution.py:286
  38.9 0.0 copy-start.1
  38.9 0.0 copy-start.2
  38.9 13.7 %all_to_all.41.refs_4_ = bf16[16,128,128]{2,1,0:T(8,128)(2,1)S(1)} all-to-all(bf16[16,128,128]{2,1,0:T(8,128)(2,1)S(1)} %get-tuple-element.38), channel_id=1, replica_groups=mesh['z'=4,'y'=4,'xh'=2,'xl'=2,'c'=2] {'z','y'}, dimensions={0} | all-to-all | bytes 1048576 | tf_op jit(solution)/shard_map/all_to_all | solution.py:602
  52.6 4.5 %apply_second_0.1 = (bf16[64,4096]{1,0:T(8,128)(2,1)S(1)}, bf16[3,64,4096]{2,1,0:T(8,128)(2,1)}, bf16[16,128,128]{2,1,0:T(8,128)(2,1)S(1)}) custom-call(s32[12,32]{1,0:T(8,128)} %bitcast.12, s32[1,2,16]{2,1,0:T(2,128)} %bitcast.20, bf16[32,12,128,128]{3,2,1,0:T(8,128)(2,1)S(1)} %get-tuple-element.36.refs_2_, bf16[64,4096]{1,0:T(8,128)(2,1)S(1)} %get-tuple-element.37.refs_3_, ...), custom_call_target="tpu_custom_call" | custom-call | tf_op jit(solution)/shard_map/apply_second_0/pallas_call | solution.py:286
  57.1 0.0 copy-done.1
  57.1 0.0 copy-done.2
  57.2 13.2 %all_to_all.42.refs_4_ = bf16[16,128,128]{2,1,0:T(8,128)(2,1)S(1)} all-to-all(bf16[16,128,128]{2,1,0:T(8,128)(2,1)S(1)} %get-tuple-element.41), channel_id=1, replica_groups=mesh['z'=4,'y'=4,'xh'=2,'xl'=2,'c'=2] {'z','y'}, dimensions={0} | all-to-all | bytes 1048576 | tf_op jit(solution)/shard_map/all_to_all | solution.py:602
  70.4 0.0 copy-start.3
  70.4 3.9 %apply_first_1.1 = (bf16[64,4096]{1,0:T(8,128)(2,1)S(1)}, bf16[16,128,128]{2,1,0:T(8,128)(2,1)S(1)}) custom-call(s32[12,32]{1,0:T(8,128)} %bitcast.13, s32[1,2,16]{2,1,0:T(2,128)} %bitcast.22, bf16[32,12,128,128]{3,2,1,0:T(8,128)(2,1)S(1)} %get-tuple-element.36.refs_2_, bf16[64,4096]{1,0:T(8,128)(2,1)S(1)} %get-tuple-element.40.refs_3_.refs_6_.refs_10_, ...), custom_call_target="tpu_custom_call" | custom-call | tf_op jit(solution)/shard_map/apply_first_1/pallas_call | solution.py:286
  74.3 13.1 %all_to_all.43.refs_4_ = bf16[16,128,128]{2,1,0:T(8,128)(2,1)S(1)} all-to-all(bf16[16,128,128]{2,1,0:T(8,128)(2,1)S(1)} %get-tuple-element.43), channel_id=1, replica_groups=mesh['z'=4,'y'=4,'xh'=2,'xl'=2,'c'=2] {'z','y'}, dimensions={0} | all-to-all | bytes 1048576 | tf_op jit(solution)/shard_map/all_to_all | solution.py:602
  87.4 0.0 copy-done.3
  87.4 5.5 %apply_second_1.1 = (bf16[64,4096]{1,0:T(8,128)(2,1)S(1)}, bf16[3,64,4096]{2,1,0:T(8,128)(2,1)}, bf16[16,128,128]{2,1,0:T(8,128)(2,1)S(1)}, bf16[192,512]{1,0:T(8,128)(2,1)}) custom-call(s32[12,32]{1,0:T(8,128)} %bitcast.14, s32[1,2,16]{2,1,0:T(2,128)} %bitcast.23, ...), custom_call_target="tpu_custom_call", output_to_operand_aliasing={{1}: (7, {})} | custom-call | tf_op jit(solution)/shard_map/apply_second_1/pallas_call | solution.py:286
  92.9 0.0 all-gather.6.cloned.1.call-update
  92.9 13.1 %all_to_all.44.refs_4_ = bf16[16,128,128]{2,1,0:T(8,128)(2,1)S(1)} all-to-all(bf16[16,128,128]{2,1,0:T(8,128)(2,1)S(1)} %get-tuple-element.46), channel_id=1, replica_groups=mesh['z'=4,'y'=4,'xh'=2,'xl'=2,'c'=2] {'z','y'}, dimensions={0} | all-to-all | bytes 1048576 | tf_op jit(solution)/shard_map/all_to_all | solution.py:602
  106.0 6.6 %apply_first_2.1 = (bf16[64,4096]{1,0:T(8,128)(2,1)S(1)}, bf16[16,128,128]{2,1,0:T(8,128)(2,1)S(1)}, bf16[32,12,128,128]{3,2,1,0:T(8,128)(2,1)S(1)}) custom-call(s32[12,32]{1,0:T(8,128)} %bitcast.15, s32[1,2,16]{2,1,0:T(2,128)} %bitcast.24, bf16[32,12,128,128]{3,2,1,0:T(8,128)(2,1)} %refs_2_.3, bf16[64,4096]{1,0:T(8,128)(2,1)S(1)} %get-tuple-element.45.refs_3_.refs_6_, ...), custom_call_target="tpu_custom_call" | custom-call | tf_op jit(solution)/shard_map/apply_first_2/pallas_call | solution.py:286
  112.6 13.1 %all_to_all.45.refs_4_ = bf16[16,128,128]{2,1,0:T(8,128)(2,1)S(1)} all-to-all(bf16[16,128,128]{2,1,0:T(8,128)(2,1)S(1)} %get-tuple-element.49), channel_id=1, replica_groups=mesh['z'=4,'y'=4,'xh'=2,'xl'=2,'c'=2] {'z','y'}, dimensions={0} | all-to-all | bytes 1048576 | tf_op jit(solution)/shard_map/all_to_all | solution.py:602
  125.7 5.6 %apply_second_2.1 = (bf16[64,4096]{1,0:T(8,128)(2,1)}, bf16[3,64,4096]{2,1,0:T(8,128)(2,1)}, bf16[8,64,256]{2,1,0:T(8,128)(2,1)}) custom-call(s32[12,32]{1,0:T(8,128)} %bitcast.16, s32[1,2,16]{2,1,0:T(2,128)} %bitcast.25, bf16[32,12,128,128]{3,2,1,0:T(8,128)(2,1)S(1)} %get-tuple-element.47.refs_2_, ...), custom_call_target="tpu_custom_call", output_to_operand_aliasing={{1}: (7, {})} | custom-call | tf_op jit(solution)/shard_map/apply_second_2/pallas_call | solution.py:286
  131.3 4.4 %all-to-all-start.6 = ((bf16[8,64,256]{2,1,0:T(8,128)(2,1)}), bf16[8,64,256]{2,1,0:T(8,128)(2,1)S(1)}, u32[]{:S(2)}, u32[]{:S(2)}) async-start(bf16[8,64,256]{2,1,0:T(8,128)(2,1)} %get-tuple-element.52), calls=%async_computation.6 | async-start | bytes 524288 | tf_op jit(solution)/shard_map/all_to_all | solution.py:602
  135.7 0.1 pad_add_fusion.place
  135.8 0.0 all-reduce.2.cloned.1.call-done.counts_h
  135.8 0.0 all-gather.4.cloned.1.call-done.grads_h
  135.8 0.0 all-gather.6.cloned.1.call-done
  135.8 5.6 %early.1 = (bf16[512,768]{1,0:T(8,128)(2,1)}, bf16[512,768]{1,0:T(8,128)(2,1)}, bf16[512,768]{1,0:T(8,128)(2,1)}, bf16[512,768]{1,0:T(8,128)(2,1)}, bf16[512,768]{1,0:T(8,128)(2,1)}, /*index=5*/bf16[512,1024]{1,0:T(8,128)(2,1)}) custom-call(s32[2]{0:T(128)S(1)} %pad_add_fusion.place, bf16[8,192,512]{2,1,0:T(8,128)(2,1)} %bitcast.10, ...), custom_call_target="tpu_custom_call" | custom-call | tf_op jit(solution)/shard_map/early/pallas_call | solution.py:371
  141.3 1.9 all-to-all-done.6.final
  143.2 22.3 %layer.1 = bf16[32,48,512]{2,1,0:T(8,128)(2,1)S(1)} custom-call(bf16[8,64,256]{2,1,0:T(8,128)(2,1)S(1)} %all-to-all-done.6.final, bf16[512,768]{1,0:T(8,128)(2,1)} %get-tuple-element.55.tokens_h, bf16[512,768]{1,0:T(8,128)(2,1)} %get-tuple-element.56.normed_h, bf16[512,768]{1,0:T(8,128)(2,1)} %get-tuple-element.57.query_ih, ...), custom_call_target="tpu_custom_call" | custom-call | tf_op jit(solution)/shard_map/layer/pallas_call | solution.py:568
  165.5 29.6 %all_to_all.46.gathered = bf16[32,48,512]{2,1,0:T(8,128)(2,1)S(1)} all-to-all(bf16[32,48,512]{2,1,0:T(8,128)(2,1)S(1)} %layer.1), channel_id=1, replica_groups=mesh['z'=4,'y'=4,'xh'=2,'xl'=2,'c'=2] {'z','y','xh'}, dimensions={0} | all-to-all | bytes 3145728 | tf_op jit(solution)/shard_map/all_to_all | solution.py:602
  195.2 0.8 sum_parts.1
Async XLA Ops:
  8.0 23.1 %copy-start = (bf16[64,4096]{1,0:T(8,128)(2,1)S(1)}, bf16[64,4096]{1,0:T(8,128)(2,1)}, u32[]{:S(2)}) copy-start(bf16[64,4096]{1,0:T(8,128)(2,1)} %refs_9_.1) | copy-start | bytes 1572868
  8.0 127.8 %all-reduce.2.cloned.1.call-start = ((), (), s32[]{:S(2)}) async-start(), calls=%async_computation.9 | async-start | bytes 131072 | tf_op jit(solution)/shard_map/psum | solution.py:614
  10.8 124.9 %all-gather.4.cloned.1.call-start = ((), (), s32[]{:S(2)}) async-start(), calls=%async_computation.8 | async-start | bytes 2359296 | tf_op jit(solution)/shard_map/all_gather | solution.py:610
  11.4 124.4 %all-gather.6.cloned.1.call-start = ((), (), s32[]{:S(2)}) async-start(), calls=%async_computation.10 | async-start | bytes 1769472 | tf_op jit(solution)/shard_map/all_gather | solution.py:640
  38.9 18.2 %copy-start.1 = (bf16[512,2048]{1,0:T(8,128)(2,1)}, bf16[512,2048]{1,0:T(8,128)(2,1)S(1)}, u32[]{:S(2)}) copy-start(bf16[512,2048]{1,0:T(8,128)(2,1)S(1)} %get-tuple-element.62.up_th) | copy-start | bytes 6291460
  38.9 18.2 %copy-start.2 = (bf16[512,512]{1,0:T(8,128)(2,1)}, bf16[512,512]{1,0:T(8,128)(2,1)S(1)}, u32[]{:S(2)}) copy-start(bf16[512,512]{1,0:T(8,128)(2,1)S(1)} %get-tuple-element.61.out_th) | copy-start | bytes 1572868
  70.4 17.1 %copy-start.3 = (s32[512]{0:T(512)S(1)}, s32[512]{0:T(512)}, u32[]{:S(2)}) copy-start(s32[512]{0:T(512)} %param.17) | copy-start | bytes 6148
  131.3 11.9 %all-to-all-start.6 = ((bf16[8,64,256]{2,1,0:T(8,128)(2,1)}), bf16[8,64,256]{2,1,0:T(8,128)(2,1)S(1)}, u32[]{:S(2)}, u32[]{:S(2)}) async-start(bf16[8,64,256]{2,1,0:T(8,128)(2,1)} %get-tuple-element.52), calls=%async_computation.6 | async-start | bytes 524288 | tf_op jit(solution)/shard_map/all_to_all | solution.py:602
Sparse Core Ops, SparseCore 0:
  12.0 84.6 all-reduce.1
Sparse Core Ops, SparseCore 1:
  13.0 27.8 all-gather.3
  93.0 21.7 all-gather.5

commit v7 on v6

--- a/solution.py
+++ b/solution.py
@@ -352,7 +352,8 @@
     for load in loads[4:]:
         load.wait()
     named = lax.broadcasted_iota(jnp.int32, (OWNERS, QUAD_NODES), 0) == owners[:, mine]
-    by_owner = jnp.concatenate([1.0 / counts[...]] * (QUAD_NODES // OWNERS), axis=1)
+    totals = jnp.sum(counts[...], axis=0)
+    by_owner = jnp.concatenate([1.0 / totals] * (QUAD_NODES // OWNERS), axis=1)
     row_scale = jnp.sum(jnp.where(named, by_owner, 0.0), axis=0, keepdims=True)
     for t in range(TOKS):
         rows = grads[:, t * FEATS : (t + 1) * FEATS, :].reshape(D, QUAD_NODES)
@@ -376,7 +377,7 @@
         scratch_shapes=[
             pltpu.VMEM((NARROW, HOPS * FEATS, QUAD_NODES), BF),
             pltpu.VMEM((NARROW, TOKS * FEATS, QUAD_NODES), BF),
-            pltpu.VMEM((OWNERS, OWNERS), F32),
+            pltpu.VMEM((PARTS, OWNERS, OWNERS), F32),
             pltpu.VMEM((1, TRAIN), jnp.int32),
             *[pltpu.VMEM(w.shape, BF) for w in weights],
             *[pltpu.VMEM(shape, BF) for shape in shapes],
@@ -611,7 +612,7 @@
     owner_row = owners.reshape(1, TRAIN)
     send_slots = jnp.transpose(send_lists, (0, 2, 1))
     outgoing, counts = pack(send_slots, features, owner_row)
-    counts = lax.psum(counts, WIDE)
+    counts = lax.all_gather(counts, WIDE)
     incoming = exchange(outgoing, WIDE)
     step = functools.partial(apply, jnp.transpose(block_lists), send_slots)
     current = features

time: 204 us -> 204 us (level)
  no operation moved by 1% of the time
where the time goes in v7:
time: 204 us; the launch traced here: 203 us
  blocking collectives  117 us (57%)
  Pallas kernels  65.1 us (32%)
  between operations  13.9 us (7%)
  starting transfers between devices  4.48 us (2%)
  waiting for transfers between devices  2.65 us (1%)
    all_to_all x7, blocking collectives, exchange(): return lax.all_to_all(array, axes, split_axis=0, concat_axis=0, tiled=True)  117 us
    pallas_call x6, Pallas kernels, apply(): pl.pallas_call(functools.partial(apply_kernel, second=second and hop + 1,...  33.6 us
    pallas_call x1, Pallas kernels, layer(): pl.pallas_call(layer_kernel, out_shape=jax.ShapeDtypeStruct((DESTS, 3 * G...  22.3 us
    pallas_call x1, Pallas kernels, early_part(): pl.pallas_call(early_kernel, out_shape=[pltpu.HBM(shape, BF) for shape in...  5.53 us
    all_to_all x1, starting transfers between devices, exchange(): return lax.all_to_all(array, axes, split_axis=0, concat_axis=0, tiled=True)  4.37 us
  transfers between devices with their start and end apart: 4, of which 1 were waited for; matrix products, arithmetic and copies ran while one was open for 0% of the time, Pallas kernels for 19%

profile of v7, /device:TPU:0, one launch (start us, length us, event | category | flops | bytes accessed | tf_op | source)
XLA Modules:
  0.0 203.1 jit_solution(16058351336814311006)
XLA Ops:
  7.2 0.0 copy-start
  7.2 0.0 all-gather.10.cloned.1.call-start
  7.2 2.8 %pack.1 = (bf16[16,128,128]{2,1,0:T(8,128)(2,1)S(1)}, f32[128,128]{1,0:T(8,128)}) custom-call(s32[1,2,16]{2,1,0:T(2,128)} %bitcast.20, bf16[64,4096]{1,0:T(8,128)(2,1)} %refs_9_.1, s32[1,512]{1,0:T(1,128)} %bitcast.28), custom_call_target="tpu_custom_call" | custom-call | tf_op jit(solution)/shard_map/pack/pallas_call | solution.py:86
  10.0 0.0 all-gather.10.cloned.1.call-update
  10.0 0.0 all-gather.6.cloned.1.call-start
  10.1 0.7 all-gather.6.cloned.1.call-update
  10.8 0.0 all-gather.8.cloned.1.call-start
  10.8 19.9 %all_to_all.40.refs_4_ = bf16[16,128,128]{2,1,0:T(8,128)(2,1)S(1)} all-to-all(bf16[16,128,128]{2,1,0:T(8,128)(2,1)S(1)} %get-tuple-element.35), channel_id=1, replica_groups=mesh['z'=4,'y'=4,'xh'=2,'xl'=2,'c'=2] {'z','y'}, dimensions={0} | all-to-all | bytes 1048576 | tf_op jit(solution)/shard_map/all_to_all | solution.py:603
  30.7 0.0 copy-done
  30.7 7.6 %apply_first_0.1 = (bf16[64,4096]{1,0:T(8,128)(2,1)S(1)}, bf16[16,128,128]{2,1,0:T(8,128)(2,1)S(1)}, f32[32,128]{1,0:T(8,128)S(1)}, bf16[32,12,128,128]{3,2,1,0:...) custom-call(s32[12,32]{1,0:T(8,128)} %bitcast.13, s32[1,2,16]{2,1,0:T(2,128)} %bitcast.21, ...), custom_call_target="tpu_custom_call" | custom-call | tf_op jit(solution)/shard_map/apply_first_0/pallas_call | solution.py:286
  38.3 0.0 copy-start.1
  38.3 0.0 copy-start.2
  38.4 15.1 %all_to_all.41.refs_4_ = bf16[16,128,128]{2,1,0:T(8,128)(2,1)S(1)} all-to-all(bf16[16,128,128]{2,1,0:T(8,128)(2,1)S(1)} %get-tuple-element.38), channel_id=1, replica_groups=mesh['z'=4,'y'=4,'xh'=2,'xl'=2,'c'=2] {'z','y'}, dimensions={0} | all-to-all | bytes 1048576 | tf_op jit(solution)/shard_map/all_to_all | solution.py:603
  53.4 4.5 %apply_second_0.1 = (bf16[64,4096]{1,0:T(8,128)(2,1)S(1)}, bf16[3,64,4096]{2,1,0:T(8,128)(2,1)}, bf16[16,128,128]{2,1,0:T(8,128)(2,1)S(1)}) custom-call(s32[12,32]{1,0:T(8,128)} %bitcast.14, s32[1,2,16]{2,1,0:T(2,128)} %bitcast.22, bf16[32,12,128,128]{3,2,1,0:T(8,128)(2,1)S(1)} %get-tuple-element.36.refs_2_, bf16[64,4096]{1,0:T(8,128)(2,1)S(1)} %get-tuple-element.37.refs_3_, ...), custom_call_target="tpu_custom_call" | custom-call | tf_op jit(solution)/shard_map/apply_second_0/pallas_call | solution.py:286
  57.9 0.0 copy-done.1
  58.0 0.0 copy-done.2
  58.0 13.1 %all_to_all.42.refs_4_ = bf16[16,128,128]{2,1,0:T(8,128)(2,1)S(1)} all-to-all(bf16[16,128,128]{2,1,0:T(8,128)(2,1)S(1)} %get-tuple-element.41), channel_id=1, replica_groups=mesh['z'=4,'y'=4,'xh'=2,'xl'=2,'c'=2] {'z','y'}, dimensions={0} | all-to-all | bytes 1048576 | tf_op jit(solution)/shard_map/all_to_all | solution.py:603
  71.0 0.0 copy-start.3
  71.0 3.9 %apply_first_1.1 = (bf16[64,4096]{1,0:T(8,128)(2,1)S(1)}, bf16[16,128,128]{2,1,0:T(8,128)(2,1)S(1)}) custom-call(s32[12,32]{1,0:T(8,128)} %bitcast.15, s32[1,2,16]{2,1,0:T(2,128)} %bitcast.24, bf16[32,12,128,128]{3,2,1,0:T(8,128)(2,1)S(1)} %get-tuple-element.36.refs_2_, bf16[64,4096]{1,0:T(8,128)(2,1)S(1)} %get-tuple-element.40.refs_3_.refs_6_.refs_10_, ...), custom_call_target="tpu_custom_call" | custom-call | tf_op jit(solution)/shard_map/apply_first_1/pallas_call | solution.py:286
  75.0 13.1 %all_to_all.43.refs_4_ = bf16[16,128,128]{2,1,0:T(8,128)(2,1)S(1)} all-to-all(bf16[16,128,128]{2,1,0:T(8,128)(2,1)S(1)} %get-tuple-element.43), channel_id=1, replica_groups=mesh['z'=4,'y'=4,'xh'=2,'xl'=2,'c'=2] {'z','y'}, dimensions={0} | all-to-all | bytes 1048576 | tf_op jit(solution)/shard_map/all_to_all | solution.py:603
  88.1 0.0 copy-done.3
  88.1 5.5 %apply_second_1.1 = (bf16[64,4096]{1,0:T(8,128)(2,1)S(1)}, bf16[3,64,4096]{2,1,0:T(8,128)(2,1)}, bf16[16,128,128]{2,1,0:T(8,128)(2,1)S(1)}, bf16[192,512]{1,0:T(8,128)(2,1)}) custom-call(s32[12,32]{1,0:T(8,128)} %bitcast.16, s32[1,2,16]{2,1,0:T(2,128)} %bitcast.25, ...), custom_call_target="tpu_custom_call", output_to_operand_aliasing={{1}: (7, {})} | custom-call | tf_op jit(solution)/shard_map/apply_second_1/pallas_call | solution.py:286
  93.6 0.0 all-gather.8.cloned.1.call-update
  93.6 13.1 %all_to_all.44.refs_4_ = bf16[16,128,128]{2,1,0:T(8,128)(2,1)S(1)} all-to-all(bf16[16,128,128]{2,1,0:T(8,128)(2,1)S(1)} %get-tuple-element.46), channel_id=1, replica_groups=mesh['z'=4,'y'=4,'xh'=2,'xl'=2,'c'=2] {'z','y'}, dimensions={0} | all-to-all | bytes 1048576 | tf_op jit(solution)/shard_map/all_to_all | solution.py:603
  106.7 6.6 %apply_first_2.1 = (bf16[64,4096]{1,0:T(8,128)(2,1)S(1)}, bf16[16,128,128]{2,1,0:T(8,128)(2,1)S(1)}, bf16[32,12,128,128]{3,2,1,0:T(8,128)(2,1)S(1)}) custom-call(s32[12,32]{1,0:T(8,128)} %bitcast.17, s32[1,2,16]{2,1,0:T(2,128)} %bitcast.26, bf16[32,12,128,128]{3,2,1,0:T(8,128)(2,1)} %refs_2_.3, bf16[64,4096]{1,0:T(8,128)(2,1)S(1)} %get-tuple-element.45.refs_3_.refs_6_, ...), custom_call_target="tpu_custom_call" | custom-call | tf_op jit(solution)/shard_map/apply_first_2/pallas_call | solution.py:286
  113.2 13.1 %all_to_all.45.refs_4_ = bf16[16,128,128]{2,1,0:T(8,128)(2,1)S(1)} all-to-all(bf16[16,128,128]{2,1,0:T(8,128)(2,1)S(1)} %get-tuple-element.49), channel_id=1, replica_groups=mesh['z'=4,'y'=4,'xh'=2,'xl'=2,'c'=2] {'z','y'}, dimensions={0} | all-to-all | bytes 1048576 | tf_op jit(solution)/shard_map/all_to_all | solution.py:603
  126.4 5.6 %apply_second_2.1 = (bf16[64,4096]{1,0:T(8,128)(2,1)}, bf16[3,64,4096]{2,1,0:T(8,128)(2,1)}, bf16[8,64,256]{2,1,0:T(8,128)(2,1)}) custom-call(s32[12,32]{1,0:T(8,128)} %bitcast.18, s32[1,2,16]{2,1,0:T(2,128)} %bitcast.27, bf16[32,12,128,128]{3,2,1,0:T(8,128)(2,1)S(1)} %get-tuple-element.47.refs_2_, ...), custom_call_target="tpu_custom_call", output_to_operand_aliasing={{1}: (7, {})} | custom-call | tf_op jit(solution)/shard_map/apply_second_2/pallas_call | solution.py:286
  131.9 4.4 %all-to-all-start.6 = ((bf16[8,64,256]{2,1,0:T(8,128)(2,1)}), bf16[8,64,256]{2,1,0:T(8,128)(2,1)S(1)}, u32[]{:S(2)}, u32[]{:S(2)}) async-start(bf16[8,64,256]{2,1,0:T(8,128)(2,1)} %get-tuple-element.52), calls=%async_computation.6 | async-start | bytes 524288 | tf_op jit(solution)/shard_map/all_to_all | solution.py:603
  136.3 0.1 pad_add_fusion.place
  136.4 0.0 all-gather.10.cloned.1.call-done
  136.4 0.0 all-gather.6.cloned.1.call-done.grads_h
  136.4 0.0 all-gather.8.cloned.1.call-done
  136.4 5.5 %early.1 = (bf16[512,768]{1,0:T(8,128)(2,1)}, bf16[512,768]{1,0:T(8,128)(2,1)}, bf16[512,768]{1,0:T(8,128)(2,1)}, bf16[512,768]{1,0:T(8,128)(2,1)}, bf16[512,768]{1,0:T(8,128)(2,1)}, /*index=5*/bf16[512,1024]{1,0:T(8,128)(2,1)}) custom-call(s32[2]{0:T(128)S(1)} %pad_add_fusion.place, bf16[8,192,512]{2,1,0:T(8,128)(2,1)} %bitcast.11, ...), custom_call_target="tpu_custom_call" | custom-call | tf_op jit(solution)/shard_map/early/pallas_call | solution.py:372
  141.9 1.9 all-to-all-done.6.final
  143.9 22.3 %layer.1 = bf16[32,48,512]{2,1,0:T(8,128)(2,1)S(1)} custom-call(bf16[8,64,256]{2,1,0:T(8,128)(2,1)S(1)} %all-to-all-done.6.final, bf16[512,768]{1,0:T(8,128)(2,1)} %get-tuple-element.55.tokens_h, bf16[512,768]{1,0:T(8,128)(2,1)} %get-tuple-element.56.normed_h, bf16[512,768]{1,0:T(8,128)(2,1)} %get-tuple-element.57.query_ih, ...), custom_call_target="tpu_custom_call" | custom-call | tf_op jit(solution)/shard_map/layer/pallas_call | solution.py:569
  166.2 29.6 %all_to_all.46.gathered = bf16[32,48,512]{2,1,0:T(8,128)(2,1)S(1)} all-to-all(bf16[32,48,512]{2,1,0:T(8,128)(2,1)S(1)} %layer.1), channel_id=1, replica_groups=mesh['z'=4,'y'=4,'xh'=2,'xl'=2,'c'=2] {'z','y','xh'}, dimensions={0} | all-to-all | bytes 3145728 | tf_op jit(solution)/shard_map/all_to_all | solution.py:603
  195.7 0.8 sum_parts.1
Async XLA Ops:
  7.2 23.6 %copy-start = (bf16[64,4096]{1,0:T(8,128)(2,1)S(1)}, bf16[64,4096]{1,0:T(8,128)(2,1)}, u32[]{:S(2)}) copy-start(bf16[64,4096]{1,0:T(8,128)(2,1)} %refs_9_.1) | copy-start | bytes 1572868
  7.2 129.2 %all-gather.10.cloned.1.call-start = ((), (), s32[]{:S(2)}) async-start(), calls=%async_computation.10 | async-start | bytes 1114112 | tf_op jit(solution)/shard_map/all_gather | solution.py:615
  10.0 126.3 %all-gather.6.cloned.1.call-start = ((), (), s32[]{:S(2)}) async-start(), calls=%async_computation.8 | async-start | bytes 2359296 | tf_op jit(solution)/shard_map/all_gather | solution.py:611
  10.8 125.6 %all-gather.8.cloned.1.call-start = ((), (), s32[]{:S(2)}) async-start(), calls=%async_computation.9 | async-start | bytes 1769472 | tf_op jit(solution)/shard_map/all_gather | solution.py:641
  38.3 19.6 %copy-start.1 = (bf16[512,2048]{1,0:T(8,128)(2,1)}, bf16[512,2048]{1,0:T(8,128)(2,1)S(1)}, u32[]{:S(2)}) copy-start(bf16[512,2048]{1,0:T(8,128)(2,1)S(1)} %get-tuple-element.62.up_th) | copy-start | bytes 6291460
  38.3 19.6 %copy-start.2 = (bf16[512,512]{1,0:T(8,128)(2,1)}, bf16[512,512]{1,0:T(8,128)(2,1)S(1)}, u32[]{:S(2)}) copy-start(bf16[512,512]{1,0:T(8,128)(2,1)S(1)} %get-tuple-element.61.out_th) | copy-start | bytes 1572868
  71.0 17.1 %copy-start.3 = (s32[512]{0:T(512)S(1)}, s32[512]{0:T(512)}, u32[]{:S(2)}) copy-start(s32[512]{0:T(512)} %param.17) | copy-start | bytes 6148
  131.9 11.9 %all-to-all-start.6 = ((bf16[8,64,256]{2,1,0:T(8,128)(2,1)}), bf16[8,64,256]{2,1,0:T(8,128)(2,1)S(1)}, u32[]{:S(2)}, u32[]{:S(2)}) async-start(bf16[8,64,256]{2,1,0:T(8,128)(2,1)} %get-tuple-element.52), calls=%async_computation.6 | async-start | bytes 524288 | tf_op jit(solution)/shard_map/all_to_all | solution.py:603
Sparse Core Ops, SparseCore 0:
  10.2 49.1 all-gather.9
  61.1 24.3 all-gather.5
  93.7 21.9 all-gather.7

commit v8 on v7

--- a/solution.py
+++ b/solution.py
@@ -30,9 +30,10 @@
 GROUP = 16
 UNROLL = 16
 CHUNK = 4
-IN_FLIGHT = 3
+IN_FLIGHT = 8
 PICK_BLOCKS = 4
 FF_CHUNK = 512
+OUT_CHUNK = 128
 EPSILON = 1e-05
 
 BF = jnp.bfloat16
@@ -120,7 +121,6 @@
     refs = list(refs)
     lists, sends, tiles, field, incoming = refs[:5]
     refs = refs[5:]
-    up_h, out_h = (refs.pop(0), refs.pop(0)) if first else (None, None)
     degree = None if first else refs.pop(0)
     previous = refs.pop(0) if second else None
     aliased = second and refs.pop(0)
@@ -132,16 +132,7 @@
     rows_out = refs.pop(0) if picking else None
     degree_out = refs.pop(0) if first else None
     tiles_h, tiles = (tiles, refs.pop(0)) if stage else (None, tiles)
-    up_t, out_t = (refs.pop(0), refs.pop(0)) if first else (None, None)
-    pool, fresh, sems = refs[:3]
-    if first:
-        up_w, out_w = refs[3:]
-        weights = [
-            pltpu.make_async_copy(up_h, up_w, sems.at[NB // CHUNK]),
-            pltpu.make_async_copy(out_h, out_w, sems.at[NB // CHUNK + 1]),
-        ]
-        for weight in weights:
-            weight.start()
+    pool, fresh, sems = refs
 
     def load(i):
         blocks = pl.ds(i * CHUNK, CHUNK)
@@ -157,12 +148,6 @@
         for i in range(IN_FLIGHT):
             load(i).start()
 
-    if first:
-        for weight in weights:
-            weight.wait()
-        for i in range(0, FF, D):
-            up_t[:, i : i + D] = jnp.transpose(up_w[i : i + D, :])
-        out_t[...] = jnp.transpose(out_w[...])
     for j in range(NB):
         pool[j] = field[:, j * BLK : (j + 1) * BLK]
     for j in range(PARTS * SEND):
@@ -226,7 +211,6 @@
 
 def apply(
     lists, sends, tiles, field, incoming, degree=None, previous=None, hops=None, hop=0, ids=None, others=(), stage=False,
-    weights=(),
 ):
     second = previous is not None
     last = second and hop == HOPS - 1
@@ -236,10 +220,7 @@
     hbm = pl.BlockSpec(memory_space=pltpu.HBM)
     operands = [in_hbm(lists), in_hbm(sends), in_hbm(tiles) if stage else in_vmem(tiles), field, incoming]
     in_specs = [smem, smem, hbm if stage else vmem, vmem, vmem]
-    if first:
-        operands += [in_hbm(w) for w in weights]
-        in_specs += [hbm, hbm]
-    else:
+    if not first:
         operands.append(degree)
         in_specs.append(vmem)
     out_shape = [jax.ShapeDtypeStruct((FEATS, NODES), BF)]
@@ -274,14 +255,10 @@
     if stage:
         out_shape.append(pltpu.VMEM(tiles.shape, BF))
         out_specs.append(vmem)
-    if first:
-        out_shape += [jax.ShapeDtypeStruct(w.shape[::-1], BF) for w in weights]
-        out_specs += [vmem, vmem]
     scratch = [
         pltpu.VMEM((2 * NB, FEATS, BLK), BF),
         pltpu.VMEM((NB, FEATS, BLK), BF),
-        pltpu.SemaphoreType.DMA((NB // CHUNK + 2,)),
-        *[pltpu.VMEM(w.shape, BF) for w in weights],
+        pltpu.SemaphoreType.DMA((NB // CHUNK,)),
     ]
     return pl.pallas_call(
         functools.partial(
@@ -293,7 +270,7 @@
         out_specs=out_specs,
         scratch_shapes=scratch,
         input_output_aliases=aliases,
-        compiler_params=params(12 if first else 8),
+        compiler_params=params(8),
         name=f"apply_{'second' if second else 'first'}_{hop}",
     )(*operands)
 
@@ -390,9 +367,9 @@
 
 def layer_kernel(
     final, tokens_h, normed_h, query_ih, key_ih, value_ih, scaled_h, place,
-    query_h, key_h, value_h, out_h, out_th, up_h, up_th, down_h,
+    query_h, key_h, value_h, out_h, up_h, down_h,
     result, query_s, key_s, value_s, mixed_s, probs_s, act_s, pre_s, gmix_s, gq_s, gk_s, gv_s, gr_s,
-    query_w, key_w, value_w, out_w, out_t, up_w, up_t, down_w, tokens_s, normed_s, scaled_s, sems,
+    query_w, key_w, value_w, out_w, up_w, down_w, out_t, up_t, tokens_s, normed_s, scaled_s, sems,
 ):
     own = place[0]
     width = TOKS * QUAD_NODES
@@ -403,8 +380,8 @@
             (query_h, query_w), (key_h, key_w), (value_h, value_w),
             (query_ih, query_s.at[:, known]), (key_ih, key_s.at[:, known]),
             (value_ih, value_s.at[:, known]), (out_h, out_w), (tokens_h, tokens_s.at[:, known]),
-            (up_h, up_w), (down_h, down_w), (scaled_h, scaled_s), (up_th, up_t),
-            (out_th, out_t), (normed_h, normed_s.at[:, known]),
+            (up_h, up_w), (down_h, down_w), (scaled_h, scaled_s),
+            (normed_h, normed_s.at[:, known]),
         ),
         sems,
     )
@@ -468,6 +445,9 @@
 
     def ffn_chunk(i, carry):
         rows = pl.ds(pl.multiple_of(i * FF_CHUNK, FF_CHUNK), FF_CHUNK)
+        up_t[:, rows] = jnp.transpose(up_w[rows, :])
+        share = pl.ds(pl.multiple_of(i * OUT_CHUNK, OUT_CHUNK), OUT_CHUNK)
+        out_t[:, share] = jnp.transpose(out_w[share, :])
         pre = dot(up_w[rows, :], normed_b)
         grad_act = dot(down_w[rows, :], scaled_s[...])
         square = pre * pre
@@ -491,7 +471,6 @@
     grad_up = dot_rows(pre_s[:, own].reshape(share, width), normed_b)
     result[:, GROUP : 2 * GROUP, :] = grad_up.astype(BF).reshape(DESTS, GROUP, D)
 
-    loads[11].wait()
     grad_normed = dot(up_t[...], pre_s[...].reshape(FF, width))
     grad_resid = (
         scaled_s[...].astype(F32)
@@ -503,7 +482,6 @@
         )
     ).astype(BF)
     gr_s[...] = grad_resid.reshape(HEADS, QUAD, GROUP, width)
-    loads[12].wait()
     gmix_s[...] = dot(out_t[...], grad_resid).astype(BF)
 
     def backward_head(step, carry):
@@ -544,7 +522,7 @@
         [ref[:, own].reshape(share, width) for ref in (gq_s, gk_s, gv_s)], axis=0
     )
     count = HEADS * 3
-    loads[13].wait()
+    loads[11].wait()
     result[:count, 0:GROUP, :] = dot_rows(stacked, normed_s[...]).astype(BF).reshape(count, GROUP, D)
     sum_out = dot_rows(gr_s[:, own].reshape(share, width), mixed_s[...])
     result[count:, 0:GROUP, :] = sum_out.astype(BF).reshape(HEADS, GROUP, D)
@@ -569,15 +547,17 @@
     return pl.pallas_call(
         layer_kernel,
         out_shape=jax.ShapeDtypeStruct((DESTS, 3 * GROUP, D), BF),
-        in_specs=[vmem] + [hbm] * 6 + [smem] + [hbm] * 8,
+        in_specs=[vmem] + [hbm] * 6 + [smem] + [hbm] * 6,
         out_specs=vmem,
         scratch_shapes=[
             square, square, square, square,
             pltpu.VMEM((2 * HEADS, TOKS * TOKS, BLK), F32),
             wide, wide, square, grouped, grouped, grouped, grouped,
             *[pltpu.VMEM(w.shape, BF) for w in weights],
+            pltpu.VMEM((D, D), BF),
+            pltpu.VMEM((D, FF), BF),
             square, square, square,
-            pltpu.SemaphoreType.DMA((14,)),
+            pltpu.SemaphoreType.DMA((12,)),
         ],
         compiler_params=params(48),
         name="layer",
@@ -620,9 +600,7 @@
     fields = [features]
     for hop in range(HOPS):
         if hop == 0:
-            once, outgoing, degree, tiles, up_t, out_t = step(
-                edge_tiles, current, incoming, stage=True, weights=(up_weight, out_weight)
-            )
+            once, outgoing, degree, tiles = step(edge_tiles, current, incoming, stage=True)
         elif hop == HOPS - 1:
             once, outgoing, tiles = step(
                 edge_tiles, current, incoming, degree, hop=hop, stage=True
@@ -650,7 +628,7 @@
     )
     partial = layer(
         final, known, place,
-        query_weight, key_weight, value_weight, out_weight, out_t, up_weight, up_t, down_weight,
+        query_weight, key_weight, value_weight, out_weight, up_weight, down_weight,
     )
     gathered = exchange(partial, QUADS)
     return (hops, *sum_parts(gathered))

time: 204 us -> 201 us (0.985)
  Pallas kernels: 65.1 us -> 62.5 us
where the time goes in v8:
time: 201 us; the launch traced here: 200 us
  blocking collectives  117 us (58%)
  Pallas kernels  62.5 us (31%)
  between operations  13.8 us (7%)
  starting transfers between devices  4.44 us (2%)
  waiting for transfers between devices  2.63 us (1%)
    all_to_all x7, blocking collectives, exchange(): return lax.all_to_all(array, axes, split_axis=0, concat_axis=0, tiled=True)  117 us
    pallas_call x6, Pallas kernels, apply(): pl.pallas_call(functools.partial(apply_kernel, second=second and hop + 1,...  31.8 us
    pallas_call x1, Pallas kernels, layer(): pl.pallas_call(layer_kernel, out_shape=jax.ShapeDtypeStruct((DESTS, 3 * G...  21.5 us
    pallas_call x1, Pallas kernels, early_part(): pl.pallas_call(early_kernel, out_shape=[pltpu.HBM(shape, BF) for shape in...  5.54 us
    all_to_all x1, starting transfers between devices, exchange(): return lax.all_to_all(array, axes, split_axis=0, concat_axis=0, tiled=True)  4.32 us
  transfers between devices with their start and end apart: 4, of which 1 were waited for; matrix products, arithmetic and copies ran while one was open for 0% of the time, Pallas kernels for 19%

profile of v8, /device:TPU:0, one launch (start us, length us, event | category | flops | bytes accessed | tf_op | source)
XLA Modules:
  0.0 200.0 jit_solution(1411983805392347537)
XLA Ops:
  7.2 0.0 copy-start
  7.2 0.0 all-gather.10.cloned.1.call-start
  7.2 2.8 %pack.1 = (bf16[16,128,128]{2,1,0:T(8,128)(2,1)S(1)}, f32[128,128]{1,0:T(8,128)}) custom-call(s32[1,2,16]{2,1,0:T(2,128)} %bitcast.20, bf16[64,4096]{1,0:T(8,128)(2,1)} %refs_9_.1, s32[1,512]{1,0:T(1,128)} %bitcast.28), custom_call_target="tpu_custom_call" | custom-call | tf_op jit(solution)/shard_map/pack/pallas_call | solution.py:87
  10.0 0.0 all-gather.10.cloned.1.call-update
  10.0 0.0 all-gather.6.cloned.1.call-start
  10.1 0.7 all-gather.6.cloned.1.call-update
  10.8 0.0 all-gather.8.cloned.1.call-start
  10.8 19.9 %all_to_all.40.refs_4_ = bf16[16,128,128]{2,1,0:T(8,128)(2,1)S(1)} all-to-all(bf16[16,128,128]{2,1,0:T(8,128)(2,1)S(1)} %get-tuple-element.33), channel_id=1, replica_groups=mesh['z'=4,'y'=4,'xh'=2,'xl'=2,'c'=2] {'z','y'}, dimensions={0} | all-to-all | bytes 1048576 | tf_op jit(solution)/shard_map/all_to_all | solution.py:583
  30.7 0.0 copy-done
  30.7 6.2 %apply_first_0.1 = (bf16[64,4096]{1,0:T(8,128)(2,1)S(1)}, bf16[16,128,128]{2,1,0:T(8,128)(2,1)S(1)}, f32[32,128]{1,0:T(8,128)S(1)}, bf16[32,12,128,128]{3,2,1,0:T(8,128)(2,1)S(1)}) custom-call(s32[12,32]{1,0:T(8,128)} %bitcast.13, s32[1,2,16]{2,1,0:T(2,128)} %bitcast.21, bf16[32,12,128,128]{3,2,1,0:T(8,128)(2,1)} %refs_2_.3, bf16[64,4096]{1,0:T(8,128)(2,1)S(1)} %copy-done, ...), custom_call_target="tpu_custom_call" | custom-call | tf_op jit(solution)/shard_map/apply_first_0/pallas_call | solution.py:263
  36.9 15.1 %all_to_all.41.refs_4_ = bf16[16,128,128]{2,1,0:T(8,128)(2,1)S(1)} all-to-all(bf16[16,128,128]{2,1,0:T(8,128)(2,1)S(1)} %get-tuple-element.36), channel_id=1, replica_groups=mesh['z'=4,'y'=4,'xh'=2,'xl'=2,'c'=2] {'z','y'}, dimensions={0} | all-to-all | bytes 1048576 | tf_op jit(solution)/shard_map/all_to_all | solution.py:583
  52.0 4.5 %apply_second_0.1 = (bf16[64,4096]{1,0:T(8,128)(2,1)S(1)}, bf16[3,64,4096]{2,1,0:T(8,128)(2,1)}, bf16[16,128,128]{2,1,0:T(8,128)(2,1)S(1)}) custom-call(s32[12,32]{1,0:T(8,128)} %bitcast.14, s32[1,2,16]{2,1,0:T(2,128)} %bitcast.22, bf16[32,12,128,128]{3,2,1,0:T(8,128)(2,1)S(1)} %get-tuple-element.34.refs_2_, bf16[64,4096]{1,0:T(8,128)(2,1)S(1)} %get-tuple-element.35.refs_3_, ...), custom_call_target="tpu_custom_call" | custom-call | tf_op jit(solution)/shard_map/apply_second_0/pallas_call | solution.py:263
  56.5 12.8 %all_to_all.42.refs_4_ = bf16[16,128,128]{2,1,0:T(8,128)(2,1)S(1)} all-to-all(bf16[16,128,128]{2,1,0:T(8,128)(2,1)S(1)} %get-tuple-element.39), channel_id=1, replica_groups=mesh['z'=4,'y'=4,'xh'=2,'xl'=2,'c'=2] {'z','y'}, dimensions={0} | all-to-all | bytes 1048576 | tf_op jit(solution)/shard_map/all_to_all | solution.py:583
  69.3 0.0 copy-start.1
  69.3 3.9 %apply_first_1.1 = (bf16[64,4096]{1,0:T(8,128)(2,1)S(1)}, bf16[16,128,128]{2,1,0:T(8,128)(2,1)S(1)}) custom-call(s32[12,32]{1,0:T(8,128)} %bitcast.15, s32[1,2,16]{2,1,0:T(2,128)} %bitcast.24, bf16[32,12,128,128]{3,2,1,0:T(8,128)(2,1)S(1)} %get-tuple-element.34.refs_2_, bf16[64,4096]{1,0:T(8,128)(2,1)S(1)} %get-tuple-element.38.refs_3_.refs_6_.refs_10_, ...), custom_call_target="tpu_custom_call" | custom-call | tf_op jit(solution)/shard_map/apply_first_1/pallas_call | solution.py:263
  73.2 13.1 %all_to_all.43.refs_4_ = bf16[16,128,128]{2,1,0:T(8,128)(2,1)S(1)} all-to-all(bf16[16,128,128]{2,1,0:T(8,128)(2,1)S(1)} %get-tuple-element.41), channel_id=1, replica_groups=mesh['z'=4,'y'=4,'xh'=2,'xl'=2,'c'=2] {'z','y'}, dimensions={0} | all-to-all | bytes 1048576 | tf_op jit(solution)/shard_map/all_to_all | solution.py:583
  86.3 0.0 copy-done.1
  86.3 5.5 %apply_second_1.1 = (bf16[64,4096]{1,0:T(8,128)(2,1)S(1)}, bf16[3,64,4096]{2,1,0:T(8,128)(2,1)}, bf16[16,128,128]{2,1,0:T(8,128)(2,1)S(1)}, bf16[192,512]{1,0:T(8,128)(2,1)}) custom-call(s32[12,32]{1,0:T(8,128)} %bitcast.16, s32[1,2,16]{2,1,0:T(2,128)} %bitcast.25, ...), custom_call_target="tpu_custom_call", output_to_operand_aliasing={{1}: (7, {})} | custom-call | tf_op jit(solution)/shard_map/apply_second_1/pallas_call | solution.py:263
  91.8 0.0 all-gather.8.cloned.1.call-update
  91.9 13.1 %all_to_all.44.refs_4_ = bf16[16,128,128]{2,1,0:T(8,128)(2,1)S(1)} all-to-all(bf16[16,128,128]{2,1,0:T(8,128)(2,1)S(1)} %get-tuple-element.44), channel_id=1, replica_groups=mesh['z'=4,'y'=4,'xh'=2,'xl'=2,'c'=2] {'z','y'}, dimensions={0} | all-to-all | bytes 1048576 | tf_op jit(solution)/shard_map/all_to_all | solution.py:583
  105.0 6.1 %apply_first_2.1 = (bf16[64,4096]{1,0:T(8,128)(2,1)S(1)}, bf16[16,128,128]{2,1,0:T(8,128)(2,1)S(1)}, bf16[32,12,128,128]{3,2,1,0:T(8,128)(2,1)S(1)}) custom-call(s32[12,32]{1,0:T(8,128)} %bitcast.17, s32[1,2,16]{2,1,0:T(2,128)} %bitcast.26, bf16[32,12,128,128]{3,2,1,0:T(8,128)(2,1)} %refs_2_.3, bf16[64,4096]{1,0:T(8,128)(2,1)S(1)} %get-tuple-element.43.refs_3_.refs_6_, ...), custom_call_target="tpu_custom_call" | custom-call | tf_op jit(solution)/shard_map/apply_first_2/pallas_call | solution.py:263
  111.1 13.1 %all_to_all.45.refs_4_ = bf16[16,128,128]{2,1,0:T(8,128)(2,1)S(1)} all-to-all(bf16[16,128,128]{2,1,0:T(8,128)(2,1)S(1)} %get-tuple-element.47), channel_id=1, replica_groups=mesh['z'=4,'y'=4,'xh'=2,'xl'=2,'c'=2] {'z','y'}, dimensions={0} | all-to-all | bytes 1048576 | tf_op jit(solution)/shard_map/all_to_all | solution.py:583
  124.2 5.5 %apply_second_2.1 = (bf16[64,4096]{1,0:T(8,128)(2,1)}, bf16[3,64,4096]{2,1,0:T(8,128)(2,1)}, bf16[8,64,256]{2,1,0:T(8,128)(2,1)}) custom-call(s32[12,32]{1,0:T(8,128)} %bitcast.18, s32[1,2,16]{2,1,0:T(2,128)} %bitcast.27, bf16[32,12,128,128]{3,2,1,0:T(8,128)(2,1)S(1)} %get-tuple-element.45.refs_2_, ...), custom_call_target="tpu_custom_call", output_to_operand_aliasing={{1}: (7, {})} | custom-call | tf_op jit(solution)/shard_map/apply_second_2/pallas_call | solution.py:263
  129.7 4.3 %all-to-all-start.6 = ((bf16[8,64,256]{2,1,0:T(8,128)(2,1)}), bf16[8,64,256]{2,1,0:T(8,128)(2,1)S(1)}, u32[]{:S(2)}, u32[]{:S(2)}) async-start(bf16[8,64,256]{2,1,0:T(8,128)(2,1)} %get-tuple-element.50), calls=%async_computation.6 | async-start | bytes 524288 | tf_op jit(solution)/shard_map/all_to_all | solution.py:583
  134.1 0.1 pad_add_fusion.place
  134.1 0.0 all-gather.10.cloned.1.call-done
  134.1 0.0 all-gather.6.cloned.1.call-done.grads_h
  134.1 0.0 all-gather.8.cloned.1.call-done
  134.2 5.5 %early.1 = (bf16[512,768]{1,0:T(8,128)(2,1)}, bf16[512,768]{1,0:T(8,128)(2,1)}, bf16[512,768]{1,0:T(8,128)(2,1)}, bf16[512,768]{1,0:T(8,128)(2,1)}, bf16[512,768]{1,0:T(8,128)(2,1)}, /*index=5*/bf16[512,1024]{1,0:T(8,128)(2,1)}) custom-call(s32[2]{0:T(128)S(1)} %pad_add_fusion.place, bf16[8,192,512]{2,1,0:T(8,128)(2,1)} %bitcast.11, ...), custom_call_target="tpu_custom_call" | custom-call | tf_op jit(solution)/shard_map/early/pallas_call | solution.py:349
  139.7 1.9 all-to-all-done.6.final
  141.6 21.5 %layer.1 = bf16[32,48,512]{2,1,0:T(8,128)(2,1)S(1)} custom-call(bf16[8,64,256]{2,1,0:T(8,128)(2,1)S(1)} %all-to-all-done.6.final, bf16[512,768]{1,0:T(8,128)(2,1)} %get-tuple-element.53.tokens_h, bf16[512,768]{1,0:T(8,128)(2,1)} %get-tuple-element.54.normed_h, bf16[512,768]{1,0:T(8,128)(2,1)} %get-tuple-element.55.query_ih, ...), custom_call_target="tpu_custom_call" | custom-call | tf_op jit(solution)/shard_map/layer/pallas_call | solution.py:547
  163.1 29.6 %all_to_all.46.gathered = bf16[32,48,512]{2,1,0:T(8,128)(2,1)S(1)} all-to-all(bf16[32,48,512]{2,1,0:T(8,128)(2,1)S(1)} %layer.1), channel_id=1, replica_groups=mesh['z'=4,'y'=4,'xh'=2,'xl'=2,'c'=2] {'z','y','xh'}, dimensions={0} | all-to-all | bytes 3145728 | tf_op jit(solution)/shard_map/all_to_all | solution.py:583
  192.7 0.8 sum_parts.1
Async XLA Ops:
  7.2 23.5 %copy-start = (bf16[64,4096]{1,0:T(8,128)(2,1)S(1)}, bf16[64,4096]{1,0:T(8,128)(2,1)}, u32[]{:S(2)}) copy-start(bf16[64,4096]{1,0:T(8,128)(2,1)} %refs_9_.1) | copy-start | bytes 1572868
  7.2 127.0 %all-gather.10.cloned.1.call-start = ((), (), s32[]{:S(2)}) async-start(), calls=%async_computation.10 | async-start | bytes 1114112 | tf_op jit(solution)/shard_map/all_gather | solution.py:595
  10.0 124.1 %all-gather.6.cloned.1.call-start = ((), (), s32[]{:S(2)}) async-start(), calls=%async_computation.8 | async-start | bytes 2359296 | tf_op jit(solution)/shard_map/all_gather | solution.py:591
  10.8 123.4 %all-gather.8.cloned.1.call-start = ((), (), s32[]{:S(2)}) async-start(), calls=%async_computation.9 | async-start | bytes 1769472 | tf_op jit(solution)/shard_map/all_gather | solution.py:619
  69.3 17.0 %copy-start.1 = (s32[512]{0:T(512)S(1)}, s32[512]{0:T(512)}, u32[]{:S(2)}) copy-start(s32[512]{0:T(512)} %param.17) | copy-start | bytes 6148
  129.7 11.9 %all-to-all-start.6 = ((bf16[8,64,256]{2,1,0:T(8,128)(2,1)}), bf16[8,64,256]{2,1,0:T(8,128)(2,1)S(1)}, u32[]{:S(2)}, u32[]{:S(2)}) async-start(bf16[8,64,256]{2,1,0:T(8,128)(2,1)} %get-tuple-element.50), calls=%async_computation.6 | async-start | bytes 524288 | tf_op jit(solution)/shard_map/all_to_all | solution.py:583
Sparse Core Ops, SparseCore 0:
  10.1 47.9 all-gather.9
  59.9 24.1 all-gather.5
  92.0 21.9 all-gather.7

commit v9 on v8

--- a/solution.py
+++ b/solution.py
@@ -385,7 +385,7 @@
         ),
         sems,
     )
-    for load in loads:
+    for load in loads[:6]:
         load.start()
     last = final[...].reshape(D, QUAD_NODES)
     tokens_s[:, added] = last
@@ -398,6 +398,8 @@
         target[:, added] = dot(weight[...], last).astype(BF)
     for load in loads[3:6]:
         load.wait()
+    for load in loads[6:]:
+        load.start()
     score_scale = 1.0 / math.sqrt(HEAD_DIM)
 
     def columns(half):

time: 201 us -> 201 us (level)
  no operation moved by 1% of the time
where the time goes in v9:
time: 201 us; the launch traced here: 200 us
  blocking collectives  117 us (58%)
  Pallas kernels  62.5 us (31%)
  between operations  13.8 us (7%)
  starting transfers between devices  4.43 us (2%)
  waiting for transfers between devices  2.63 us (1%)
    all_to_all x7, blocking collectives, exchange(): return lax.all_to_all(array, axes, split_axis=0, concat_axis=0, tiled=True)  117 us
    pallas_call x6, Pallas kernels, apply(): pl.pallas_call(functools.partial(apply_kernel, second=second and hop + 1,...  31.8 us
    pallas_call x1, Pallas kernels, layer(): pl.pallas_call(layer_kernel, out_shape=jax.ShapeDtypeStruct((DESTS, 3 * G...  21.5 us
    pallas_call x1, Pallas kernels, early_part(): pl.pallas_call(early_kernel, out_shape=[pltpu.HBM(shape, BF) for shape in...  5.54 us
    all_to_all x1, starting transfers between devices, exchange(): return lax.all_to_all(array, axes, split_axis=0, concat_axis=0, tiled=True)  4.32 us
  transfers between devices with their start and end apart: 4, of which 1 were waited for; matrix products, arithmetic and copies ran while one was open for 0% of the time, Pallas kernels for 19%

profile of v9, /device:TPU:0, one launch (start us, length us, event | category | flops | bytes accessed | tf_op | source)
XLA Modules:
  0.0 200.1 jit_solution(5871621392335995484)
XLA Ops:
  7.2 0.0 copy-start
  7.2 0.0 all-gather.10.cloned.1.call-start
  7.2 2.9 %pack.1 = (bf16[16,128,128]{2,1,0:T(8,128)(2,1)S(1)}, f32[128,128]{1,0:T(8,128)}) custom-call(s32[1,2,16]{2,1,0:T(2,128)} %bitcast.20, bf16[64,4096]{1,0:T(8,128)(2,1)} %refs_9_.1, s32[1,512]{1,0:T(1,128)} %bitcast.28), custom_call_target="tpu_custom_call" | custom-call | tf_op jit(solution)/shard_map/pack/pallas_call | solution.py:87
  10.1 0.0 all-gather.10.cloned.1.call-update
  10.1 0.0 all-gather.6.cloned.1.call-start
  10.2 0.7 all-gather.6.cloned.1.call-update
  10.9 0.0 all-gather.8.cloned.1.call-start
  10.9 19.8 %all_to_all.40.refs_4_ = bf16[16,128,128]{2,1,0:T(8,128)(2,1)S(1)} all-to-all(bf16[16,128,128]{2,1,0:T(8,128)(2,1)S(1)} %get-tuple-element.33), channel_id=1, replica_groups=mesh['z'=4,'y'=4,'xh'=2,'xl'=2,'c'=2] {'z','y'}, dimensions={0} | all-to-all | bytes 1048576 | tf_op jit(solution)/shard_map/all_to_all | solution.py:585
  30.7 0.0 copy-done
  30.7 6.2 %apply_first_0.1 = (bf16[64,4096]{1,0:T(8,128)(2,1)S(1)}, bf16[16,128,128]{2,1,0:T(8,128)(2,1)S(1)}, f32[32,128]{1,0:T(8,128)S(1)}, bf16[32,12,128,128]{3,2,1,0:T(8,128)(2,1)S(1)}) custom-call(s32[12,32]{1,0:T(8,128)} %bitcast.13, s32[1,2,16]{2,1,0:T(2,128)} %bitcast.21, bf16[32,12,128,128]{3,2,1,0:T(8,128)(2,1)} %refs_2_.3, bf16[64,4096]{1,0:T(8,128)(2,1)S(1)} %copy-done, ...), custom_call_target="tpu_custom_call" | custom-call | tf_op jit(solution)/shard_map/apply_first_0/pallas_call | solution.py:263
  36.9 15.1 %all_to_all.41.refs_4_ = bf16[16,128,128]{2,1,0:T(8,128)(2,1)S(1)} all-to-all(bf16[16,128,128]{2,1,0:T(8,128)(2,1)S(1)} %get-tuple-element.36), channel_id=1, replica_groups=mesh['z'=4,'y'=4,'xh'=2,'xl'=2,'c'=2] {'z','y'}, dimensions={0} | all-to-all | bytes 1048576 | tf_op jit(solution)/shard_map/all_to_all | solution.py:585
  52.1 4.5 %apply_second_0.1 = (bf16[64,4096]{1,0:T(8,128)(2,1)S(1)}, bf16[3,64,4096]{2,1,0:T(8,128)(2,1)}, bf16[16,128,128]{2,1,0:T(8,128)(2,1)S(1)}) custom-call(s32[12,32]{1,0:T(8,128)} %bitcast.14, s32[1,2,16]{2,1,0:T(2,128)} %bitcast.22, bf16[32,12,128,128]{3,2,1,0:T(8,128)(2,1)S(1)} %get-tuple-element.34.refs_2_, bf16[64,4096]{1,0:T(8,128)(2,1)S(1)} %get-tuple-element.35.refs_3_, ...), custom_call_target="tpu_custom_call" | custom-call | tf_op jit(solution)/shard_map/apply_second_0/pallas_call | solution.py:263
  56.6 12.8 %all_to_all.42.refs_4_ = bf16[16,128,128]{2,1,0:T(8,128)(2,1)S(1)} all-to-all(bf16[16,128,128]{2,1,0:T(8,128)(2,1)S(1)} %get-tuple-element.39), channel_id=1, replica_groups=mesh['z'=4,'y'=4,'xh'=2,'xl'=2,'c'=2] {'z','y'}, dimensions={0} | all-to-all | bytes 1048576 | tf_op jit(solution)/shard_map/all_to_all | solution.py:585
  69.3 0.0 copy-start.1
  69.3 3.9 %apply_first_1.1 = (bf16[64,4096]{1,0:T(8,128)(2,1)S(1)}, bf16[16,128,128]{2,1,0:T(8,128)(2,1)S(1)}) custom-call(s32[12,32]{1,0:T(8,128)} %bitcast.15, s32[1,2,16]{2,1,0:T(2,128)} %bitcast.24, bf16[32,12,128,128]{3,2,1,0:T(8,128)(2,1)S(1)} %get-tuple-element.34.refs_2_, bf16[64,4096]{1,0:T(8,128)(2,1)S(1)} %get-tuple-element.38.refs_3_.refs_6_.refs_10_, ...), custom_call_target="tpu_custom_call" | custom-call | tf_op jit(solution)/shard_map/apply_first_1/pallas_call | solution.py:263
  73.3 13.1 %all_to_all.43.refs_4_ = bf16[16,128,128]{2,1,0:T(8,128)(2,1)S(1)} all-to-all(bf16[16,128,128]{2,1,0:T(8,128)(2,1)S(1)} %get-tuple-element.41), channel_id=1, replica_groups=mesh['z'=4,'y'=4,'xh'=2,'xl'=2,'c'=2] {'z','y'}, dimensions={0} | all-to-all | bytes 1048576 | tf_op jit(solution)/shard_map/all_to_all | solution.py:585
  86.4 0.0 copy-done.1
  86.4 5.5 %apply_second_1.1 = (bf16[64,4096]{1,0:T(8,128)(2,1)S(1)}, bf16[3,64,4096]{2,1,0:T(8,128)(2,1)}, bf16[16,128,128]{2,1,0:T(8,128)(2,1)S(1)}, bf16[192,512]{1,0:T(8,128)(2,1)}) custom-call(s32[12,32]{1,0:T(8,128)} %bitcast.16, s32[1,2,16]{2,1,0:T(2,128)} %bitcast.25, ...), custom_call_target="tpu_custom_call", output_to_operand_aliasing={{1}: (7, {})} | custom-call | tf_op jit(solution)/shard_map/apply_second_1/pallas_call | solution.py:263
  91.9 0.0 all-gather.8.cloned.1.call-update
  91.9 13.1 %all_to_all.44.refs_4_ = bf16[16,128,128]{2,1,0:T(8,128)(2,1)S(1)} all-to-all(bf16[16,128,128]{2,1,0:T(8,128)(2,1)S(1)} %get-tuple-element.44), channel_id=1, replica_groups=mesh['z'=4,'y'=4,'xh'=2,'xl'=2,'c'=2] {'z','y'}, dimensions={0} | all-to-all | bytes 1048576 | tf_op jit(solution)/shard_map/all_to_all | solution.py:585
  105.0 6.1 %apply_first_2.1 = (bf16[64,4096]{1,0:T(8,128)(2,1)S(1)}, bf16[16,128,128]{2,1,0:T(8,128)(2,1)S(1)}, bf16[32,12,128,128]{3,2,1,0:T(8,128)(2,1)S(1)}) custom-call(s32[12,32]{1,0:T(8,128)} %bitcast.17, s32[1,2,16]{2,1,0:T(2,128)} %bitcast.26, bf16[32,12,128,128]{3,2,1,0:T(8,128)(2,1)} %refs_2_.3, bf16[64,4096]{1,0:T(8,128)(2,1)S(1)} %get-tuple-element.43.refs_3_.refs_6_, ...), custom_call_target="tpu_custom_call" | custom-call | tf_op jit(solution)/shard_map/apply_first_2/pallas_call | solution.py:263
  111.2 13.1 %all_to_all.45.refs_4_ = bf16[16,128,128]{2,1,0:T(8,128)(2,1)S(1)} all-to-all(bf16[16,128,128]{2,1,0:T(8,128)(2,1)S(1)} %get-tuple-element.47), channel_id=1, replica_groups=mesh['z'=4,'y'=4,'xh'=2,'xl'=2,'c'=2] {'z','y'}, dimensions={0} | all-to-all | bytes 1048576 | tf_op jit(solution)/shard_map/all_to_all | solution.py:585
  124.2 5.5 %apply_second_2.1 = (bf16[64,4096]{1,0:T(8,128)(2,1)}, bf16[3,64,4096]{2,1,0:T(8,128)(2,1)}, bf16[8,64,256]{2,1,0:T(8,128)(2,1)}) custom-call(s32[12,32]{1,0:T(8,128)} %bitcast.18, s32[1,2,16]{2,1,0:T(2,128)} %bitcast.27, bf16[32,12,128,128]{3,2,1,0:T(8,128)(2,1)S(1)} %get-tuple-element.45.refs_2_, ...), custom_call_target="tpu_custom_call", output_to_operand_aliasing={{1}: (7, {})} | custom-call | tf_op jit(solution)/shard_map/apply_second_2/pallas_call | solution.py:263
  129.8 4.3 %all-to-all-start.6 = ((bf16[8,64,256]{2,1,0:T(8,128)(2,1)}), bf16[8,64,256]{2,1,0:T(8,128)(2,1)S(1)}, u32[]{:S(2)}, u32[]{:S(2)}) async-start(bf16[8,64,256]{2,1,0:T(8,128)(2,1)} %get-tuple-element.50), calls=%async_computation.6 | async-start | bytes 524288 | tf_op jit(solution)/shard_map/all_to_all | solution.py:585
  134.1 0.1 pad_add_fusion.place
  134.2 0.0 all-gather.10.cloned.1.call-done
  134.2 0.0 all-gather.6.cloned.1.call-done.grads_h
  134.2 0.0 all-gather.8.cloned.1.call-done
  134.2 5.5 %early.1 = (bf16[512,768]{1,0:T(8,128)(2,1)}, bf16[512,768]{1,0:T(8,128)(2,1)}, bf16[512,768]{1,0:T(8,128)(2,1)}, bf16[512,768]{1,0:T(8,128)(2,1)}, bf16[512,768]{1,0:T(8,128)(2,1)}, /*index=5*/bf16[512,1024]{1,0:T(8,128)(2,1)}) custom-call(s32[2]{0:T(128)S(1)} %pad_add_fusion.place, bf16[8,192,512]{2,1,0:T(8,128)(2,1)} %bitcast.11, ...), custom_call_target="tpu_custom_call" | custom-call | tf_op jit(solution)/shard_map/early/pallas_call | solution.py:349
  139.8 1.9 all-to-all-done.6.final
  141.6 21.5 %layer.1 = bf16[32,48,512]{2,1,0:T(8,128)(2,1)S(1)} custom-call(bf16[8,64,256]{2,1,0:T(8,128)(2,1)S(1)} %all-to-all-done.6.final, bf16[512,768]{1,0:T(8,128)(2,1)} %get-tuple-element.53.tokens_h, bf16[512,768]{1,0:T(8,128)(2,1)} %get-tuple-element.54.normed_h, bf16[512,768]{1,0:T(8,128)(2,1)} %get-tuple-element.55.query_ih, ...), custom_call_target="tpu_custom_call" | custom-call | tf_op jit(solution)/shard_map/layer/pallas_call | solution.py:549
  163.1 29.6 %all_to_all.46.gathered = bf16[32,48,512]{2,1,0:T(8,128)(2,1)S(1)} all-to-all(bf16[32,48,512]{2,1,0:T(8,128)(2,1)S(1)} %layer.1), channel_id=1, replica_groups=mesh['z'=4,'y'=4,'xh'=2,'xl'=2,'c'=2] {'z','y','xh'}, dimensions={0} | all-to-all | bytes 3145728 | tf_op jit(solution)/shard_map/all_to_all | solution.py:585
  192.7 0.8 sum_parts.1
Async XLA Ops:
  7.2 23.6 %copy-start = (bf16[64,4096]{1,0:T(8,128)(2,1)S(1)}, bf16[64,4096]{1,0:T(8,128)(2,1)}, u32[]{:S(2)}) copy-start(bf16[64,4096]{1,0:T(8,128)(2,1)} %refs_9_.1) | copy-start | bytes 1572868
  7.2 127.0 %all-gather.10.cloned.1.call-start = ((), (), s32[]{:S(2)}) async-start(), calls=%async_computation.10 | async-start | bytes 1114112 | tf_op jit(solution)/shard_map/all_gather | solution.py:597
  10.1 124.1 %all-gather.6.cloned.1.call-start = ((), (), s32[]{:S(2)}) async-start(), calls=%async_computation.8 | async-start | bytes 2359296 | tf_op jit(solution)/shard_map/all_gather | solution.py:593
  10.9 123.3 %all-gather.8.cloned.1.call-start = ((), (), s32[]{:S(2)}) async-start(), calls=%async_computation.9 | async-start | bytes 1769472 | tf_op jit(solution)/shard_map/all_gather | solution.py:621
  69.3 17.0 %copy-start.1 = (s32[512]{0:T(512)S(1)}, s32[512]{0:T(512)}, u32[]{:S(2)}) copy-start(s32[512]{0:T(512)} %param.17) | copy-start | bytes 6148
  129.8 11.9 %all-to-all-start.6 = ((bf16[8,64,256]{2,1,0:T(8,128)(2,1)}), bf16[8,64,256]{2,1,0:T(8,128)(2,1)S(1)}, u32[]{:S(2)}, u32[]{:S(2)}) async-start(bf16[8,64,256]{2,1,0:T(8,128)(2,1)} %get-tuple-element.50), calls=%async_computation.6 | async-start | bytes 524288 | tf_op jit(solution)/shard_map/all_to_all | solution.py:585
Sparse Core Ops, SparseCore 0:
  10.2 47.9 all-gather.9
  59.9 24.2 all-gather.5
  92.0 21.9 all-gather.7
